TPU v7x, 32 devices: a whole 2x2x4 slice. The times are simulated.
32 devices in a mesh: ctx: 8 (over z, core), fsdp: 4 (over y, x).
Axes of the slice: x: 2, y: 2, z: 4, core: 2. Of those that a mesh axis runs over, the one named last changes fastest.
Arguments:
- inputs: float32 [4, 16, 64, 1024], P('fsdp', 'ctx'), may hold values from -6 to 6
- block_order: int32 [16], replicated, may hold values from 0 to 15, as said below
- w_qkv: bfloat16 [1, 1024, 3072], P(None, 'fsdp'), may hold values from -0.1875 to 0.1875
- w_out: bfloat16 [1, 1024, 1024], P(None, 'fsdp'), may hold values from -1.5 to 1.5
- w_up: bfloat16 [1, 1024, 4096], P(None, 'fsdp'), may hold values from -0.1875 to 0.1875
- w_down: bfloat16 [1, 4096, 1024], P(None, 'fsdp'), may hold values from -0.09375 to 0.09375
- norm_gains: bfloat16 [1, 2, 1024], P(None, None, 'fsdp'), may hold values from 0.099609375 to 1.8984375
- biases: bfloat16 [1, 6, 1024], P(None, None, 'fsdp'), may hold values from -2.390625 to 2.390625
- up_bias: bfloat16 [1, 4096], P(None, 'fsdp'), may hold values from -2.390625 to 2.390625
- out_grad: float32 [4, 16, 64, 1024], P('fsdp', 'ctx'), may hold values from -6 to 6
Outputs:
- outputs: float32 [4, 16, 64, 1024], P('fsdp', 'ctx')
- input_grad: float32 [4, 16, 64, 1024], P('fsdp', 'ctx')
- g_qkv: float32 [1, 1024, 3072], P(None, ('ctx', 'fsdp'))
- g_out: float32 [1, 1024, 1024], P(None, ('ctx', 'fsdp'))
- g_up: float32 [1, 1024, 4096], P(None, ('ctx', 'fsdp'))
- g_down: float32 [1, 4096, 1024], P(None, ('ctx', 'fsdp'))
- g_gains: float32 [1, 2, 1024], P(None, None, ('ctx', 'fsdp'))
- g_biases: float32 [1, 6, 1024], P(None, None, ('ctx', 'fsdp'))
- g_up_bias: float32 [1, 4096], P(None, ('ctx', 'fsdp'))
Inputs may be any that keep to these rules, and one draw needn't show every extreme that they name: `block_order`: every block number appears once; slots 2c and 2c + 1 hold a pair b and 15 - b, in either order.
All inputs are finite; a program needn't handle non-finite values.
Results may differ from a plain program's by a relative error of at most 0.013.
Values may be sent and summed in bfloat16 or wider, within the bound.
No kernel may reach another device: no remote copies, remote signals or barrier semaphores. Data moves between devices by JAX's collectives and lax.ppermute only.
A program may use at most 192 MiB of HBM per device.

v0:
```python
import jax
import jax.numpy as jnp
from jax import lax
from jax.experimental import pallas as pl
from jax.experimental.pallas import tpu as pltpu
from jax.sharding import PartitionSpec as P


HEADS = 16
EPS = 1e-05
SCALE = 0.125
GELU_C = 0.7978845608028654
BF = jnp.bfloat16
F32 = jnp.float32


CI, FI, Z, CORE, ORDER = 0, 1, 2, 3, 8


def normalize(x):
    centred = x - jnp.mean(x, axis=1, keepdims=True)
    inv = lax.rsqrt(jnp.mean(centred * centred, axis=1, keepdims=True) + EPS)
    return (centred * inv, inv)


def norm_back(grad, normed, inv):
    return inv * (
        grad
        - jnp.mean(grad, axis=1, keepdims=True)
        - normed * jnp.mean(grad * normed, axis=1, keepdims=True)
    )


def gelu_parts(u):
    inner = GELU_C * (u + 0.044715 * u * u * u)
    tanhed = jnp.tanh(inner)
    value = 0.5 * u * (1.0 + tanhed)
    slope = 0.5 * (1.0 + tanhed) + 0.5 * u * (1.0 - tanhed * tanhed) * GELU_C * (
        1.0 + 3.0 * 0.044715 * u * u
    )
    return (value, slope)


def dot(a, b):
    return jnp.dot(a, b, preferred_element_type=F32)


def outer(left, right):
    return lax.dot_general(left, right, (((0,), (0,)), ((), ())), preferred_element_type=F32)


def through(left, weight):
    return lax.dot_general(left, weight, (((1,), (1,)), ((), ())), preferred_element_type=F32)


def shaped(shape, kind):
    return jax.ShapeDtypeStruct(shape, kind)


def total_bytes(arrays):
    return sum(a.size * a.dtype.itemsize for a in arrays)


def call(kernel, outs, idx, ins, scratch=(), flops=0):
    vmem = pl.BlockSpec(memory_space=pltpu.VMEM)
    return pl.pallas_call(
        kernel,
        out_shape=outs,
        in_specs=[pl.BlockSpec(memory_space=pltpu.SMEM)] + [vmem] * len(ins),
        out_specs=[vmem] * len(outs),
        scratch_shapes=list(scratch),
        compiler_params=pltpu.CompilerParams(vmem_limit_bytes=20 * 1024 * 1024),
        cost_estimate=pl.CostEstimate(
            flops=flops, bytes_accessed=total_bytes(ins) + total_bytes(outs), transcendentals=0
        ),
    )(idx, *ins)


def build(mesh):
    n_ctx, n_f = mesh.shape["ctx"], mesh.shape["fsdp"]
    n_z = n_ctx // 2

    def fsdp_to(x, k):
        return lax.ppermute(x, "fsdp", [(f, f ^ k) for f in range(n_f)])

    def ctx_to(x, e):
        return lax.ppermute(x, "ctx", [(i, i ^ e) for i in range(n_ctx)])

    def both_to(x, target):
        pairs = []
        for i in range(n_ctx):
            for f in range(n_f):
                to_i, to_f = target(i, f)
                pairs.append((i * n_f + f, to_i * n_f + to_f))
        return lax.ppermute(x, ("ctx", "fsdp"), pairs)

    def gather_f(block):
        return [block] + [fsdp_to(block, k) for k in range(1, n_f)]

    def send_f(blocks):
        return [fsdp_to(b, k + 1) for k, b in enumerate(blocks)]

    def share_core(blocks):
        return [ctx_to(b, 1) for b in blocks]

    def fill_rows(full, own, got, other, fi, core, cut=slice(None)):
        depth = own.shape[0]
        half = depth // 2
        full[pl.ds(fi * depth, depth), :] = own[:, cut]
        for k in range(1, n_f):
            base = (fi ^ k) * depth
            full[pl.ds(base + core * half, half), :] = got[k - 1][:half, cut]
            full[pl.ds(base + (1 - core) * half, half), :] = other[k - 1][:half, cut]

    def layer(inputs, block_order, w_qkv, w_out, w_up, w_down, gains, biases, up_bias, out_grad):
        seqs, slots, blk, width = inputs.shape
        rows = seqs * slots * blk
        ci = lax.axis_index("ctx")
        fi = lax.axis_index("fsdp")
        z, c = ci // 2, ci % 2
        mine = 2 * fi + c
        wide = width // n_f
        pair = wide // 2
        hidden = up_bias.shape[1]
        hd = width // HEADS
        heads = pair // hd
        length = n_ctx * rows
        half = wide // 2
        all_rows = n_f * rows
        x = inputs.reshape(rows, width)
        d_result = out_grad.reshape(rows, width)
        w_qkv, w_out, w_up, w_down = w_qkv[0], w_out[0], w_up[0], w_down[0]
        zero = jnp.zeros((), jnp.int32)
        idx = jnp.concatenate(
            [jnp.stack([ci, fi, z, c, mine, zero, zero, zero]).astype(jnp.int32), block_order]
        )
        own_small = jnp.concatenate([gains[0], biases[0]])
        n_small = own_small.shape[0]

        def prep(i, x_ref, w_ref, s_ref, n_ref, own_ref, *send):
            normed, _ = normalize(x_ref[...])
            n_ref[...] = normed.astype(BF)
            f, core = i[FI], i[CORE]
            for q in range(3):
                to = slice(q * wide, (q + 1) * wide)
                at = pl.multiple_of(q * width + f * wide, wide)
                own_ref[:, to] = w_ref[:, pl.ds(at, wide)]
                for k in range(1, n_f):
                    at = pl.multiple_of(q * width + (f ^ k) * wide, wide)
                    row = pl.multiple_of(core * half, half)
                    send[k - 1][:half, to] = w_ref[pl.ds(row, half), pl.ds(at, wide)]
            for k in range(1, n_f):
                send[k - 1][half : half + n_small, :wide] = s_ref[...]

        outs = [shaped((rows, width), BF), shaped((wide, 3 * wide), BF)]
        outs += [shaped((half + 16, 3 * wide), BF)] * (n_f - 1)
        n_one, own_qkv, *sends = call(prep, outs, idx, [x, w_qkv, own_small])
        got_qkv = send_f(sends)
        other_qkv = share_core(got_qkv)
        n_all = gather_f(n_one)

        def project(i, *refs):
            n_refs, refs = refs[:n_f], refs[n_f:]
            own, s_ref, refs = refs[0], refs[1], refs[2:]
            got, refs = refs[: n_f - 1], refs[n_f - 1 :]
            other, refs = refs[: n_f - 1], refs[n_f - 1 :]
            a_ref, full, small, refs = refs[0], refs[1], refs[2], refs[3:]
            send, held = refs[:n_ctx], refs[n_ctx]
            f, core = i[FI], i[CORE]
            for k in range(n_f):
                piece = s_ref[...] if k == 0 else got[k - 1][half : half + n_small, :wide]
                small[:, pl.ds(pl.multiple_of((f ^ k) * wide, wide), wide)] = piece.astype(F32)
            fill_rows(full, own, got, other, f, core)
            at = pl.ds(pl.multiple_of(f * wide, wide), wide)
            q_shift, v_shift = small[3:4, at], small[4:5, at]
            for k in range(n_f):
                a_one = (n_refs[k][...].astype(F32) * small[0:1, :] + small[2:3, :]).astype(BF)
                a_ref[k * rows : (k + 1) * rows, :] = a_one
                proj = dot(a_one, full[...])
                query = ((proj[:, :wide] + q_shift) * SCALE).astype(BF)
                keys = proj[:, wide : 2 * wide].astype(BF)
                values = (proj[:, 2 * wide :] + v_shift).astype(BF)
                for p in range(2):
                    cut = slice(p * pair, (p + 1) * pair)
                    for q, part in enumerate((query, keys, values)):
                        held[k, p, :, q * pair : (q + 1) * pair] = part[:, cut]
            for e in range(n_ctx):
                send[e][...] = held[i[FI] ^ i[Z] ^ (e >> 1), core ^ (e & 1)]

        outs = [
            shaped((all_rows, width), BF),
            shaped((width, 3 * wide), BF),
            shaped((n_small, width), F32),
        ] + [shaped((rows, 3 * pair), BF)] * n_ctx
        a_all, full_qkv, small, *sends = call(
            project, outs, idx,
            n_all + [own_qkv, own_small] + got_qkv + other_qkv,
            [pltpu.VMEM((n_f, 2, rows, 3 * pair), BF)],
            flops=6 * all_rows * width * wide,
        )
        got = [sends[0]] + [ctx_to(sends[e], e) for e in range(1, n_ctx)]

        def cut_weights(i, up_ref, out_ref, own_ref, *send):
            f, core = i[FI], i[CORE]
            row = pl.ds(pl.multiple_of(core * half, half), half)
            own_ref[:, :hidden] = up_ref[:, pl.ds(pl.multiple_of(f * hidden, hidden), hidden)]
            own_ref[:, hidden:] = out_ref[...]
            for k in range(1, n_f):
                at = pl.ds(pl.multiple_of((f ^ k) * hidden, hidden), hidden)
                send[k - 1][:, :hidden] = up_ref[row, at]
                send[k - 1][:, hidden:] = out_ref[row, :]

        outs = [shaped((wide, hidden + width), BF)]
        outs += [shaped((half, hidden + width), BF)] * (n_f - 1)
        own_w, *sends = call(cut_weights, outs, idx, [w_up, w_out])
        got_w = send_f(sends)
        other_w = share_core(got_w)
        dz, _ = lax.optimization_barrier((d_result.astype(BF), n_all))
        dz_all = lax.all_gather(dz, "fsdp", axis=0, tiled=True)

        def positions(i, block, along):
            dims = (rows, 1) if along == 0 else (1, rows)
            at = lax.broadcasted_iota(jnp.int32, dims, along)
            pos = at + i[ORDER + block * slots] * blk
            for s in range(1, slots):
                moved = at - s * blk + i[ORDER + block * slots + s] * blk
                pos = jnp.where(at >= s * blk, moved, pos)
            return pos

        def fill_positions(i, kpos, qpos):
            for e in range(n_ctx):
                here = slice(e * rows, (e + 1) * rows)
                kpos[:, here] = positions(i, i[CI] ^ e, 1)
                qpos[here, :] = positions(i, i[CI] ^ e, 0)

        tall = 2 * rows
        places = [pltpu.VMEM((1, length), jnp.int32), pltpu.VMEM((length, 1), jnp.int32)]

        def attend(i, *refs):
            got, refs = refs[:n_ctx], refs[n_ctx:]
            seq, att, lse_ref, refs = refs[0], refs[1], refs[2], refs[3:]
            send, (kpos, qpos) = refs[:n_f], refs[n_f:]
            for e in range(n_ctx):
                seq[e * rows : (e + 1) * rows, :] = got[e][...]
            fill_positions(i, kpos, qpos)

            def step(e, _):
                here = pl.ds(pl.multiple_of(e * tall, tall), tall)
                allowed = kpos[...] <= qpos[here, :]
                for h in range(heads):
                    cut = slice(h * hd, (h + 1) * hd)
                    keys = seq[:, pair + h * hd : pair + (h + 1) * hd]
                    values = seq[:, 2 * pair + h * hd : 2 * pair + (h + 1) * hd]
                    scores = jnp.where(allowed, through(seq[here, cut], keys), -1e30)
                    top = jnp.max(scores, axis=1, keepdims=True)
                    probs = jnp.exp(scores - top)
                    norm = jnp.sum(probs, axis=1, keepdims=True)
                    out = dot(probs.astype(BF), values) / norm
                    att[here, cut] = out.astype(BF)
                    lse_ref[here, cut] = jnp.broadcast_to(top + jnp.log(norm), (tall, hd))
                return 0

            lax.fori_loop(0, length // tall, step, 0)
            for m in range(n_f):
                for core in range(2):
                    block = (2 * (m ^ i[FI]) + core) ^ i[CI]
                    at = pl.multiple_of(block * rows, rows)
                    send[m][core * rows : (core + 1) * rows, :] = att[pl.ds(at, rows), :]

        outs = [shaped((length, 3 * pair), BF), shaped((length, pair), BF), shaped((length, pair), F32)]
        outs += [shaped((tall, pair), BF)] * n_f
        seq, att, lse, *sends = call(
            attend, outs, idx, got, places, flops=4 * length * length * pair
        )
        got = [both_to(sends[m], lambda i, f: (2 * (m ^ f) + i % 2, i // 2)) for m in range(n_f)]
        o_parts = got + [ctx_to(g, 1) for g in got]

        def o_part(i, refs, core, m):
            here = pl.ds(pl.multiple_of(i[CORE] * rows, rows), rows)
            own, other = refs[m][here, :], refs[n_f + m][here, :]
            return jnp.where(core == i[CORE], own, other)

        def finish(i, *refs):
            x_ref, small_ref, refs = refs[0], refs[1], refs[2:]
            o_refs, refs = refs[: 2 * n_f], refs[2 * n_f :]
            own, refs = refs[0], refs[1:]
            got_o, refs = refs[: n_f - 1], refs[n_f - 1 :]
            other_o, refs = refs[: n_f - 1], refs[n_f - 1 :]
            mid_ref, a_ref, full = refs
            fill_rows(full, own, got_o, other_o, i[FI], i[CORE], slice(hidden, None))
            mid = x_ref[...] + small_ref[5:6, :]
            for m in range(n_f):
                for core in range(2):
                    at = pl.multiple_of((2 * (m ^ i[Z]) + core) * pair, pair)
                    mid = mid + dot(o_part(i, o_refs, core, m), full[pl.ds(at, pair), :])
            mid_ref[...] = mid
            normed, _ = normalize(mid)
            a_ref[...] = (normed * small_ref[1:2, :] + small_ref[6:7, :]).astype(BF)

        outs = [shaped((rows, width), F32), shaped((rows, width), BF), shaped((width, width), BF)]
        mid, a_two, full_out = call(
            finish, outs, idx,
            [x, small] + o_parts + [own_w] + got_w + other_w,
            flops=2 * rows * width * width,
        )
        a2_parts = gather_f(a_two)

        def forward(i, *refs):
            a_refs, refs = refs[:n_f], refs[n_f:]
            own, bias, refs = refs[0], refs[1], refs[2:]
            got_u, refs = refs[: n_f - 1], refs[n_f - 1 :]
            other_u, refs = refs[: n_f - 1], refs[n_f - 1 :]
            full, a_ref, gel, slope_ref = refs
            fill_rows(full, own, got_u, other_u, i[FI], i[CORE], slice(0, hidden))
            for k in range(n_f):
                here = slice(k * rows, (k + 1) * rows)
                a_ref[here, :] = a_refs[k][...]
                value, slope = gelu_parts(dot(a_refs[k][...], full[...]) + bias[...].astype(F32))
                gel[here, :] = value.astype(BF)
                slope_ref[here, :] = slope

        outs = [
            shaped((width, hidden), BF),
            shaped((all_rows, width), BF),
            shaped((all_rows, hidden), BF),
            shaped((all_rows, hidden), F32),
        ]
        full_up, a2_all, gelled, slope = call(
            forward, outs, idx, a2_parts + [own_w, up_bias] + got_w + other_w,
            flops=2 * all_rows * width * hidden,
        )

        def backward(i, *refs):
            dz_nat, slope_ref, down, up, refs = refs[0], refs[1], refs[2], refs[3], refs[4:]
            dz_ref, du_ref, sum_ref, own, send = refs[0], refs[1], refs[2], refs[3], refs[4:]
            total = jnp.zeros((1, hidden), F32)
            for k in range(n_f):
                here = slice(k * rows, (k + 1) * rows)
                dz_k = dz_nat[pl.ds(pl.multiple_of((i[FI] ^ k) * rows, rows), rows), :]
                dz_ref[here, :] = dz_k
                d_pre = through(dz_k, down[...]) * slope_ref[here, :]
                total = total + jnp.sum(d_pre, axis=0, keepdims=True)
                d_hidden = d_pre.astype(BF)
                du_ref[here, :] = d_hidden
                part = through(d_hidden, up[...])
                if k:
                    send[k - 1][...] = part.astype(BF)
                else:
                    own[...] = part
            sum_ref[...] = total

        outs = [
            shaped((all_rows, width), BF),
            shaped((all_rows, hidden), BF),
            shaped((1, hidden), F32),
            shaped((rows, width), F32),
        ] + [shaped((rows, width), BF)] * (n_f - 1)
        dz_all, d_hidden, up_sum, d_own, *sends = call(
            backward, outs, idx, [dz_all, slope, w_down, full_up],
            flops=4 * all_rows * width * hidden,
        )
        got_a = send_f(sends)
        g_down = outer(gelled, dz_all).astype(BF)
        g_up = outer(a2_all, d_hidden).astype(BF)

        def scatter_ctx(g):
            return lax.psum_scatter(g, "ctx", scatter_dimension=0, tiled=True)

        part_down = scatter_ctx(g_down)
        part_up = scatter_ctx(g_up)

        def second(i, *refs):
            d_ref, mid_ref, small_ref, full, own, refs = (*refs[:5], refs[5:])
            got, refs = refs[: n_f - 1], refs[n_f - 1 :]
            dmid_ref, dy_ref, sums, send = refs[0], refs[1], refs[2], refs[3:]
            d_a = own[...]
            for g in got:
                d_a = d_a + g[...].astype(F32)
            normed, inv = normalize(mid_ref[...])
            d_res = d_ref[...]
            d_mid = d_res + norm_back(d_a * small_ref[1:2, :], normed, inv)
            dmid_ref[...] = d_mid
            dy = d_mid.astype(BF)
            dy_ref[...] = dy
            for m in range(n_f):
                at = pl.multiple_of((m ^ i[Z]) * wide, wide)
                send[m][...] = through(dy, full[pl.ds(at, wide), :]).astype(BF)
            sums[...] = jnp.zeros_like(sums)
            sums[1:2, :] = jnp.sum(d_a * normed, axis=0, keepdims=True)
            sums[5:6, :] = jnp.sum(d_mid, axis=0, keepdims=True)
            sums[6:7, :] = jnp.sum(d_a, axis=0, keepdims=True)
            sums[7:8, :] = jnp.sum(d_res, axis=0, keepdims=True)

        outs = [shaped((rows, width), F32), shaped((rows, width), BF), shaped((8, width), F32)]
        outs += [shaped((rows, wide), BF)] * n_f
        d_mid, dy, sums, *sends = call(
            second, outs, idx, [d_result, mid, small, full_out, d_own] + got_a,
            flops=2 * rows * width * width,
        )
        got = [both_to(sends[m], lambda i, f: (2 * f + i % 2, m ^ (i // 2))) for m in range(n_f)]
        got += [ctx_to(g, 1) for g in got]

        def down(i, gel, w_ref, own, *send):
            for k in range(n_f):
                part = dot(gel[k * rows : (k + 1) * rows, :], w_ref[...])
                if k:
                    send[k - 1][...] = part.astype(BF)
                else:
                    own[...] = part

        outs = [shaped((rows, width), F32)] + [shaped((rows, width), BF)] * (n_f - 1)
        result, *sends = call(
            down, outs, idx, [gelled, w_down], flops=2 * all_rows * width * hidden
        )
        result = result + mid + small[7]
        for g in send_f(sends):
            result = result + g.astype(F32)

        def attend_back(i, *refs):
            seq_ref, att_ref, lse_ref, refs = refs[0], refs[1], refs[2], refs[3:]
            got, refs = refs[: 2 * n_f], refs[2 * n_f :]
            sum_ref, refs = refs[0], refs[1:]
            send, (kpos, qpos, d_out, d_query, d_keys, d_values) = refs[:n_ctx], refs[n_ctx:]
            fill_positions(i, kpos, qpos)
            for m in range(n_f):
                for swap in range(2):
                    part = got[swap * n_f + m]
                    block = (2 * (m ^ i[FI]) + (i[CORE] ^ swap)) ^ i[CI]
                    at = pl.multiple_of(block * rows, rows)
                    d_out[pl.ds(at, rows), :] = jnp.where(
                        i[CORE] == 0, part[:, :pair], part[:, pair:]
                    )
            d_keys[...] = jnp.zeros_like(d_keys)
            d_values[...] = jnp.zeros_like(d_values)

            def step(e, _):
                here = pl.ds(pl.multiple_of(e * tall, tall), tall)
                allowed = kpos[...] <= qpos[here, :]
                for h in range(heads):
                    cut = slice(h * hd, (h + 1) * hd)
                    query, d_att = seq_ref[here, cut], d_out[here, cut]
                    keys = seq_ref[:, pair + h * hd : pair + (h + 1) * hd]
                    values = seq_ref[:, 2 * pair + h * hd : 2 * pair + (h + 1) * hd]
                    lse = lse_ref[here, h * hd : h * hd + 1]
                    scores = jnp.where(allowed, through(query, keys), -1e30)
                    probs = jnp.exp(scores - lse)
                    delta = jnp.sum(
                        d_att.astype(F32) * att_ref[here, cut].astype(F32), axis=1, keepdims=True
                    )
                    d_scores = (probs * (through(d_att, values) - delta)).astype(BF)
                    d_query[here, cut] = dot(d_scores, keys) * SCALE
                    d_keys[:, cut] += outer(d_scores, query)
                    d_values[:, cut] += outer(probs.astype(BF), d_att)
                return 0

            lax.fori_loop(0, length // tall, step, 0)
            for e in range(n_ctx):
                here = slice(e * rows, (e + 1) * rows)
                send[e][:, :pair] = d_query[here, :].astype(BF)
                send[e][:, pair : 2 * pair] = d_keys[here, :].astype(BF)
                send[e][:, 2 * pair :] = d_values[here, :].astype(BF)
            sum_ref[...] = jnp.zeros_like(sum_ref)
            sum_ref[3:4, :] = jnp.sum(d_query[...], axis=0, keepdims=True)
            sum_ref[4:5, :] = jnp.sum(d_values[...], axis=0, keepdims=True)

        outs = [shaped((8, pair), F32)] + [shaped((rows, 3 * pair), BF)] * n_ctx
        qv_sum, *sends = call(
            attend_back, outs, idx, [seq, att, lse] + got,
            places
            + [
                pltpu.VMEM((length, pair), BF),
                pltpu.VMEM((length, pair), F32),
                pltpu.VMEM((length, pair), F32),
                pltpu.VMEM((length, pair), F32),
            ],
            flops=10 * length * length * pair,
        )
        got = [sends[0]] + [ctx_to(sends[e], e) for e in range(1, n_ctx)]

        n_all_dev = n_ctx * n_f
        per = width // n_all_dev

        def grad_out(i, dy_ref, *refs):
            o_refs, (away, keep, held) = refs[: 2 * n_f], refs[2 * n_f :]
            for m in range(n_f):
                for core in range(2):
                    at = pl.multiple_of((2 * (m ^ i[Z]) + core) * pair, pair)
                    held[pl.ds(at, pair), :] = outer(o_part(i, o_refs, core, m), dy_ref[...])
            for b in range(n_z):
                for f in range(n_f):
                    at = (2 * b + i[CORE]) * n_f * per + f * per
                    keep[f, b * per : (b + 1) * per, :] = held[pl.ds(at, per), :]
                    at = (2 * b + 1 - i[CORE]) * n_f * per + f * per
                    away[f, b * per : (b + 1) * per, :] = held[pl.ds(at, per), :].astype(BF)

        dims = (n_f, n_z * per, width)
        away, out_keep = call(
            grad_out, [shaped(dims, BF), shaped(dims, F32)], idx, [dy] + o_parts,
            [pltpu.VMEM((width, width), F32)], flops=2 * rows * width * width,
        )
        away = ctx_to(away, 1)

        def out_first(i, keep, got, own, *send):
            f = i[FI]
            own[...] = keep[f] + got[f].astype(F32)
            for k in range(1, n_f):
                send[k - 1][...] = (keep[f ^ k] + got[f ^ k].astype(F32)).astype(BF)

        outs = [shaped((n_z * per, width), F32)] + [shaped((n_z * per, width), BF)] * (n_f - 1)
        out_own, *sends = call(out_first, outs, idx, [out_keep, away])
        for g in send_f(sends):
            out_own = out_own + g.astype(F32)

        def first(i, *refs):
            got, refs = refs[:n_ctx], refs[n_ctx:]
            n_refs, refs = refs[:n_f], refs[n_f:]
            full, sum_in, refs = refs[0], refs[1], refs[2:]
            proj_ref, sums, own, send, held = refs[0], refs[1], refs[2], refs[3:-1], refs[-1]
            for e in range(n_ctx):
                held[e] = got[e][...]
            gain_sum = jnp.zeros((1, width), F32)
            shift_sum = jnp.zeros((1, width), F32)
            for k in range(n_f):
                here = slice(k * rows, (k + 1) * rows)
                for p in range(2):
                    e = 2 * (i[FI] ^ i[Z] ^ k) + (i[CORE] ^ p)
                    for q in range(3):
                        at = q * wide + p * pair
                        proj_ref[here, at : at + pair] = held[e, :, q * pair : (q + 1) * pair]
                part = through(proj_ref[here, :], full[...])
                gain_sum += jnp.sum(part * n_refs[k][...].astype(F32), axis=0, keepdims=True)
                shift_sum += jnp.sum(part, axis=0, keepdims=True)
                if k:
                    send[k - 1][...] = part.astype(BF)
                else:
                    own[...] = part
            sums[...] = sum_in[...]
            sums[0:1, :] = gain_sum
            sums[2:3, :] = shift_sum

        outs = [
            shaped((all_rows, 3 * wide), BF),
            shaped((8, width), F32),
            shaped((rows, width), F32),
        ] + [shaped((rows, width), BF)] * (n_f - 1)
        d_proj, sums, d_own, *sends = call(
            first, outs, idx, got + n_all + [full_qkv, sums],
            [pltpu.VMEM((n_ctx, rows, 3 * pair), BF)],
            flops=6 * all_rows * width * wide,
        )
        got_x = send_f(sends)

        block = width // n_ctx
        per_up = hidden // n_ctx

        def pack(i, a_ref, p_ref, sums_ref, up_ref, qv_ref, away, keep, held):
            f, core = i[FI], i[CORE]
            for zz in range(n_z):
                at = slice(2 * zz * block, 2 * (zz + 1) * block)
                held[...] = outer(a_ref[:, at], p_ref[...])
                both = sums_ref[:, at]
                for par, out in ((core, keep), (1 - core, away)):
                    row = pl.ds(pl.multiple_of(par * block, block), block)
                    out[zz, :block, :] = held[row, :].astype(out.dtype)
                    out[zz, block:, :] = jnp.zeros((16, 3 * wide), out.dtype)
                    hit = jnp.logical_and(zz == f, par == core)
                    small = jnp.where(par == 0, both[:, :block], both[:, block:])
                    small = small + jnp.where(hit, qv_ref[...], 0.0)
                    ups = up_ref[:, pl.ds(pl.multiple_of(par * n_f * per_up, n_f * per_up), n_f * per_up)]
                    ups = jnp.where(zz == f, ups, 0.0)
                    out[zz, block : block + 8, :block] = small.astype(out.dtype)
                    for g in range(n_f):
                        out[zz, block + 8 + g : block + 9 + g, :per_up] = ups[
                            :, g * per_up : (g + 1) * per_up
                        ].astype(out.dtype)

        dims = (n_z, block + 16, 3 * wide)
        away, keep = call(
            pack, [shaped(dims, BF), shaped(dims, F32)], idx,
            [a_all, d_proj, sums, up_sum, qv_sum], [pltpu.VMEM((2 * block, 3 * wide), F32)],
            flops=6 * all_rows * width * wide,
        )
        away = ctx_to(away, 1)

        out_own = out_own.reshape(n_z, per, width)
        part_w = 4 * wide

        def over_core(i, keep_ref, got, o_ref, own, *send):
            def fill(out, at):
                out[:, : 3 * wide] = (keep_ref[at] + got[at].astype(F32)).astype(out.dtype)
                out[block:, 3 * wide :] = jnp.zeros((16, wide), out.dtype)
                for g in range(n_f):
                    piece = o_ref[at, :, g * wide : (g + 1) * wide]
                    out[g * per : (g + 1) * per, 3 * wide :] = piece.astype(out.dtype)

            fill(own, i[Z])
            for m in range(1, n_z):
                fill(send[m - 1], i[Z] ^ m)

        dims = (block + 16, part_w)
        outs = [shaped(dims, F32)] + [shaped(dims, BF)] * (n_z - 1)
        own, *sends = call(over_core, outs, idx, [keep, away, out_own])
        got = [ctx_to(s, 2 * (m + 1)) for m, s in enumerate(sends)]
        out_down = both_to(
            part_down, lambda i, f: ((f * n_ctx + i) // n_f, (f * n_ctx + i) % n_f)
        ).astype(F32)

        def over_z(i, *refs):
            own_ref, got, up_ref, refs = refs[0], refs[1:n_z], refs[n_z], refs[n_z + 1 :]
            out_ref, own, send, (held, held_up) = refs[0], refs[1], refs[2:-2], refs[-2:]
            total = own_ref[...]
            for g in got:
                total = total + g[...].astype(F32)
            held[...] = total
            held_up[...] = up_ref[...].astype(F32)
            for g in range(n_f):
                out_ref[:, g * wide : (g + 1) * wide] = total[g * per : (g + 1) * per, 3 * wide :]
            for k in range(n_f):
                at = pl.ds(pl.multiple_of((i[FI] ^ k) * per, per), per)
                out = send[k - 1] if k else own
                out[:per, : 3 * wide] = held[at, : 3 * wide].astype(out.dtype)
                out[:per, 3 * wide :] = held_up[at, :].astype(out.dtype)
                out[per:, :] = jnp.zeros((16, 3 * wide + hidden), out.dtype)
                out[per:, : 3 * wide] = held[block:, : 3 * wide].astype(out.dtype)

        dims = (per + 16, 3 * wide + hidden)
        outs = [shaped((per, width), F32), shaped(dims, F32)] + [shaped(dims, BF)] * (n_f - 1)
        out_out, own, *sends = call(
            over_z, outs, idx, [own] + got + [part_up],
            [pltpu.VMEM((block + 16, part_w), F32), pltpu.VMEM((block, hidden), F32)],
        )
        got = send_f(sends)

        def last(i, own_ref, *refs):
            got, (out, up, small_ref) = refs[: n_f - 1], refs[n_f - 1 :]
            total = own_ref[per:, :block]
            for k in range(n_f):
                src = got[k - 1] if k else own_ref
                for q in range(3):
                    at = pl.ds(pl.multiple_of(q * width + (i[FI] ^ k) * wide, wide), wide)
                    out[:, at] = src[:per, q * wide : (q + 1) * wide].astype(F32)
                at = pl.ds(pl.multiple_of((i[FI] ^ k) * hidden, hidden), hidden)
                up[:, at] = src[:per, 3 * wide :].astype(F32)
                if k:
                    total = total + src[per:, :block].astype(F32)
            small_ref[...] = total

        outs = [shaped((per, 3 * width), F32), shaped((per, n_f * hidden), F32)]
        outs += [shaped((16, block), F32)]
        out_qkv, out_up, tile = call(last, outs, idx, [own] + got)
        out_small = lax.dynamic_slice(tile, (0, fi * per), (8, per))
        out_upb = lax.dynamic_slice(tile, (8 + fi, 0), (1, per_up))

        normed, inv = normalize(x)
        d_a = d_own
        for g in got_x:
            d_a = d_a + g.astype(F32)
        d_input = d_mid + norm_back(d_a * small[0], normed, inv)

        shape = (seqs, slots, blk, width)
        return (
            result.reshape(shape),
            d_input.reshape(shape),
            out_qkv[None],
            out_out[None],
            out_up[None],
            out_down[None],
            out_small[:2][None],
            out_small[2:][None],
            out_upb.reshape(1, -1),
        )

    return layer


def solution(mesh):
    return jax.shard_map(
        build(mesh),
        mesh=mesh,
        in_specs=(
            P("fsdp", "ctx", None, None),
            P(),
            P(None, "fsdp", None),
            P(None, "fsdp", None),
            P(None, "fsdp", None),
            P(None, "fsdp", None),
            P(None, None, "fsdp"),
            P(None, None, "fsdp"),
            P(None, "fsdp"),
            P("fsdp", "ctx", None, None),
        ),
        out_specs=(
            P("fsdp", "ctx", None, None),
            P("fsdp", "ctx", None, None),
            P(None, ("ctx", "fsdp"), None),
            P(None, ("ctx", "fsdp"), None),
            P(None, ("ctx", "fsdp"), None),
            P(None, ("ctx", "fsdp"), None),
            P(None, None, ("ctx", "fsdp")),
            P(None, None, ("ctx", "fsdp")),
            P(None, ("ctx", "fsdp")),
        ),
        check_vma=False,
    )
```

profile of v0, /device:TPU:25, one launch (start us, length us, event | category | flops | bytes accessed | tf_op | source)
XLA Modules:
  0.0 343.4 jit_solution(951510331836883641)
XLA Ops:
  22.4 5.7 %collective-permute-done.2.refs_3_.refs_11_ = bf16[128,1024]{1,0:T(8,128)(2,1)} collective-permute-done((bf16[128,1024]{1,0:T(8,128)(2,1)S(1)}, bf16[128,1024]{1,0:T(8,128)(2,1)}, u32[]{:S(2)}, u32[]{:S(2)}) %collective-permute-start.2) | collective-permute-done | bytes 262176 | tf_op jit(solution)/shard_map/ppermute | solution.py:84
  29.4 2.5 collective-permute-done.3.refs_6_
  31.8 2.7 collective-permute-start.6
  37.9 2.8 collective-permute-start.7
  42.4 2.6 shard_map.170
  48.0 3.7 %collective-permute-done.24.refs_11_.refs_6_ = bf16[128,2048]{1,0:T(8,128)(2,1)S(1)} collective-permute-done((bf16[128,2048]{1,0:T(8,128)(2,1)S(1)}, bf16[128,2048]{1,0:T(8,128)(2,1)S(1)}, u32[]{:S(2)}, u32[]{:S(2)}) %collective-permute-start.24) | collective-permute-done | bytes 524320 | tf_op jit(solution)/shard_map/ppermute | solution.py:84
  52.5 6.6 %collective-permute-start.27 = (bf16[128,2048]{1,0:T(8,128)(2,1)S(1)}, bf16[128,2048]{1,0:T(8,128)(2,1)S(1)}, u32[]{:S(2)}, u32[]{:S(2)}) collective-permute-start(bf16[128,2048]{1,0:T(8,128)(2,1)S(1)} %collective-permute-done.24.refs_11_.refs_6_), channel_id=1, source_target_pairs={{0,4},{4,0},{8,12},{12,8},{16,20},{20,16},{24,28},{28,24},{1,5},{5... | collective-permute-start | bytes 1572872 | tf_op jit(solution)/shard_map/ppermute | solution.py:87
  59.1 10.3 %collective-permute-done.26.refs_13_.refs_8_ = bf16[128,2048]{1,0:T(8,128)(2,1)S(1)} collective-permute-done((bf16[128,2048]{1,0:T(8,128)(2,1)S(1)}, bf16[128,2048]{1,0:T(8,128)(2,1)S(1)}, u32[]{:S(2)}, u32[]{:S(2)}) %collective-permute-start.26) | collective-permute-done | bytes 524320 | tf_op jit(solution)/shard_map/ppermute | solution.py:84
  72.9 7.5 %collective-permute-done.13.refs_5_ = bf16[128,384]{1,0:T(8,128)(2,1)S(1)} collective-permute-done((bf16[128,384]{1,0:T(8,128)(2,1)S(1)}, bf16[128,384]{1,0:T(8,128)(2,1)S(1)}, u32[]{:S(2)}, u32[]{:S(2)}) %collective-permute-start.13) | collective-permute-done | bytes 98336 | tf_op jit(solution)/shard_map/ppermute | solution.py:87
  80.9 6.2 %collective-permute-done.15.refs_7_ = bf16[128,384]{1,0:T(8,128)(2,1)S(1)} collective-permute-done((bf16[128,384]{1,0:T(8,128)(2,1)S(1)}, bf16[128,384]{1,0:T(8,128)(2,1)S(1)}, u32[]{:S(2)}, u32[]{:S(2)}) %collective-permute-start.15) | collective-permute-done | bytes 98336 | tf_op jit(solution)/shard_map/ppermute | solution.py:87
  87.1 6.5 %shard_map.171 = (bf16[1024,384]{1,0:T(8,128)(2,1)S(1)}, bf16[1024,128]{1,0:T(8,128)(2,1)S(1)}, f32[1024,128]{1,0:T(8,128)S(1)}, bf16[256,128]{1,0:T(8,128)(2,1)...) custom-call(s32[24]{0:T(128)S(1)} %concatenate.6.i, ...), custom_call_target="tpu_custom_call" | custom-call | flops 536870912 | bytes 2621440 | tf_op jit(solution)/shard_map/pallas_call | solution.py:66
  95.3 2.7 collective-permute-start.16
  98.0 3.4 collective-permute-start.17
  101.4 3.2 collective-permute-done.16.refs_2_.refs_0_
  104.9 5.7 %collective-permute-done.18.refs_4_.refs_2_ = bf16[256,128]{1,0:T(8,128)(2,1)S(1)} collective-permute-done((bf16[256,128]{1,0:T(8,128)(2,1)S(1)}, bf16[256,128]{1,0:T(8,128)(2,1)S(1)}, u32[]{:S(2)}, u32[]{:S(2)}) %collective-permute-start.18) | collective-permute-done | bytes 65568 | tf_op jit(solution)/shard_map/ppermute | solution.py:95
  110.5 3.2 collective-permute-start.20
  121.5 5.0 %collective-permute-done.30.refs_1_ = bf16[128,1024]{1,0:T(8,128)(2,1)S(1)} collective-permute-done((bf16[128,1024]{1,0:T(8,128)(2,1)S(1)}, bf16[128,1024]{1,0:T(8,128)(2,1)S(1)}, u32[]{:S(2)}, u32[]{:S(2)}) %collective-permute-start.30) | collective-permute-done | bytes 262176 | tf_op jit(solution)/shard_map/ppermute | solution.py:84
  126.5 6.4 %collective-permute-done.31.refs_2_ = bf16[128,1024]{1,0:T(8,128)(2,1)S(1)} collective-permute-done((bf16[128,1024]{1,0:T(8,128)(2,1)S(1)}, bf16[128,1024]{1,0:T(8,128)(2,1)S(1)}, u32[]{:S(2)}, u32[]{:S(2)}) %collective-permute-start.31) | collective-permute-done | bytes 262176 | tf_op jit(solution)/shard_map/ppermute | solution.py:84
  132.9 3.2 shard_map.174
  146.7 6.1 %shard_map.176 = (bf16[512,1024]{1,0:T(8,128)(2,1)S(1)}, bf16[512,1024]{1,0:T(8,128)(2,1)S(1)}, f32[1,1024]{1,0:T(1,128)S(1)}, f32[128,1024]{1,0:T(8,128)S(1)}, ...) custom-call(s32[24]{0:T(128)S(1)} %concatenate.6.i, ...), custom_call_target="tpu_custom_call" | custom-call | flops 2147483648 | bytes 10752000 | tf_op jit(solution)/shard_map/pallas_call | solution.py:66
  156.7 2.6 convolution_convert_fusion.1
  159.4 4.2 %convolution_convert_fusion = bf16[1024,1024]{1,0:T(8,128)(2,1)} fusion(bf16[512,1024]{1,0:T(8,128)(2,1)} %copy-done.44, bf16[512,1024]{1,0:T(8,128)(2,1)} %copy-done.64), kind=kOutput, calls=%fused_computation | convolution fusion | flops 1074790400 | bytes 4194304 | tf_op jit(solution)/shard_map/dot_general | solution.py:49
  166.3 4.1 %collective-permute-done.36.refs_5_ = bf16[128,1024]{1,0:T(8,128)(2,1)S(1)} collective-permute-done((bf16[128,1024]{1,0:T(8,128)(2,1)}, bf16[128,1024]{1,0:T(8,128)(2,1)S(1)}, u32[]{:S(2)}, u32[]{:S(2)}) %collective-permute-start.36) | collective-permute-done | bytes 262176 | tf_op jit(solution)/shard_map/ppermute | solution.py:84
  170.5 6.0 %collective-permute-done.38.refs_7_ = bf16[128,1024]{1,0:T(8,128)(2,1)S(1)} collective-permute-done((bf16[128,1024]{1,0:T(8,128)(2,1)}, bf16[128,1024]{1,0:T(8,128)(2,1)S(1)}, u32[]{:S(2)}, u32[]{:S(2)}) %collective-permute-start.38) | collective-permute-done | bytes 262176 | tf_op jit(solution)/shard_map/ppermute | solution.py:84
  178.6 2.5 shard_map.177
  182.6 3.7 %collective-permute-start.39 = (bf16[128,256]{1,0:T(8,128)(2,1)}, bf16[128,256]{1,0:T(8,128)(2,1)S(1)}, u32[]{:S(2)}, u32[]{:S(2)}) collective-permute-start(bf16[128,256]{1,0:T(8,128)(2,1)} %get-tuple-element.138), channel_id=1, source_target_pairs={{0,0},{1,8},{2,16},{3,24},{4,4},{5,12},{6,20},{7,28},{8,1},{9,9},{... | collective-permute-start | bytes 196616 | tf_op jit(solution)/shard_map/ppermute | solution.py:95
  187.8 2.3 collective-permute-start.42
  197.0 2.5 shard_map.181
  199.5 3.6 %collective-permute-start.58 = (bf16[4,128,1024]{2,1,0:T(8,128)(2,1)}, bf16[4,128,1024]{2,1,0:T(8,128)(2,1)}, u32[]{:S(2)}, u32[]{:S(2)}) collective-permute-start(bf16[4,128,1024]{2,1,0:T(8,128)(2,1)} %get-tuple-element.165), channel_id=1, source_target_pairs={{0,4},{4,0},{8,12},{12,8},{16,20},{20,16},{24,28},{28,24},{1,5},{5... | collective-permute-start | bytes 3145736 | tf_op jit(solution)/shard_map/ppermute | solution.py:87
  203.7 4.1 %collective-permute-done.41.refs_5_ = bf16[128,256]{1,0:T(8,128)(2,1)S(1)} collective-permute-done((bf16[128,256]{1,0:T(8,128)(2,1)}, bf16[128,256]{1,0:T(8,128)(2,1)S(1)}, u32[]{:S(2)}, u32[]{:S(2)}) %collective-permute-start.41) | collective-permute-done | bytes 65568 | tf_op jit(solution)/shard_map/ppermute | solution.py:95
  213.7 10.2 %shard_map.178 = (f32[8,128]{1,0:T(8,128)S(1)}, bf16[128,384]{1,0:T(8,128)(2,1)S(1)}, bf16[128,384]{1,0:T(8,128)(2,1)S(1)}, bf16[128,384]{1,0:T(8,128)(2,1)S(1)}...) custom-call(s32[24]{0:T(128)S(1)} %concatenate.6.i, ...), custom_call_target="tpu_custom_call" | custom-call | flops 1342177280 | bytes 2887680 | tf_op jit(solution)/shard_map/pallas_call | solution.py:66
  226.4 2.4 collective-permute-start.51
  228.8 3.0 collective-permute-done.48.refs_2_
  231.8 6.9 %collective-permute-done.49.refs_3_ = bf16[128,384]{1,0:T(8,128)(2,1)S(1)} collective-permute-done((bf16[128,384]{1,0:T(8,128)(2,1)S(1)}, bf16[128,384]{1,0:T(8,128)(2,1)S(1)}, u32[]{:S(2)}, u32[]{:S(2)}) %collective-permute-start.49) | collective-permute-done | bytes 98336 | tf_op jit(solution)/shard_map/ppermute | solution.py:87
  238.8 2.5 shard_map.175
  242.1 7.8 %collective-permute-done.51.refs_5_ = bf16[128,384]{1,0:T(8,128)(2,1)S(1)} collective-permute-done((bf16[128,384]{1,0:T(8,128)(2,1)S(1)}, bf16[128,384]{1,0:T(8,128)(2,1)S(1)}, u32[]{:S(2)}, u32[]{:S(2)}) %collective-permute-start.51) | collective-permute-done | bytes 98336 | tf_op jit(solution)/shard_map/ppermute | solution.py:87
  249.9 2.4 collective-permute-start.35
  252.3 3.3 shard_map.179
  256.4 2.6 shard_map.180
  265.0 2.2 convert_add_fusion.1
  269.9 6.3 %collective-permute-done.60 = bf16[128,1024]{1,0:T(8,128)(2,1)S(1)} collective-permute-done((bf16[128,1024]{1,0:T(8,128)(2,1)S(1)}, bf16[128,1024]{1,0:T(8,128)(2,1)S(1)}, u32[]{:S(2)}, u32[]{:S(2)}) %collective-permute-start.60) | collective-permute-done | bytes 262176 | tf_op jit(solution)/shard_map/ppermute | solution.py:84
  277.8 3.9 %collective-permute-start.62 = (bf16[144,1024]{1,0:T(8,128)(2,1)S(1)}, bf16[144,1024]{1,0:T(8,128)(2,1)S(1)}, u32[]{:S(2)}, u32[]{:S(2)}) collective-permute-start(bf16[144,1024]{1,0:T(8,128)(2,1)S(1)} %get-tuple-element.171), channel_id=1, source_target_pairs={{0,8},{4,12},{8,0},{12,4},{16,24},{20,28},{24,16},{28,20},{1,9},{5... | collective-permute-start | bytes 884744 | tf_op jit(solution)/shard_map/ppermute | solution.py:87
  283.8 3.9 %collective-permute-done.55 = bf16[128,1024]{1,0:T(8,128)(2,1)S(1)} collective-permute-done((bf16[128,1024]{1,0:T(8,128)(2,1)S(1)}, bf16[128,1024]{1,0:T(8,128)(2,1)S(1)}, u32[]{:S(2)}, u32[]{:S(2)}) %collective-permute-start.55) | collective-permute-done | bytes 262176 | tf_op jit(solution)/shard_map/ppermute | solution.py:84
  289.0 4.3 %collective-permute-done.63.refs_2_ = bf16[144,1024]{1,0:T(8,128)(2,1)S(1)} collective-permute-done((bf16[144,1024]{1,0:T(8,128)(2,1)S(1)}, bf16[144,1024]{1,0:T(8,128)(2,1)S(1)}, u32[]{:S(2)}, u32[]{:S(2)}) %collective-permute-start.63) | collective-permute-done | bytes 294944 | tf_op jit(solution)/shard_map/ppermute | solution.py:87
  293.3 5.1 %collective-permute-done.64.refs_3_ = bf16[144,1024]{1,0:T(8,128)(2,1)S(1)} collective-permute-done((bf16[144,1024]{1,0:T(8,128)(2,1)S(1)}, bf16[144,1024]{1,0:T(8,128)(2,1)S(1)}, u32[]{:S(2)}, u32[]{:S(2)}) %collective-permute-start.64) | collective-permute-done | bytes 294944 | tf_op jit(solution)/shard_map/ppermute | solution.py:87
  302.4 4.0 %collective-permute-start.66 = (bf16[48,1792]{1,0:T(8,128)(2,1)S(1)}, bf16[48,1792]{1,0:T(8,128)(2,1)S(1)}, u32[]{:S(2)}, u32[]{:S(2)}) collective-permute-start(bf16[48,1792]{1,0:T(8,128)(2,1)S(1)} %get-tuple-element.178), channel_id=1, source_target_pairs={{0,2},{1,3},{2,0},{3,1},{4,6},{5,7},{6,4},{7,5},{8,10},{9,11},{10,... | collective-permute-start | bytes 516104 | tf_op jit(solution)/shard_map/ppermute | solution.py:84
  307.4 2.9 collective-permute-start.68
  314.8 21.2 %collective-permute-done.68 = bf16[128,1024]{1,0:T(8,128)(2,1)S(1)} collective-permute-done((bf16[128,1024]{1,0:T(8,128)(2,1)}, bf16[128,1024]{1,0:T(8,128)(2,1)S(1)}, u32[]{:S(2)}, u32[]{:S(2)}) %collective-permute-start.68) | collective-permute-done | bytes 262176 | tf_op jit(solution)/shard_map/ppermute | solution.py:95
  (284 shorter events, 102.4 us)
Async XLA Ops:
  7.2 133.5 %all-gather.2.cloned.1.call-start = ((), (), s32[]{:S(2)}) async-start(), calls=%async_computation.2 | async-start | bytes 1310720 | tf_op jit(solution)/shard_map/all_gather | solution.py:219
  16.6 11.5 %collective-permute-start.2 = (bf16[128,1024]{1,0:T(8,128)(2,1)S(1)}, bf16[128,1024]{1,0:T(8,128)(2,1)}, u32[]{:S(2)}, u32[]{:S(2)}) collective-permute-start(bf16[128,1024]{1,0:T(8,128)(2,1)S(1)} %get-tuple-element.97.refs_0_.refs_8_), channel_id=1, source_target_pairs={{0,3},{1,2},{2,1},{3,0},{4,7},{5,6},{6,5},{7,4},{8,11},{9,10},{10,... | collective-permute-start | bytes 786440 | tf_op jit(solution)/shard_map/ppermute | solution.py:84
  16.8 15.0 %collective-permute-start.3 = (bf16[144,768]{1,0:T(8,128)(2,1)}, bf16[144,768]{1,0:T(8,128)(2,1)}, u32[]{:S(2)}, u32[]{:S(2)}) collective-permute-start(bf16[144,768]{1,0:T(8,128)(2,1)} %get-tuple-element.99), channel_id=1, source_target_pairs={{0,1},{1,0},{2,3},{3,2},{4,5},{5,4},{6,7},{7,6},{8,9},{9,8},{10,11... | collective-permute-start | bytes 663560 | tf_op jit(solution)/shard_map/ppermute | solution.py:84
  18.0 19.7 %collective-permute-start.4 = (bf16[144,768]{1,0:T(8,128)(2,1)}, bf16[144,768]{1,0:T(8,128)(2,1)}, u32[]{:S(2)}, u32[]{:S(2)}) collective-permute-start(bf16[144,768]{1,0:T(8,128)(2,1)} %get-tuple-element.100), channel_id=1, source_target_pairs={{0,2},{1,3},{2,0},{3,1},{4,6},{5,7},{6,4},{7,5},{8,10},{9,11},{10,... | collective-permute-start | bytes 663560 | tf_op jit(solution)/shard_map/ppermute | solution.py:84
  28.1 270.4 %reduce-scatter.3.cloned.1.call-start = ((), (), s32[]{:S(2)}) async-start(), calls=%async_computation.3 | async-start | bytes 2359296 | tf_op jit(solution)/shard_map/reduce_scatter | solution.py:367
  28.1 9.8 %collective-permute-start.5 = (bf16[144,768]{1,0:T(8,128)(2,1)}, bf16[144,768]{1,0:T(8,128)(2,1)S(1)}, u32[]{:S(2)}, u32[]{:S(2)}) collective-permute-start(bf16[144,768]{1,0:T(8,128)(2,1)} %copy-done.61), channel_id=1, source_target_pairs={{0,3},{1,2},{2,1},{3,0},{4,7},{5,6},{6,5},{7,4},{8,11},{9,10},{10,... | collective-permute-start | bytes 663560 | tf_op jit(solution)/shard_map/ppermute | solution.py:84
  31.8 8.9 %collective-permute-start.6 = (bf16[144,768]{1,0:T(8,128)(2,1)}, bf16[144,768]{1,0:T(8,128)(2,1)S(1)}, u32[]{:S(2)}, u32[]{:S(2)}) collective-permute-start(bf16[144,768]{1,0:T(8,128)(2,1)} %collective-permute-done.3.refs_6_), channel_id=1, source_target_pairs={{0,4},{4,0},{8,12},{12,8},{16,20},{20,16},{24,28},{28,24},{1,5},{5... | collective-permute-start | bytes 663560 | tf_op jit(solution)/shard_map/ppermute | solution.py:87
  35.2 16.5 %collective-permute-start.24 = (bf16[128,2048]{1,0:T(8,128)(2,1)S(1)}, bf16[128,2048]{1,0:T(8,128)(2,1)S(1)}, u32[]{:S(2)}, u32[]{:S(2)}) collective-permute-start(bf16[128,2048]{1,0:T(8,128)(2,1)S(1)} %get-tuple-element.116), channel_id=1, source_target_pairs={{0,1},{1,0},{2,3},{3,2},{4,5},{5,4},{6,7},{7,6},{8,9},{9,8},{10,11... | collective-permute-start | bytes 1572872 | tf_op jit(solution)/shard_map/ppermute | solution.py:84
  36.5 16.0 %collective-permute-start.25 = (bf16[128,2048]{1,0:T(8,128)(2,1)S(1)}, bf16[128,2048]{1,0:T(8,128)(2,1)S(1)}, u32[]{:S(2)}, u32[]{:S(2)}) collective-permute-start(bf16[128,2048]{1,0:T(8,128)(2,1)S(1)} %get-tuple-element.117), channel_id=1, source_target_pairs={{0,2},{1,3},{2,0},{3,1},{4,6},{5,7},{6,4},{7,5},{8,10},{9,11},{10,... | collective-permute-start | bytes 1572872 | tf_op jit(solution)/shard_map/ppermute | solution.py:84
  37.7 31.7 %collective-permute-start.26 = (bf16[128,2048]{1,0:T(8,128)(2,1)S(1)}, bf16[128,2048]{1,0:T(8,128)(2,1)S(1)}, u32[]{:S(2)}, u32[]{:S(2)}) collective-permute-start(bf16[128,2048]{1,0:T(8,128)(2,1)S(1)} %get-tuple-element.118), channel_id=1, source_target_pairs={{0,3},{1,2},{2,1},{3,0},{4,7},{5,6},{6,5},{7,4},{8,11},{9,10},{10,... | collective-permute-start | bytes 1572872 | tf_op jit(solution)/shard_map/ppermute | solution.py:84
  46.0 24.3 %collective-permute-start.10 = (bf16[128,384]{1,0:T(8,128)(2,1)S(1)}, bf16[128,384]{1,0:T(8,128)(2,1)S(1)}, u32[]{:S(2)}, u32[]{:S(2)}) collective-permute-start(bf16[128,384]{1,0:T(8,128)(2,1)S(1)} %get-tuple-element.105), channel_id=1, source_target_pairs={{0,8},{4,12},{8,0},{12,4},{16,24},{20,28},{24,16},{28,20},{1,9},{5... | collective-permute-start | bytes 294920 | tf_op jit(solution)/shard_map/ppermute | solution.py:87
  46.2 24.1 %collective-permute-start.11 = (bf16[128,384]{1,0:T(8,128)(2,1)S(1)}, bf16[128,384]{1,0:T(8,128)(2,1)S(1)}, u32[]{:S(2)}, u32[]{:S(2)}) collective-permute-start(bf16[128,384]{1,0:T(8,128)(2,1)S(1)} %get-tuple-element.106), channel_id=1, source_target_pairs={{0,12},{4,8},{8,4},{12,0},{16,28},{20,24},{24,20},{28,16},{1,13},{... | collective-permute-start | bytes 294920 | tf_op jit(solution)/shard_map/ppermute | solution.py:87
  51.7 19.0 %collective-permute-start.12 = (bf16[128,384]{1,0:T(8,128)(2,1)S(1)}, bf16[128,384]{1,0:T(8,128)(2,1)S(1)}, u32[]{:S(2)}, u32[]{:S(2)}) collective-permute-start(bf16[128,384]{1,0:T(8,128)(2,1)S(1)} %get-tuple-element.107), channel_id=1, source_target_pairs={{0,16},{4,20},{8,24},{12,28},{16,0},{20,4},{24,8},{28,12},{1,17},{... | collective-permute-start | bytes 294920 | tf_op jit(solution)/shard_map/ppermute | solution.py:87
  52.5 63.8 %collective-permute-start.27 = (bf16[128,2048]{1,0:T(8,128)(2,1)S(1)}, bf16[128,2048]{1,0:T(8,128)(2,1)S(1)}, u32[]{:S(2)}, u32[]{:S(2)}) collective-permute-start(bf16[128,2048]{1,0:T(8,128)(2,1)S(1)} %collective-permute-done.24.refs_11_.refs_6_), channel_id=1, source_target_pairs={{0,4},{4,0},{8,12},{12,8},{16,20},{20,16},{24,28},{28,24},{1,5},{5... | collective-permute-start | bytes 1572872 | tf_op jit(solution)/shard_map/ppermute | solution.py:87
  69.4 46.9 %collective-permute-start.28 = (bf16[128,2048]{1,0:T(8,128)(2,1)S(1)}, bf16[128,2048]{1,0:T(8,128)(2,1)S(1)}, u32[]{:S(2)}, u32[]{:S(2)}) collective-permute-start(bf16[128,2048]{1,0:T(8,128)(2,1)S(1)} %collective-permute-done.25.refs_12_.refs_7_), channel_id=1, source_target_pairs={{0,4},{4,0},{8,12},{12,8},{16,20},{20,16},{24,28},{28,24},{1,5},{5... | collective-permute-start | bytes 1572872 | tf_op jit(solution)/shard_map/ppermute | solution.py:87
  70.3 46.0 %collective-permute-start.29 = (bf16[128,2048]{1,0:T(8,128)(2,1)S(1)}, bf16[128,2048]{1,0:T(8,128)(2,1)S(1)}, u32[]{:S(2)}, u32[]{:S(2)}) collective-permute-start(bf16[128,2048]{1,0:T(8,128)(2,1)S(1)} %collective-permute-done.26.refs_13_.refs_8_), channel_id=1, source_target_pairs={{0,4},{4,0},{8,12},{12,8},{16,20},{20,16},{24,28},{28,24},{1,5},{5... | collective-permute-start | bytes 1572872 | tf_op jit(solution)/shard_map/ppermute | solution.py:87
  70.3 10.2 %collective-permute-start.13 = (bf16[128,384]{1,0:T(8,128)(2,1)S(1)}, bf16[128,384]{1,0:T(8,128)(2,1)S(1)}, u32[]{:S(2)}, u32[]{:S(2)}) collective-permute-start(bf16[128,384]{1,0:T(8,128)(2,1)S(1)} %get-tuple-element.108), channel_id=1, source_target_pairs={{0,20},{4,16},{8,28},{12,24},{16,4},{20,0},{24,12},{28,8},{1,21},{... | collective-permute-start | bytes 294920 | tf_op jit(solution)/shard_map/ppermute | solution.py:87
  70.7 9.8 %collective-permute-start.14 = (bf16[128,384]{1,0:T(8,128)(2,1)S(1)}, bf16[128,384]{1,0:T(8,128)(2,1)S(1)}, u32[]{:S(2)}, u32[]{:S(2)}) collective-permute-start(bf16[128,384]{1,0:T(8,128)(2,1)S(1)} %get-tuple-element.109), channel_id=1, source_target_pairs={{0,24},{4,28},{8,16},{12,20},{16,8},{20,12},{24,0},{28,4},{1,25},{... | collective-permute-start | bytes 294920 | tf_op jit(solution)/shard_map/ppermute | solution.py:87
  95.3 9.3 %collective-permute-start.16 = (bf16[256,128]{1,0:T(8,128)(2,1)S(1)}, bf16[256,128]{1,0:T(8,128)(2,1)S(1)}, u32[]{:S(2)}, u32[]{:S(2)}) collective-permute-start(bf16[256,128]{1,0:T(8,128)(2,1)S(1)} %get-tuple-element.111), channel_id=1, source_target_pairs={{0,0},{1,8},{2,16},{3,24},{4,4},{5,12},{6,20},{7,28},{8,1},{9,9},{... | collective-permute-start | bytes 196616 | tf_op jit(solution)/shard_map/ppermute | solution.py:95
  104.6 9.2 %collective-permute-start.19 = (bf16[256,128]{1,0:T(8,128)(2,1)S(1)}, bf16[256,128]{1,0:T(8,128)(2,1)S(1)}, u32[]{:S(2)}, u32[]{:S(2)}) collective-permute-start(bf16[256,128]{1,0:T(8,128)(2,1)S(1)} %get-tuple-element.114), channel_id=1, source_target_pairs={{0,24},{1,16},{2,8},{3,0},{4,28},{5,20},{6,12},{7,4},{8,25},{9,17}... | collective-permute-start | bytes 196616 | tf_op jit(solution)/shard_map/ppermute | solution.py:95
  119.8 13.1 %collective-permute-start.31 = (bf16[128,1024]{1,0:T(8,128)(2,1)S(1)}, bf16[128,1024]{1,0:T(8,128)(2,1)S(1)}, u32[]{:S(2)}, u32[]{:S(2)}) collective-permute-start(bf16[128,1024]{1,0:T(8,128)(2,1)S(1)} %get-tuple-element.119.refs_0_), channel_id=1, source_target_pairs={{0,2},{1,3},{2,0},{3,1},{4,6},{5,7},{6,4},{7,5},{8,10},{9,11},{10,... | collective-permute-start | bytes 786440 | tf_op jit(solution)/shard_map/ppermute | solution.py:84
  119.8 13.1 %collective-permute-start.32 = (bf16[128,1024]{1,0:T(8,128)(2,1)S(1)}, bf16[128,1024]{1,0:T(8,128)(2,1)S(1)}, u32[]{:S(2)}, u32[]{:S(2)}) collective-permute-start(bf16[128,1024]{1,0:T(8,128)(2,1)S(1)} %get-tuple-element.119.refs_0_), channel_id=1, source_target_pairs={{0,3},{1,2},{2,1},{3,0},{4,7},{5,6},{6,5},{7,4},{8,11},{9,10},{10,... | collective-permute-start | bytes 786440 | tf_op jit(solution)/shard_map/ppermute | solution.py:84
  159.3 148.1 %reduce-scatter.5.cloned.1.call-start = ((), (), s32[]{:S(2)}) async-start(), calls=%async_computation.4 | async-start | bytes 2359296 | tf_op jit(solution)/shard_map/reduce_scatter | solution.py:367
  165.1 11.4 %collective-permute-start.38 = (bf16[128,1024]{1,0:T(8,128)(2,1)}, bf16[128,1024]{1,0:T(8,128)(2,1)S(1)}, u32[]{:S(2)}, u32[]{:S(2)}) collective-permute-start(bf16[128,1024]{1,0:T(8,128)(2,1)} %copy-done.56), channel_id=1, source_target_pairs={{0,3},{1,2},{2,1},{3,0},{4,7},{5,6},{6,5},{7,4},{8,11},{9,10},{10,... | collective-permute-start | bytes 786440 | tf_op jit(solution)/shard_map/ppermute | solution.py:84
  182.6 20.6 %collective-permute-start.39 = (bf16[128,256]{1,0:T(8,128)(2,1)}, bf16[128,256]{1,0:T(8,128)(2,1)S(1)}, u32[]{:S(2)}, u32[]{:S(2)}) collective-permute-start(bf16[128,256]{1,0:T(8,128)(2,1)} %get-tuple-element.138), channel_id=1, source_target_pairs={{0,0},{1,8},{2,16},{3,24},{4,4},{5,12},{6,20},{7,28},{8,1},{9,9},{... | collective-permute-start | bytes 196616 | tf_op jit(solution)/shard_map/ppermute | solution.py:95
  186.3 16.8 %collective-permute-start.40 = (bf16[128,256]{1,0:T(8,128)(2,1)}, bf16[128,256]{1,0:T(8,128)(2,1)S(1)}, u32[]{:S(2)}, u32[]{:S(2)}) collective-permute-start(bf16[128,256]{1,0:T(8,128)(2,1)} %get-tuple-element.139), channel_id=1, source_target_pairs={{0,1},{1,9},{2,17},{3,25},{4,5},{5,13},{6,21},{7,29},{8,0},{9,8},{... | collective-permute-start | bytes 196616 | tf_op jit(solution)/shard_map/ppermute | solution.py:95
  187.8 20.0 %collective-permute-start.41 = (bf16[128,256]{1,0:T(8,128)(2,1)}, bf16[128,256]{1,0:T(8,128)(2,1)S(1)}, u32[]{:S(2)}, u32[]{:S(2)}) collective-permute-start(bf16[128,256]{1,0:T(8,128)(2,1)} %get-tuple-element.140), channel_id=1, source_target_pairs={{0,2},{1,10},{2,18},{3,26},{4,6},{5,14},{6,22},{7,30},{8,3},{9,11}... | collective-permute-start | bytes 196616 | tf_op jit(solution)/shard_map/ppermute | solution.py:95
  187.8 21.5 %collective-permute-start.42 = (bf16[128,256]{1,0:T(8,128)(2,1)}, bf16[128,256]{1,0:T(8,128)(2,1)S(1)}, u32[]{:S(2)}, u32[]{:S(2)}) collective-permute-start(bf16[128,256]{1,0:T(8,128)(2,1)} %get-tuple-element.141), channel_id=1, source_target_pairs={{0,3},{1,11},{2,19},{3,27},{4,7},{5,15},{6,23},{7,31},{8,2},{9,10}... | collective-permute-start | bytes 196616 | tf_op jit(solution)/shard_map/ppermute | solution.py:95
  199.5 61.2 %collective-permute-start.58 = (bf16[4,128,1024]{2,1,0:T(8,128)(2,1)}, bf16[4,128,1024]{2,1,0:T(8,128)(2,1)}, u32[]{:S(2)}, u32[]{:S(2)}) collective-permute-start(bf16[4,128,1024]{2,1,0:T(8,128)(2,1)} %get-tuple-element.165), channel_id=1, source_target_pairs={{0,4},{4,0},{8,12},{12,8},{16,20},{20,16},{24,28},{28,24},{1,5},{5... | collective-permute-start | bytes 3145736 | tf_op jit(solution)/shard_map/ppermute | solution.py:87
  224.2 14.6 %collective-permute-start.49 = (bf16[128,384]{1,0:T(8,128)(2,1)S(1)}, bf16[128,384]{1,0:T(8,128)(2,1)S(1)}, u32[]{:S(2)}, u32[]{:S(2)}) collective-permute-start(bf16[128,384]{1,0:T(8,128)(2,1)S(1)} %get-tuple-element.145), channel_id=1, source_target_pairs={{0,12},{4,8},{8,4},{12,0},{16,28},{20,24},{24,20},{28,16},{1,13},{... | collective-permute-start | bytes 294920 | tf_op jit(solution)/shard_map/ppermute | solution.py:87
  226.3 15.8 %collective-permute-start.50 = (bf16[128,384]{1,0:T(8,128)(2,1)S(1)}, bf16[128,384]{1,0:T(8,128)(2,1)S(1)}, u32[]{:S(2)}, u32[]{:S(2)}) collective-permute-start(bf16[128,384]{1,0:T(8,128)(2,1)S(1)} %get-tuple-element.146), channel_id=1, source_target_pairs={{0,16},{4,20},{8,24},{12,28},{16,0},{20,4},{24,8},{28,12},{1,17},{... | collective-permute-start | bytes 294920 | tf_op jit(solution)/shard_map/ppermute | solution.py:87
  226.4 23.5 %collective-permute-start.51 = (bf16[128,384]{1,0:T(8,128)(2,1)S(1)}, bf16[128,384]{1,0:T(8,128)(2,1)S(1)}, u32[]{:S(2)}, u32[]{:S(2)}) collective-permute-start(bf16[128,384]{1,0:T(8,128)(2,1)S(1)} %get-tuple-element.147), channel_id=1, source_target_pairs={{0,20},{4,16},{8,28},{12,24},{16,4},{20,0},{24,12},{28,8},{1,21},{... | collective-permute-start | bytes 294920 | tf_op jit(solution)/shard_map/ppermute | solution.py:87
  231.8 18.1 %collective-permute-start.52 = (bf16[128,384]{1,0:T(8,128)(2,1)S(1)}, bf16[128,384]{1,0:T(8,128)(2,1)S(1)}, u32[]{:S(2)}, u32[]{:S(2)}) collective-permute-start(bf16[128,384]{1,0:T(8,128)(2,1)S(1)} %get-tuple-element.148), channel_id=1, source_target_pairs={{0,24},{4,28},{8,16},{12,20},{16,8},{20,12},{24,0},{28,4},{1,25},{... | collective-permute-start | bytes 294920 | tf_op jit(solution)/shard_map/ppermute | solution.py:87
  238.7 13.6 %collective-permute-start.53 = (bf16[128,384]{1,0:T(8,128)(2,1)S(1)}, bf16[128,384]{1,0:T(8,128)(2,1)S(1)}, u32[]{:S(2)}, u32[]{:S(2)}) collective-permute-start(bf16[128,384]{1,0:T(8,128)(2,1)S(1)} %get-tuple-element.149), channel_id=1, source_target_pairs={{0,28},{4,24},{8,20},{12,16},{16,12},{20,8},{24,4},{28,0},{1,29},{... | collective-permute-start | bytes 294920 | tf_op jit(solution)/shard_map/ppermute | solution.py:87
  242.1 21.2 %collective-permute-start.33 = (bf16[128,1024]{1,0:T(8,128)(2,1)}, bf16[128,1024]{1,0:T(8,128)(2,1)}, u32[]{:S(2)}, u32[]{:S(2)}) collective-permute-start(bf16[128,1024]{1,0:T(8,128)(2,1)} %get-tuple-element.123), channel_id=1, source_target_pairs={{0,1},{1,0},{2,3},{3,2},{4,5},{5,4},{6,7},{7,6},{8,9},{9,8},{10,11... | collective-permute-start | bytes 786440 | tf_op jit(solution)/shard_map/ppermute | solution.py:84
  249.9 13.4 %collective-permute-start.34 = (bf16[128,1024]{1,0:T(8,128)(2,1)}, bf16[128,1024]{1,0:T(8,128)(2,1)}, u32[]{:S(2)}, u32[]{:S(2)}) collective-permute-start(bf16[128,1024]{1,0:T(8,128)(2,1)} %get-tuple-element.124), channel_id=1, source_target_pairs={{0,2},{1,3},{2,0},{3,1},{4,6},{5,7},{6,4},{7,5},{8,10},{9,11},{10,... | collective-permute-start | bytes 786440 | tf_op jit(solution)/shard_map/ppermute | solution.py:84
  249.9 15.1 %collective-permute-start.35 = (bf16[128,1024]{1,0:T(8,128)(2,1)}, bf16[128,1024]{1,0:T(8,128)(2,1)}, u32[]{:S(2)}, u32[]{:S(2)}) collective-permute-start(bf16[128,1024]{1,0:T(8,128)(2,1)} %get-tuple-element.125), channel_id=1, source_target_pairs={{0,3},{1,2},{2,1},{3,0},{4,7},{5,6},{6,5},{7,4},{8,11},{9,10},{10,... | collective-permute-start | bytes 786440 | tf_op jit(solution)/shard_map/ppermute | solution.py:84
  260.3 16.1 %collective-permute-start.57 = (bf16[4,144,768]{2,1,0:T(8,128)(2,1)}, bf16[4,144,768]{2,1,0:T(8,128)(2,1)}, u32[]{:S(2)}, u32[]{:S(2)}) collective-permute-start(bf16[4,144,768]{2,1,0:T(8,128)(2,1)} %get-tuple-element.162), channel_id=1, source_target_pairs={{0,4},{4,0},{8,12},{12,8},{16,20},{20,16},{24,28},{28,24},{1,5},{5... | collective-permute-start | bytes 2654216 | tf_op jit(solution)/shard_map/ppermute | solution.py:87
  263.3 12.9 %collective-permute-start.60 = (bf16[128,1024]{1,0:T(8,128)(2,1)S(1)}, bf16[128,1024]{1,0:T(8,128)(2,1)S(1)}, u32[]{:S(2)}, u32[]{:S(2)}) collective-permute-start(bf16[128,1024]{1,0:T(8,128)(2,1)S(1)} %get-tuple-element.168), channel_id=1, source_target_pairs={{0,2},{1,3},{2,0},{3,1},{4,6},{5,7},{6,4},{7,5},{8,10},{9,11},{10,... | collective-permute-start | bytes 786440 | tf_op jit(solution)/shard_map/ppermute | solution.py:84
  263.3 12.9 %collective-permute-start.61 = (bf16[128,1024]{1,0:T(8,128)(2,1)S(1)}, bf16[128,1024]{1,0:T(8,128)(2,1)S(1)}, u32[]{:S(2)}, u32[]{:S(2)}) collective-permute-start(bf16[128,1024]{1,0:T(8,128)(2,1)S(1)} %get-tuple-element.169), channel_id=1, source_target_pairs={{0,3},{1,2},{2,1},{3,0},{4,7},{5,6},{6,5},{7,4},{8,11},{9,10},{10,... | collective-permute-start | bytes 786440 | tf_op jit(solution)/shard_map/ppermute | solution.py:84
  267.2 14.4 %collective-permute-start.54 = (bf16[128,1024]{1,0:T(8,128)(2,1)S(1)}, bf16[128,1024]{1,0:T(8,128)(2,1)S(1)}, u32[]{:S(2)}, u32[]{:S(2)}) collective-permute-start(bf16[128,1024]{1,0:T(8,128)(2,1)S(1)} %copy-done.55), channel_id=1, source_target_pairs={{0,1},{1,0},{2,3},{3,2},{4,5},{5,4},{6,7},{7,6},{8,9},{9,8},{10,11... | collective-permute-start | bytes 786440 | tf_op jit(solution)/shard_map/ppermute | solution.py:84
  269.9 17.8 %collective-permute-start.55 = (bf16[128,1024]{1,0:T(8,128)(2,1)S(1)}, bf16[128,1024]{1,0:T(8,128)(2,1)S(1)}, u32[]{:S(2)}, u32[]{:S(2)}) collective-permute-start(bf16[128,1024]{1,0:T(8,128)(2,1)S(1)} %copy-done.53), channel_id=1, source_target_pairs={{0,2},{1,3},{2,0},{3,1},{4,6},{5,7},{6,4},{7,5},{8,10},{9,11},{10,... | collective-permute-start | bytes 786440 | tf_op jit(solution)/shard_map/ppermute | solution.py:84
  276.2 11.5 %collective-permute-start.56 = (bf16[128,1024]{1,0:T(8,128)(2,1)S(1)}, bf16[128,1024]{1,0:T(8,128)(2,1)S(1)}, u32[]{:S(2)}, u32[]{:S(2)}) collective-permute-start(bf16[128,1024]{1,0:T(8,128)(2,1)S(1)} %copy-done.51), channel_id=1, source_target_pairs={{0,3},{1,2},{2,1},{3,0},{4,7},{5,6},{6,5},{7,4},{8,11},{9,10},{10,... | collective-permute-start | bytes 786440 | tf_op jit(solution)/shard_map/ppermute | solution.py:84
  277.8 11.2 %collective-permute-start.62 = (bf16[144,1024]{1,0:T(8,128)(2,1)S(1)}, bf16[144,1024]{1,0:T(8,128)(2,1)S(1)}, u32[]{:S(2)}, u32[]{:S(2)}) collective-permute-start(bf16[144,1024]{1,0:T(8,128)(2,1)S(1)} %get-tuple-element.171), channel_id=1, source_target_pairs={{0,8},{4,12},{8,0},{12,4},{16,24},{20,28},{24,16},{28,20},{1,9},{5... | collective-permute-start | bytes 884744 | tf_op jit(solution)/shard_map/ppermute | solution.py:87
  281.7 11.6 %collective-permute-start.63 = (bf16[144,1024]{1,0:T(8,128)(2,1)S(1)}, bf16[144,1024]{1,0:T(8,128)(2,1)S(1)}, u32[]{:S(2)}, u32[]{:S(2)}) collective-permute-start(bf16[144,1024]{1,0:T(8,128)(2,1)S(1)} %get-tuple-element.172), channel_id=1, source_target_pairs={{0,16},{4,20},{8,24},{12,28},{16,0},{20,4},{24,8},{28,12},{1,17},{... | collective-permute-start | bytes 884744 | tf_op jit(solution)/shard_map/ppermute | solution.py:87
  281.7 16.8 %collective-permute-start.64 = (bf16[144,1024]{1,0:T(8,128)(2,1)S(1)}, bf16[144,1024]{1,0:T(8,128)(2,1)S(1)}, u32[]{:S(2)}, u32[]{:S(2)}) collective-permute-start(bf16[144,1024]{1,0:T(8,128)(2,1)S(1)} %get-tuple-element.173), channel_id=1, source_target_pairs={{0,24},{4,28},{8,16},{12,20},{16,8},{20,12},{24,0},{28,4},{1,25},{... | collective-permute-start | bytes 884744 | tf_op jit(solution)/shard_map/ppermute | solution.py:87
  300.9 9.4 %collective-permute-start.65 = (bf16[48,1792]{1,0:T(8,128)(2,1)}, bf16[48,1792]{1,0:T(8,128)(2,1)S(1)}, u32[]{:S(2)}, u32[]{:S(2)}) collective-permute-start(bf16[48,1792]{1,0:T(8,128)(2,1)} %get-tuple-element.177), channel_id=1, source_target_pairs={{0,1},{1,0},{2,3},{3,2},{4,5},{5,4},{6,7},{7,6},{8,9},{9,8},{10,11... | collective-permute-start | bytes 516104 | tf_op jit(solution)/shard_map/ppermute | solution.py:84
  307.4 28.6 %collective-permute-start.68 = (bf16[128,1024]{1,0:T(8,128)(2,1)}, bf16[128,1024]{1,0:T(8,128)(2,1)S(1)}, u32[]{:S(2)}, u32[]{:S(2)}) collective-permute-start(bf16[128,1024]{1,0:T(8,128)(2,1)} %reduce-scatter.5.cloned.1.call-done), channel_id=1, source_target_pairs={{0,0},{1,8},{2,16},{3,24},{4,1},{5,9},{6,17},{7,25},{8,2},{9,10},{... | collective-permute-start | bytes 786440 | tf_op jit(solution)/shard_map/ppermute | solution.py:95
  (96 other events, 659.9 us)
Sparse Core Ops, SparseCore 0:
  28.2 42.0 all-gather.1
  159.4 34.9 reduce-scatter.2
  196.8 53.3 reduce-scatter.4
where the time goes:
time: 345 us; the launch traced here: 343 us
  waiting for transfers between devices  140 us (41%)
  starting transfers between devices  81.5 us (24%)
  Pallas kernels  51.8 us (15%)
  local copies, waits for them, and re-layouts  41.9 us (12%)
  between operations  14.3 us (4%)
  other arithmetic  6.98 us (2%)
  matrix products  6.77 us (2%)
    ppermute x27, waiting for transfers between devices, fsdp_to(): return lax.ppermute(x, 'fsdp', [(f, f ^ k) for f in range(n_f)])  60.1 us
    pallas_call x17, Pallas kernels, call(): pl.pallas_call(kernel, out_shape=outs, in_specs=[pl.BlockSpec(memory_spac...  51.8 us
    ppermute x33, waiting for transfers between devices, ctx_to(): return lax.ppermute(x, 'ctx', [(i, i ^ e) for i in range(n_ctx)])  45.8 us
    unnamed x145, local copies, waits for them, and re-layouts  39.8 us
    ppermute x33, starting transfers between devices, ctx_to(): return lax.ppermute(x, 'ctx', [(i, i ^ e) for i in range(n_ctx)])  38.6 us
    ppermute x9, waiting for transfers between devices, both_to(): return lax.ppermute(x, ('ctx', 'fsdp'), pairs)  34.1 us
    ppermute x27, starting transfers between devices, fsdp_to(): return lax.ppermute(x, 'fsdp', [(f, f ^ k) for f in range(n_f)])  26 us
    ppermute x9, starting transfers between devices, both_to(): return lax.ppermute(x, ('ctx', 'fsdp'), pairs)  16.7 us
  transfers between devices with their start and end apart: 72, of which 36 were waited for; matrix products, arithmetic and copies ran while one was open for 3% of the time, Pallas kernels for 13%

commit v1 on v0

--- a/solution.py
+++ b/solution.py
@@ -61,7 +61,7 @@
     return sum(a.size * a.dtype.itemsize for a in arrays)
 
 
-def call(kernel, outs, idx, ins, scratch=(), flops=0):
+def call(kernel, outs, idx, ins, scratch=(), flops=0, mib=20):
     vmem = pl.BlockSpec(memory_space=pltpu.VMEM)
     return pl.pallas_call(
         kernel,
@@ -69,7 +69,7 @@
         in_specs=[pl.BlockSpec(memory_space=pltpu.SMEM)] + [vmem] * len(ins),
         out_specs=[vmem] * len(outs),
         scratch_shapes=list(scratch),
-        compiler_params=pltpu.CompilerParams(vmem_limit_bytes=20 * 1024 * 1024),
+        compiler_params=pltpu.CompilerParams(vmem_limit_bytes=mib * 1024 * 1024),
         cost_estimate=pl.CostEstimate(
             flops=flops, bytes_accessed=total_bytes(ins) + total_bytes(outs), transcendentals=0
         ),
@@ -307,38 +307,40 @@
 
         def forward(i, *refs):
             a_refs, refs = refs[:n_f], refs[n_f:]
-            own, bias, refs = refs[0], refs[1], refs[2:]
-            got_u, refs = refs[: n_f - 1], refs[n_f - 1 :]
-            other_u, refs = refs[: n_f - 1], refs[n_f - 1 :]
-            full, a_ref, gel, slope_ref = refs
-            fill_rows(full, own, got_u, other_u, i[FI], i[CORE], slice(0, hidden))
+            own_w_ref, bias, refs = refs[0], refs[1], refs[2:]
+            got_u, other_u = refs[: n_f - 1], refs[n_f - 1 : 2 * n_f - 2]
+            up, a_ref, gel, slope_ref = refs[2 * n_f - 2 :]
+            fill_rows(up, own_w_ref, got_u, other_u, i[FI], i[CORE], slice(0, hidden))
             for k in range(n_f):
-                here = slice(k * rows, (k + 1) * rows)
-                a_ref[here, :] = a_refs[k][...]
-                value, slope = gelu_parts(dot(a_refs[k][...], full[...]) + bias[...].astype(F32))
+                here = pl.ds(pl.multiple_of((i[FI] ^ k) * rows, rows), rows)
+                a_two = a_refs[k][...]
+                a_ref[here, :] = a_two
+                value, slope = gelu_parts(dot(a_two, up[...]) + bias[...].astype(F32))
                 gel[here, :] = value.astype(BF)
-                slope_ref[here, :] = slope
+                slope_ref[here, :] = slope.astype(BF)
 
         outs = [
             shaped((width, hidden), BF),
             shaped((all_rows, width), BF),
             shaped((all_rows, hidden), BF),
-            shaped((all_rows, hidden), F32),
+            shaped((all_rows, hidden), BF),
         ]
         full_up, a2_all, gelled, slope = call(
             forward, outs, idx, a2_parts + [own_w, up_bias] + got_w + other_w,
-            flops=2 * all_rows * width * hidden,
-        )
-
-        def backward(i, *refs):
-            dz_nat, slope_ref, down, up, refs = refs[0], refs[1], refs[2], refs[3], refs[4:]
-            dz_ref, du_ref, sum_ref, own, send = refs[0], refs[1], refs[2], refs[3], refs[4:]
+            flops=2 * all_rows * width * hidden, mib=54,
+        )
+        g_down = outer(gelled, dz_all).astype(BF)
+
+        def scatter_ctx(g):
+            return lax.psum_scatter(g, "ctx", scatter_dimension=0, tiled=True)
+
+        part_down = scatter_ctx(g_down)
+
+        def backward(i, dz_ref, slope_ref, down, up, du_ref, sum_ref, own, *send):
             total = jnp.zeros((1, hidden), F32)
             for k in range(n_f):
-                here = slice(k * rows, (k + 1) * rows)
-                dz_k = dz_nat[pl.ds(pl.multiple_of((i[FI] ^ k) * rows, rows), rows), :]
-                dz_ref[here, :] = dz_k
-                d_pre = through(dz_k, down[...]) * slope_ref[here, :]
+                here = pl.ds(pl.multiple_of((i[FI] ^ k) * rows, rows), rows)
+                d_pre = through(dz_ref[here, :], down[...]) * slope_ref[here, :].astype(F32)
                 total = total + jnp.sum(d_pre, axis=0, keepdims=True)
                 d_hidden = d_pre.astype(BF)
                 du_ref[here, :] = d_hidden
@@ -350,23 +352,17 @@
             sum_ref[...] = total
 
         outs = [
-            shaped((all_rows, width), BF),
             shaped((all_rows, hidden), BF),
             shaped((1, hidden), F32),
             shaped((rows, width), F32),
         ] + [shaped((rows, width), BF)] * (n_f - 1)
-        dz_all, d_hidden, up_sum, d_own, *sends = call(
+        d_hidden, up_sum, d_own, *sends = call(
             backward, outs, idx, [dz_all, slope, w_down, full_up],
-            flops=4 * all_rows * width * hidden,
+            flops=4 * all_rows * width * hidden, mib=54,
         )
         got_a = send_f(sends)
-        g_down = outer(gelled, dz_all).astype(BF)
         g_up = outer(a2_all, d_hidden).astype(BF)
 
-        def scatter_ctx(g):
-            return lax.psum_scatter(g, "ctx", scatter_dimension=0, tiled=True)
-
-        part_down = scatter_ctx(g_down)
         part_up = scatter_ctx(g_up)
 
         def second(i, *refs):
@@ -400,22 +396,6 @@
         got = [both_to(sends[m], lambda i, f: (2 * f + i % 2, m ^ (i // 2))) for m in range(n_f)]
         got += [ctx_to(g, 1) for g in got]
 
-        def down(i, gel, w_ref, own, *send):
-            for k in range(n_f):
-                part = dot(gel[k * rows : (k + 1) * rows, :], w_ref[...])
-                if k:
-                    send[k - 1][...] = part.astype(BF)
-                else:
-                    own[...] = part
-
-        outs = [shaped((rows, width), F32)] + [shaped((rows, width), BF)] * (n_f - 1)
-        result, *sends = call(
-            down, outs, idx, [gelled, w_down], flops=2 * all_rows * width * hidden
-        )
-        result = result + mid + small[7]
-        for g in send_f(sends):
-            result = result + g.astype(F32)
-
         def attend_back(i, *refs):
             seq_ref, att_ref, lse_ref, refs = refs[0], refs[1], refs[2], refs[3:]
             got, refs = refs[: 2 * n_f], refs[2 * n_f :]
@@ -508,8 +488,25 @@
 
         outs = [shaped((n_z * per, width), F32)] + [shaped((n_z * per, width), BF)] * (n_f - 1)
         out_own, *sends = call(out_first, outs, idx, [out_keep, away])
-        for g in send_f(sends):
-            out_own = out_own + g.astype(F32)
+        out_got = send_f(sends)
+
+        def out_second(i, own_ref, *refs):
+            got, (own, *send), held = refs[: n_f - 1], refs[n_f - 1 : -1], refs[-1]
+            total = own_ref[...]
+            for g in got:
+                total = total + g[...].astype(F32)
+            held[...] = total
+            own[...] = held[pl.ds(pl.multiple_of(i[Z] * per, per), per), :]
+            for m in range(1, n_z):
+                at = pl.ds(pl.multiple_of((i[Z] ^ m) * per, per), per)
+                send[m - 1][...] = held[at, :].astype(BF)
+
+        outs = [shaped((per, width), F32)] + [shaped((per, width), BF)] * (n_z - 1)
+        out_own, *sends = call(
+            out_second, outs, idx, [out_own] + out_got,
+            [pltpu.VMEM((n_z * per, width), F32)],
+        )
+        out_got = [ctx_to(s, 2 * (m + 1)) for m, s in enumerate(sends)]
 
         def first(i, *refs):
             got, refs = refs[:n_ctx], refs[n_ctx:]
@@ -546,7 +543,7 @@
         d_proj, sums, d_own, *sends = call(
             first, outs, idx, got + n_all + [full_qkv, sums],
             [pltpu.VMEM((n_ctx, rows, 3 * pair), BF)],
-            flops=6 * all_rows * width * wide,
+            flops=6 * all_rows * width * wide, mib=54,
         )
         got_x = send_f(sends)
 
@@ -582,39 +579,63 @@
         )
         away = ctx_to(away, 1)
 
-        out_own = out_own.reshape(n_z, per, width)
-        part_w = 4 * wide
-
-        def over_core(i, keep_ref, got, o_ref, own, *send):
-            def fill(out, at):
-                out[:, : 3 * wide] = (keep_ref[at] + got[at].astype(F32)).astype(out.dtype)
-                out[block:, 3 * wide :] = jnp.zeros((16, wide), out.dtype)
-                for g in range(n_f):
-                    piece = o_ref[at, :, g * wide : (g + 1) * wide]
-                    out[g * per : (g + 1) * per, 3 * wide :] = piece.astype(out.dtype)
-
-            fill(own, i[Z])
+        def over_core(i, keep_ref, got, own, *send):
+            own[...] = keep_ref[i[Z]] + got[i[Z]].astype(F32)
             for m in range(1, n_z):
-                fill(send[m - 1], i[Z] ^ m)
-
-        dims = (block + 16, part_w)
-        outs = [shaped(dims, F32)] + [shaped(dims, BF)] * (n_z - 1)
-        own, *sends = call(over_core, outs, idx, [keep, away, out_own])
+                at = i[Z] ^ m
+                send[m - 1][...] = (keep_ref[at] + got[at].astype(F32)).astype(BF)
+
+        outs = [shaped(dims[1:], F32)] + [shaped(dims[1:], BF)] * (n_z - 1)
+        own, *sends = call(over_core, outs, idx, [keep, away])
         got = [ctx_to(s, 2 * (m + 1)) for m, s in enumerate(sends)]
-        out_down = both_to(
-            part_down, lambda i, f: ((f * n_ctx + i) // n_f, (f * n_ctx + i) % n_f)
-        ).astype(F32)
+        low_down = both_to(part_down, lambda i, f: ((f * n_ctx + i) // n_f, (f * n_ctx + i) % n_f))
+
+        def down(i, gel, w_ref, own, *send):
+            for k in range(n_f):
+                here = pl.ds(pl.multiple_of((i[FI] ^ k) * rows, rows), rows)
+                part = dot(gel[here, :], w_ref[...])
+                if k:
+                    send[k - 1][...] = part.astype(BF)
+                else:
+                    own[...] = part
+
+        outs = [shaped((rows, width), F32)] + [shaped((rows, width), BF)] * (n_f - 1)
+        z_own, *sends = call(down, outs, idx, [gelled, w_down], flops=2 * all_rows * width * hidden)
+        z_got = send_f(sends)
+
+        def add_up(i, own, mid_ref, small_ref, *refs):
+            total = own[...]
+            for g in refs[:-1]:
+                total = total + g[...].astype(F32)
+            refs[-1][...] = total + mid_ref[...] + small_ref[7:8, :]
+
+        (result,) = call(add_up, [shaped((rows, width), F32)], idx, [z_own, mid, small] + z_got)
+
+        def input_grad(i, x_ref, dmid_ref, small_ref, low_ref, own, *refs):
+            got, (out, wider) = refs[:-2], refs[-2:]
+            normed, inv = normalize(x_ref[...])
+            d_a = own[...]
+            for g in got:
+                d_a = d_a + g[...].astype(F32)
+            out[...] = dmid_ref[...] + norm_back(d_a * small_ref[0:1, :], normed, inv)
+            wider[...] = low_ref[...].astype(F32)
+
+        outs = [shaped((rows, width), F32), shaped(low_down.shape, F32)]
+        d_input, out_down = call(input_grad, outs, idx, [x, d_mid, small, low_down, d_own] + got_x)
 
         def over_z(i, *refs):
-            own_ref, got, up_ref, refs = refs[0], refs[1:n_z], refs[n_z], refs[n_z + 1 :]
+            own_ref, got, refs = refs[0], refs[1:n_z], refs[n_z:]
+            o_ref, got_o, up_ref, refs = refs[0], refs[1:n_z], refs[n_z], refs[n_z + 1 :]
             out_ref, own, send, (held, held_up) = refs[0], refs[1], refs[2:-2], refs[-2:]
+            out = o_ref[...]
+            for g in got_o:
+                out = out + g[...].astype(F32)
+            out_ref[...] = out
             total = own_ref[...]
             for g in got:
                 total = total + g[...].astype(F32)
             held[...] = total
             held_up[...] = up_ref[...].astype(F32)
-            for g in range(n_f):
-                out_ref[:, g * wide : (g + 1) * wide] = total[g * per : (g + 1) * per, 3 * wide :]
             for k in range(n_f):
                 at = pl.ds(pl.multiple_of((i[FI] ^ k) * per, per), per)
                 out = send[k - 1] if k else own
@@ -626,13 +647,14 @@
         dims = (per + 16, 3 * wide + hidden)
         outs = [shaped((per, width), F32), shaped(dims, F32)] + [shaped(dims, BF)] * (n_f - 1)
         out_out, own, *sends = call(
-            over_z, outs, idx, [own] + got + [part_up],
-            [pltpu.VMEM((block + 16, part_w), F32), pltpu.VMEM((block, hidden), F32)],
+            over_z, outs, idx, [own] + got + [out_own] + out_got + [part_up],
+            [pltpu.VMEM((block + 16, 3 * wide), F32), pltpu.VMEM((block, hidden), F32)],
+            mib=54,
         )
         got = send_f(sends)
 
         def last(i, own_ref, *refs):
-            got, (out, up, small_ref) = refs[: n_f - 1], refs[n_f - 1 :]
+            got, (out, up, small_ref, bias_ref) = refs[: n_f - 1], refs[n_f - 1 :]
             total = own_ref[per:, :block]
             for k in range(n_f):
                 src = got[k - 1] if k else own_ref
@@ -643,19 +665,16 @@
                 up[:, at] = src[:per, 3 * wide :].astype(F32)
                 if k:
                     total = total + src[per:, :block].astype(F32)
-            small_ref[...] = total
+            share, ups = total[:8, :per], total[8:9, :per_up]
+            for g in range(1, n_f):
+                share = jnp.where(i[FI] == g, total[:8, g * per : (g + 1) * per], share)
+                ups = jnp.where(i[FI] == g, total[8 + g : 9 + g, :per_up], ups)
+            small_ref[...] = share
+            bias_ref[...] = ups
 
         outs = [shaped((per, 3 * width), F32), shaped((per, n_f * hidden), F32)]
-        outs += [shaped((16, block), F32)]
-        out_qkv, out_up, tile = call(last, outs, idx, [own] + got)
-        out_small = lax.dynamic_slice(tile, (0, fi * per), (8, per))
-        out_upb = lax.dynamic_slice(tile, (8 + fi, 0), (1, per_up))
-
-        normed, inv = normalize(x)
-        d_a = d_own
-        for g in got_x:
-            d_a = d_a + g.astype(F32)
-        d_input = d_mid + norm_back(d_a * small[0], normed, inv)
+        outs += [shaped((8, per), F32), shaped((1, per_up), F32)]
+        out_qkv, out_up, out_small, out_upb = call(last, outs, idx, [own] + got)
 
         shape = (seqs, slots, blk, width)
         return (

time: 345 us -> 336 us (0.974)
  the two profiles are of different devices: /device:TPU:25 before, /device:TPU:0 now
where the time goes in v1:
time: 336 us
  waiting for transfers between devices  123 us (37%)
  starting transfers between devices  110 us (33%)
  Pallas kernels  62.5 us (19%)
  local copies, waits for them, and re-layouts  16 us (5%)
  between operations  14.5 us (4%)
  matrix products  8.06 us (2%)
    ppermute x27, waiting for transfers between devices, fsdp_to(): return lax.ppermute(x, 'fsdp', [(f, f ^ k) for f in range(n_f)])  68.5 us
    pallas_call x20, Pallas kernels, call(): pl.pallas_call(kernel, out_shape=outs, in_specs=[pl.BlockSpec(memory_spac...  62.5 us
    ppermute x36, starting transfers between devices, ctx_to(): return lax.ppermute(x, 'ctx', [(i, i ^ e) for i in range(n_ctx)])  45.2 us
    ppermute x27, starting transfers between devices, fsdp_to(): return lax.ppermute(x, 'fsdp', [(f, f ^ k) for f in range(n_f)])  41.3 us
    ppermute x36, waiting for transfers between devices, ctx_to(): return lax.ppermute(x, 'ctx', [(i, i ^ e) for i in range(n_ctx)])  36.2 us
    ppermute x9, starting transfers between devices, both_to(): return lax.ppermute(x, ('ctx', 'fsdp'), pairs)  23.4 us
    ppermute x9, waiting for transfers between devices, both_to(): return lax.ppermute(x, ('ctx', 'fsdp'), pairs)  18.5 us
    unnamed x141, local copies, waits for them, and re-layouts  14.7 us
  transfers between devices with their start and end apart: 75, of which 30 were waited for; matrix products, arithmetic and copies ran while one was open for 2% of the time, Pallas kernels for 15%

profile of v1, /device:TPU:0, one launch (start us, length us, event | category | flops | bytes accessed | tf_op | source)
XLA Modules:
  0.0 335.6 jit_solution(13373261718111513919)
XLA Ops:
  14.2 3.0 collective-permute-start
  24.4 7.6 %collective-permute-done.1.refs_2_.refs_10_ = bf16[128,1024]{1,0:T(8,128)(2,1)} collective-permute-done((bf16[128,1024]{1,0:T(8,128)(2,1)S(1)}, bf16[128,1024]{1,0:T(8,128)(2,1)}, u32[]{:S(2)}, u32[]{:S(2)}) %collective-permute-start.1) | collective-permute-done | bytes 262176 | tf_op jit(solution)/shard_map/ppermute | solution.py:84
  43.6 2.5 shard_map.170
  48.8 4.9 %collective-permute-done.24.refs_11_.refs_6_ = bf16[128,2048]{1,0:T(8,128)(2,1)S(1)} collective-permute-done((bf16[128,2048]{1,0:T(8,128)(2,1)S(1)}, bf16[128,2048]{1,0:T(8,128)(2,1)S(1)}, u32[]{:S(2)}, u32[]{:S(2)}) %collective-permute-start.24) | collective-permute-done | bytes 524320 | tf_op jit(solution)/shard_map/ppermute | solution.py:84
  53.7 2.6 collective-permute-start.12
  56.3 3.7 %collective-permute-done.25.refs_12_.refs_7_ = bf16[128,2048]{1,0:T(8,128)(2,1)S(1)} collective-permute-done((bf16[128,2048]{1,0:T(8,128)(2,1)S(1)}, bf16[128,2048]{1,0:T(8,128)(2,1)S(1)}, u32[]{:S(2)}, u32[]{:S(2)}) %collective-permute-start.25) | collective-permute-done | bytes 524320 | tf_op jit(solution)/shard_map/ppermute | solution.py:84
  60.1 11.1 %collective-permute-done.26.refs_13_.refs_8_ = bf16[128,2048]{1,0:T(8,128)(2,1)S(1)} collective-permute-done((bf16[128,2048]{1,0:T(8,128)(2,1)S(1)}, bf16[128,2048]{1,0:T(8,128)(2,1)S(1)}, u32[]{:S(2)}, u32[]{:S(2)}) %collective-permute-start.26) | collective-permute-done | bytes 524320 | tf_op jit(solution)/shard_map/ppermute | solution.py:84
  75.3 6.3 %collective-permute-done.13.refs_5_ = bf16[128,384]{1,0:T(8,128)(2,1)S(1)} collective-permute-done((bf16[128,384]{1,0:T(8,128)(2,1)S(1)}, bf16[128,384]{1,0:T(8,128)(2,1)S(1)}, u32[]{:S(2)}, u32[]{:S(2)}) %collective-permute-start.13) | collective-permute-done | bytes 98336 | tf_op jit(solution)/shard_map/ppermute | solution.py:87
  81.6 3.4 %collective-permute-start.15 = (bf16[128,384]{1,0:T(8,128)(2,1)S(1)}, bf16[128,384]{1,0:T(8,128)(2,1)S(1)}, u32[]{:S(2)}, u32[]{:S(2)}) collective-permute-start(bf16[128,384]{1,0:T(8,128)(2,1)S(1)} %get-tuple-element.116), channel_id=1, source_target_pairs={{0,28},{4,24},{8,20},{12,16},{16,12},{20,8},{24,4},{28,0},{1,29},{... | collective-permute-start | bytes 294920 | tf_op jit(solution)/shard_map/ppermute | solution.py:87
  85.4 2.7 collective-permute-done.15.refs_7_
  88.1 6.4 %shard_map.171 = (bf16[1024,384]{1,0:T(8,128)(2,1)S(1)}, bf16[1024,128]{1,0:T(8,128)(2,1)S(1)}, f32[1024,128]{1,0:T(8,128)S(1)}, bf16[256,128]{1,0:T(8,128)(2,1)...) custom-call(s32[24]{0:T(128)S(1)} %concatenate.6.i, ...), custom_call_target="tpu_custom_call" | custom-call | flops 536870912 | bytes 2621440 | tf_op jit(solution)/shard_map/pallas_call | solution.py:66
  96.1 4.2 %collective-permute-start.17 = (bf16[256,128]{1,0:T(8,128)(2,1)S(1)}, bf16[256,128]{1,0:T(8,128)(2,1)S(1)}, u32[]{:S(2)}, u32[]{:S(2)}) collective-permute-start(bf16[256,128]{1,0:T(8,128)(2,1)S(1)} %get-tuple-element.118), channel_id=1, source_target_pairs={{0,8},{1,0},{2,24},{3,16},{4,12},{5,4},{6,28},{7,20},{8,9},{9,1},{... | collective-permute-start | bytes 196616 | tf_op jit(solution)/shard_map/ppermute | solution.py:95
  100.3 3.7 %collective-permute-start.18 = (bf16[256,128]{1,0:T(8,128)(2,1)S(1)}, bf16[256,128]{1,0:T(8,128)(2,1)S(1)}, u32[]{:S(2)}, u32[]{:S(2)}) collective-permute-start(bf16[256,128]{1,0:T(8,128)(2,1)S(1)} %get-tuple-element.119), channel_id=1, source_target_pairs={{0,16},{1,24},{2,0},{3,8},{4,20},{5,28},{6,4},{7,12},{8,17},{9,25}... | collective-permute-start | bytes 196616 | tf_op jit(solution)/shard_map/ppermute | solution.py:95
  104.0 6.2 %collective-permute-start.19 = (bf16[256,128]{1,0:T(8,128)(2,1)S(1)}, bf16[256,128]{1,0:T(8,128)(2,1)S(1)}, u32[]{:S(2)}, u32[]{:S(2)}) collective-permute-start(bf16[256,128]{1,0:T(8,128)(2,1)S(1)} %get-tuple-element.120), channel_id=1, source_target_pairs={{0,24},{1,16},{2,8},{3,0},{4,28},{5,20},{6,12},{7,4},{8,25},{9,17}... | collective-permute-start | bytes 196616 | tf_op jit(solution)/shard_map/ppermute | solution.py:95
  110.2 2.9 collective-permute-done.19.refs_5_.refs_3_
  118.3 4.3 %collective-permute-start.30 = (bf16[128,1024]{1,0:T(8,128)(2,1)S(1)}, bf16[128,1024]{1,0:T(8,128)(2,1)S(1)}, u32[]{:S(2)}, u32[]{:S(2)}) collective-permute-start(bf16[128,1024]{1,0:T(8,128)(2,1)S(1)} %get-tuple-element.125.refs_0_), channel_id=1, source_target_pairs={{0,1},{1,0},{2,3},{3,2},{4,5},{5,4},{6,7},{7,6},{8,9},{9,8},{10,11... | collective-permute-start | bytes 786440 | tf_op jit(solution)/shard_map/ppermute | solution.py:84
  124.1 5.7 %collective-permute-done.30.refs_1_ = bf16[128,1024]{1,0:T(8,128)(2,1)S(1)} collective-permute-done((bf16[128,1024]{1,0:T(8,128)(2,1)S(1)}, bf16[128,1024]{1,0:T(8,128)(2,1)S(1)}, u32[]{:S(2)}, u32[]{:S(2)}) %collective-permute-start.30) | collective-permute-done | bytes 262176 | tf_op jit(solution)/shard_map/ppermute | solution.py:84
  129.8 6.6 %collective-permute-done.31.refs_2_ = bf16[128,1024]{1,0:T(8,128)(2,1)S(1)} collective-permute-done((bf16[128,1024]{1,0:T(8,128)(2,1)S(1)}, bf16[128,1024]{1,0:T(8,128)(2,1)S(1)}, u32[]{:S(2)}, u32[]{:S(2)}) %collective-permute-start.31) | collective-permute-done | bytes 262176 | tf_op jit(solution)/shard_map/ppermute | solution.py:84
  137.7 6.4 %shard_map.174 = (bf16[1024,1024]{1,0:T(8,128)(2,1)}, bf16[512,1024]{1,0:T(8,128)(2,1)}, bf16[512,1024]{1,0:T(8,128)(2,1)}, bf16[512,1024]{1,0:T(8,128)(2,1)}) custom-call(s32[24]{0:T(128)} %copy-done.26, bf16[128,1024]{1,0:T(8,128)(2,1)} %copy-done.24, bf16[128,1024]{1,0:T(8,128)(2,1)} %copy-done.54, bf16[128,1024]{1,0:T(8,128)(2,1)} %copy-done.55, ...), custom_call_target="tpu_custom_call" | custom-call | flops 1073741824 | bytes 10487808 | tf_op jit(solution)/shard_map/pallas_call | solution.py:66
  144.1 9.3 %shard_map.177 = (bf16[512,1024]{1,0:T(8,128)(2,1)}, f32[1,1024]{1,0:T(1,128)}, f32[128,1024]{1,0:T(8,128)}, bf16[128,1024]{1,0:T(8,128)(2,1)}, bf16[128,1024]{1,0:T(8,128)(2,1)}, /*index=5*/bf16[128,1024]{1,0:T(8,128)(2,1)}) custom-call(s32[24]{0:T(128)} %copy-done.26, bf16[512,1024]{1,0:T(8,128)(2,1)} %all-gather.2.cloned.1.call-done.dz_ref, ...), custom_call_target="tpu_custom_call" | custom-call | flops 2147483648 | bytes 8654848 | tf_op jit(solution)/shard_map/pallas_call | solution.py:66
  153.4 3.9 %convolution_convert_fusion = bf16[1024,1024]{1,0:T(8,128)(2,1)} fusion(bf16[512,1024]{1,0:T(8,128)(2,1)S(1)} %copy-done.69, bf16[512,1024]{1,0:T(8,128)(2,1)} %get-tuple-element.186), kind=kOutput, calls=%fused_computation | convolution fusion | flops 1074790400 | bytes 4194304 | tf_op jit(solution)/shard_map/dot_general | solution.py:49
  157.4 4.2 %convolution_convert_fusion.1 = bf16[1024,1024]{1,0:T(8,128)(2,1)} fusion(bf16[512,1024]{1,0:T(8,128)(2,1)} %get-tuple-element.126.gel, bf16[512,1024]{1,0:T(8,128)(2,1)} %all-gather.2.cloned.1.call-done.dz_ref), kind=kOutput, calls=%fused_computation.1 | convolution fusion | flops 1074790400 | bytes 4194304 | tf_op jit(solution)/shard_map/dot_general | solution.py:49
  162.7 2.4 collective-permute-start.38
  165.1 5.9 %collective-permute-done.36.refs_5_ = bf16[128,1024]{1,0:T(8,128)(2,1)S(1)} collective-permute-done((bf16[128,1024]{1,0:T(8,128)(2,1)}, bf16[128,1024]{1,0:T(8,128)(2,1)S(1)}, u32[]{:S(2)}, u32[]{:S(2)}) %collective-permute-start.36) | collective-permute-done | bytes 262176 | tf_op jit(solution)/shard_map/ppermute | solution.py:84
  171.0 3.7 %collective-permute-done.37.refs_6_ = bf16[128,1024]{1,0:T(8,128)(2,1)S(1)} collective-permute-done((bf16[128,1024]{1,0:T(8,128)(2,1)}, bf16[128,1024]{1,0:T(8,128)(2,1)S(1)}, u32[]{:S(2)}, u32[]{:S(2)}) %collective-permute-start.37) | collective-permute-done | bytes 262176 | tf_op jit(solution)/shard_map/ppermute | solution.py:84
  179.5 3.2 collective-permute-start.41
  182.6 3.2 collective-permute-start.42
  185.8 15.5 %collective-permute-done.41.refs_4_ = bf16[128,256]{1,0:T(8,128)(2,1)S(1)} collective-permute-done((bf16[128,256]{1,0:T(8,128)(2,1)S(1)}, bf16[128,256]{1,0:T(8,128)(2,1)S(1)}, u32[]{:S(2)}, u32[]{:S(2)}) %collective-permute-start.41) | collective-permute-done | bytes 65568 | tf_op jit(solution)/shard_map/ppermute | solution.py:95
  204.0 10.2 %shard_map.179 = (f32[8,128]{1,0:T(8,128)S(1)}, bf16[128,384]{1,0:T(8,128)(2,1)S(1)}, bf16[128,384]{1,0:T(8,128)(2,1)S(1)}, bf16[128,384]{1,0:T(8,128)(2,1)S(1)}...) custom-call(s32[24]{0:T(128)S(1)} %copy-done.27, ...), custom_call_target="tpu_custom_call" | custom-call | flops 1342177280 | bytes 2887680 | tf_op jit(solution)/shard_map/pallas_call | solution.py:66
  216.7 3.2 collective-permute-start.51
  219.9 5.1 %collective-permute-done.49.refs_2_ = bf16[128,384]{1,0:T(8,128)(2,1)S(1)} collective-permute-done((bf16[128,384]{1,0:T(8,128)(2,1)S(1)}, bf16[128,384]{1,0:T(8,128)(2,1)S(1)}, u32[]{:S(2)}, u32[]{:S(2)}) %collective-permute-start.49) | collective-permute-done | bytes 98336 | tf_op jit(solution)/shard_map/ppermute | solution.py:87
  225.0 5.8 %collective-permute-start.53 = (bf16[128,384]{1,0:T(8,128)(2,1)S(1)}, bf16[128,384]{1,0:T(8,128)(2,1)S(1)}, u32[]{:S(2)}, u32[]{:S(2)}) collective-permute-start(bf16[128,384]{1,0:T(8,128)(2,1)S(1)} %get-tuple-element.154), channel_id=1, source_target_pairs={{0,24},{4,28},{8,16},{12,20},{16,8},{20,12},{24,0},{28,4},{1,25},{... | collective-permute-start | bytes 294920 | tf_op jit(solution)/shard_map/ppermute | solution.py:87
  231.3 3.7 %collective-permute-start.54 = (bf16[128,384]{1,0:T(8,128)(2,1)S(1)}, bf16[128,384]{1,0:T(8,128)(2,1)S(1)}, u32[]{:S(2)}, u32[]{:S(2)}) collective-permute-start(bf16[128,384]{1,0:T(8,128)(2,1)S(1)} %get-tuple-element.155), channel_id=1, source_target_pairs={{0,28},{4,24},{8,20},{12,16},{16,12},{20,8},{24,4},{28,0},{1,29},{... | collective-permute-start | bytes 294920 | tf_op jit(solution)/shard_map/ppermute | solution.py:87
  235.0 6.3 %collective-permute-done.53.refs_6_ = bf16[128,384]{1,0:T(8,128)(2,1)S(1)} collective-permute-done((bf16[128,384]{1,0:T(8,128)(2,1)S(1)}, bf16[128,384]{1,0:T(8,128)(2,1)S(1)}, u32[]{:S(2)}, u32[]{:S(2)}) %collective-permute-start.53) | collective-permute-done | bytes 98336 | tf_op jit(solution)/shard_map/ppermute | solution.py:87
  241.3 3.1 collective-permute-done.54.refs_7_
  245.0 5.2 %shard_map.180 = (bf16[512,768]{1,0:T(8,128)(2,1)}, f32[8,1024]{1,0:T(8,128)}, f32[128,1024]{1,0:T(8,128)}, bf16[128,1024]{1,0:T(8,128)(2,1)}, bf16[128,1024]{1,0:T(8,128)(2,1)}, /*index=5*/bf16[128,1024]{1,0:T(8,128)(2,1)}) custom-call(s32[24]{0:T(128)} %copy-done.26, bf16[128,384]{1,0:T(8,128)(2,1)} %copy-done.30, bf16[128,384]{1,0:T(8,128)(2,1)} %copy-done.60, ...), custom_call_target="tpu_custom_call" | custom-call | flops 805306368 | bytes 5570560 | tf_op jit(solution)/shard_map/pallas_call | solution.py:66
  255.8 3.2 collective-permute-start.65
  259.7 4.9 %collective-permute-start.59 = (bf16[144,768]{1,0:T(8,128)(2,1)S(1)}, bf16[144,768]{1,0:T(8,128)(2,1)S(1)}, u32[]{:S(2)}, u32[]{:S(2)}) collective-permute-start(bf16[144,768]{1,0:T(8,128)(2,1)S(1)} %get-tuple-element.171), channel_id=1, source_target_pairs={{0,8},{4,12},{8,0},{12,4},{16,24},{20,28},{24,16},{28,20},{1,9},{5... | collective-permute-start | bytes 663560 | tf_op jit(solution)/shard_map/ppermute | solution.py:87
  267.6 2.5 shard_map.175
  273.5 4.0 %collective-permute-start.66 = (bf16[32,1024]{1,0:T(8,128)(2,1)S(1)}, bf16[32,1024]{1,0:T(8,128)(2,1)S(1)}, u32[]{:S(2)}, u32[]{:S(2)}) collective-permute-start(bf16[32,1024]{1,0:T(8,128)(2,1)S(1)} %get-tuple-element.182), channel_id=1, source_target_pairs={{0,8},{4,12},{8,0},{12,4},{16,24},{20,28},{24,16},{28,20},{1,9},{5... | collective-permute-start | bytes 196616 | tf_op jit(solution)/shard_map/ppermute | solution.py:87
  279.6 3.8 %collective-permute-done.60.refs_2_ = bf16[144,768]{1,0:T(8,128)(2,1)S(1)} collective-permute-done((bf16[144,768]{1,0:T(8,128)(2,1)S(1)}, bf16[144,768]{1,0:T(8,128)(2,1)S(1)}, u32[]{:S(2)}, u32[]{:S(2)}) %collective-permute-start.60) | collective-permute-done | bytes 221216 | tf_op jit(solution)/shard_map/ppermute | solution.py:87
  283.4 2.6 collective-permute-start.35
  285.9 2.6 collective-permute-start.67
  289.5 3.0 collective-permute-done.67.refs_6_
  294.7 2.7 shard_map.187
  312.8 4.4 %collective-permute-done.55.refs_0_ = bf16[128,1024]{1,0:T(8,128)(2,1)S(1)} collective-permute-done((bf16[128,1024]{1,0:T(8,128)(2,1)}, bf16[128,1024]{1,0:T(8,128)(2,1)S(1)}, u32[]{:S(2)}, u32[]{:S(2)}) %collective-permute-start.55) | collective-permute-done | bytes 262176 | tf_op jit(solution)/shard_map/ppermute | solution.py:84
  317.2 2.3 collective-permute-done.56.refs_1_
  319.5 7.6 %collective-permute-done.57.refs_2_ = bf16[128,1024]{1,0:T(8,128)(2,1)S(1)} collective-permute-done((bf16[128,1024]{1,0:T(8,128)(2,1)}, bf16[128,1024]{1,0:T(8,128)(2,1)S(1)}, u32[]{:S(2)}, u32[]{:S(2)}) %collective-permute-start.57) | collective-permute-done | bytes 262176 | tf_op jit(solution)/shard_map/ppermute | solution.py:84
  (274 shorter events, 89.6 us)
Async XLA Ops:
  7.2 137.0 %all-gather.2.cloned.1.call-start = ((), (), s32[]{:S(2)}) async-start(), calls=%async_computation.2 | async-start | bytes 1310720 | tf_op jit(solution)/shard_map/all_gather | solution.py:219
  14.2 10.2 %collective-permute-start = (bf16[128,1024]{1,0:T(8,128)(2,1)S(1)}, bf16[128,1024]{1,0:T(8,128)(2,1)}, u32[]{:S(2)}, u32[]{:S(2)}) collective-permute-start(bf16[128,1024]{1,0:T(8,128)(2,1)S(1)} %get-tuple-element.103.refs_0_.refs_8_), channel_id=1, source_target_pairs={{0,1},{1,0},{2,3},{3,2},{4,5},{5,4},{6,7},{7,6},{8,9},{9,8},{10,11... | collective-permute-start | bytes 786440 | tf_op jit(solution)/shard_map/ppermute | solution.py:84
  17.1 14.9 %collective-permute-start.1 = (bf16[128,1024]{1,0:T(8,128)(2,1)S(1)}, bf16[128,1024]{1,0:T(8,128)(2,1)}, u32[]{:S(2)}, u32[]{:S(2)}) collective-permute-start(bf16[128,1024]{1,0:T(8,128)(2,1)S(1)} %get-tuple-element.103.refs_0_.refs_8_), channel_id=1, source_target_pairs={{0,2},{1,3},{2,0},{3,1},{4,6},{5,7},{6,4},{7,5},{8,10},{9,11},{10,... | collective-permute-start | bytes 786440 | tf_op jit(solution)/shard_map/ppermute | solution.py:84
  18.7 13.4 %collective-permute-start.2 = (bf16[128,1024]{1,0:T(8,128)(2,1)S(1)}, bf16[128,1024]{1,0:T(8,128)(2,1)}, u32[]{:S(2)}, u32[]{:S(2)}) collective-permute-start(bf16[128,1024]{1,0:T(8,128)(2,1)S(1)} %get-tuple-element.103.refs_0_.refs_8_), channel_id=1, source_target_pairs={{0,3},{1,2},{2,1},{3,0},{4,7},{5,6},{6,5},{7,4},{8,11},{9,10},{10,... | collective-permute-start | bytes 786440 | tf_op jit(solution)/shard_map/ppermute | solution.py:84
  18.7 16.1 %collective-permute-start.3 = (bf16[144,768]{1,0:T(8,128)(2,1)}, bf16[144,768]{1,0:T(8,128)(2,1)}, u32[]{:S(2)}, u32[]{:S(2)}) collective-permute-start(bf16[144,768]{1,0:T(8,128)(2,1)} %get-tuple-element.105), channel_id=1, source_target_pairs={{0,1},{1,0},{2,3},{3,2},{4,5},{5,4},{6,7},{7,6},{8,9},{9,8},{10,11... | collective-permute-start | bytes 663560 | tf_op jit(solution)/shard_map/ppermute | solution.py:84
  20.6 19.5 %collective-permute-start.4 = (bf16[144,768]{1,0:T(8,128)(2,1)}, bf16[144,768]{1,0:T(8,128)(2,1)}, u32[]{:S(2)}, u32[]{:S(2)}) collective-permute-start(bf16[144,768]{1,0:T(8,128)(2,1)} %get-tuple-element.106), channel_id=1, source_target_pairs={{0,2},{1,3},{2,0},{3,1},{4,6},{5,7},{6,4},{7,5},{8,10},{9,11},{10,... | collective-permute-start | bytes 663560 | tf_op jit(solution)/shard_map/ppermute | solution.py:84
  32.1 262.6 %reduce-scatter.5.cloned.1.call-start = ((), (), s32[]{:S(2)}) async-start(), calls=%async_computation.4 | async-start | bytes 2359296 | tf_op jit(solution)/shard_map/reduce_scatter | solution.py:335
  35.5 18.2 %collective-permute-start.24 = (bf16[128,2048]{1,0:T(8,128)(2,1)S(1)}, bf16[128,2048]{1,0:T(8,128)(2,1)S(1)}, u32[]{:S(2)}, u32[]{:S(2)}) collective-permute-start(bf16[128,2048]{1,0:T(8,128)(2,1)S(1)} %get-tuple-element.122), channel_id=1, source_target_pairs={{0,1},{1,0},{2,3},{3,2},{4,5},{5,4},{6,7},{7,6},{8,9},{9,8},{10,11... | collective-permute-start | bytes 1572872 | tf_op jit(solution)/shard_map/ppermute | solution.py:84
  37.6 22.4 %collective-permute-start.25 = (bf16[128,2048]{1,0:T(8,128)(2,1)S(1)}, bf16[128,2048]{1,0:T(8,128)(2,1)S(1)}, u32[]{:S(2)}, u32[]{:S(2)}) collective-permute-start(bf16[128,2048]{1,0:T(8,128)(2,1)S(1)} %get-tuple-element.123), channel_id=1, source_target_pairs={{0,2},{1,3},{2,0},{3,1},{4,6},{5,7},{6,4},{7,5},{8,10},{9,11},{10,... | collective-permute-start | bytes 1572872 | tf_op jit(solution)/shard_map/ppermute | solution.py:84
  40.1 31.0 %collective-permute-start.26 = (bf16[128,2048]{1,0:T(8,128)(2,1)S(1)}, bf16[128,2048]{1,0:T(8,128)(2,1)S(1)}, u32[]{:S(2)}, u32[]{:S(2)}) collective-permute-start(bf16[128,2048]{1,0:T(8,128)(2,1)S(1)} %get-tuple-element.124), channel_id=1, source_target_pairs={{0,3},{1,2},{2,1},{3,0},{4,7},{5,6},{6,5},{7,4},{8,11},{9,10},{10,... | collective-permute-start | bytes 1572872 | tf_op jit(solution)/shard_map/ppermute | solution.py:84
  47.2 23.9 %collective-permute-start.10 = (bf16[128,384]{1,0:T(8,128)(2,1)S(1)}, bf16[128,384]{1,0:T(8,128)(2,1)S(1)}, u32[]{:S(2)}, u32[]{:S(2)}) collective-permute-start(bf16[128,384]{1,0:T(8,128)(2,1)S(1)} %get-tuple-element.111), channel_id=1, source_target_pairs={{0,8},{4,12},{8,0},{12,4},{16,24},{20,28},{24,16},{28,20},{1,9},{5... | collective-permute-start | bytes 294920 | tf_op jit(solution)/shard_map/ppermute | solution.py:87
  48.8 22.9 %collective-permute-start.11 = (bf16[128,384]{1,0:T(8,128)(2,1)S(1)}, bf16[128,384]{1,0:T(8,128)(2,1)S(1)}, u32[]{:S(2)}, u32[]{:S(2)}) collective-permute-start(bf16[128,384]{1,0:T(8,128)(2,1)S(1)} %get-tuple-element.112), channel_id=1, source_target_pairs={{0,12},{4,8},{8,4},{12,0},{16,28},{20,24},{24,20},{28,16},{1,13},{... | collective-permute-start | bytes 294920 | tf_op jit(solution)/shard_map/ppermute | solution.py:87
  53.7 20.2 %collective-permute-start.12 = (bf16[128,384]{1,0:T(8,128)(2,1)S(1)}, bf16[128,384]{1,0:T(8,128)(2,1)S(1)}, u32[]{:S(2)}, u32[]{:S(2)}) collective-permute-start(bf16[128,384]{1,0:T(8,128)(2,1)S(1)} %get-tuple-element.113), channel_id=1, source_target_pairs={{0,16},{4,20},{8,24},{12,28},{16,0},{20,4},{24,8},{28,12},{1,17},{... | collective-permute-start | bytes 294920 | tf_op jit(solution)/shard_map/ppermute | solution.py:87
  60.1 55.6 %collective-permute-start.27 = (bf16[128,2048]{1,0:T(8,128)(2,1)S(1)}, bf16[128,2048]{1,0:T(8,128)(2,1)S(1)}, u32[]{:S(2)}, u32[]{:S(2)}) collective-permute-start(bf16[128,2048]{1,0:T(8,128)(2,1)S(1)} %collective-permute-done.24.refs_11_.refs_6_), channel_id=1, source_target_pairs={{0,4},{4,0},{8,12},{12,8},{16,20},{20,16},{24,28},{28,24},{1,5},{5... | collective-permute-start | bytes 1572872 | tf_op jit(solution)/shard_map/ppermute | solution.py:87
  71.1 44.6 %collective-permute-start.28 = (bf16[128,2048]{1,0:T(8,128)(2,1)S(1)}, bf16[128,2048]{1,0:T(8,128)(2,1)S(1)}, u32[]{:S(2)}, u32[]{:S(2)}) collective-permute-start(bf16[128,2048]{1,0:T(8,128)(2,1)S(1)} %collective-permute-done.25.refs_12_.refs_7_), channel_id=1, source_target_pairs={{0,4},{4,0},{8,12},{12,8},{16,20},{20,16},{24,28},{28,24},{1,5},{5... | collective-permute-start | bytes 1572872 | tf_op jit(solution)/shard_map/ppermute | solution.py:87
  71.1 44.6 %collective-permute-start.29 = (bf16[128,2048]{1,0:T(8,128)(2,1)S(1)}, bf16[128,2048]{1,0:T(8,128)(2,1)S(1)}, u32[]{:S(2)}, u32[]{:S(2)}) collective-permute-start(bf16[128,2048]{1,0:T(8,128)(2,1)S(1)} %collective-permute-done.26.refs_13_.refs_8_), channel_id=1, source_target_pairs={{0,4},{4,0},{8,12},{12,8},{16,20},{20,16},{24,28},{28,24},{1,5},{5... | collective-permute-start | bytes 1572872 | tf_op jit(solution)/shard_map/ppermute | solution.py:87
  73.9 11.1 %collective-permute-start.14 = (bf16[128,384]{1,0:T(8,128)(2,1)S(1)}, bf16[128,384]{1,0:T(8,128)(2,1)S(1)}, u32[]{:S(2)}, u32[]{:S(2)}) collective-permute-start(bf16[128,384]{1,0:T(8,128)(2,1)S(1)} %get-tuple-element.115), channel_id=1, source_target_pairs={{0,24},{4,28},{8,16},{12,20},{16,8},{20,12},{24,0},{28,4},{1,25},{... | collective-permute-start | bytes 294920 | tf_op jit(solution)/shard_map/ppermute | solution.py:87
  118.3 11.4 %collective-permute-start.30 = (bf16[128,1024]{1,0:T(8,128)(2,1)S(1)}, bf16[128,1024]{1,0:T(8,128)(2,1)S(1)}, u32[]{:S(2)}, u32[]{:S(2)}) collective-permute-start(bf16[128,1024]{1,0:T(8,128)(2,1)S(1)} %get-tuple-element.125.refs_0_), channel_id=1, source_target_pairs={{0,1},{1,0},{2,3},{3,2},{4,5},{5,4},{6,7},{7,6},{8,9},{9,8},{10,11... | collective-permute-start | bytes 786440 | tf_op jit(solution)/shard_map/ppermute | solution.py:84
  122.6 13.7 %collective-permute-start.31 = (bf16[128,1024]{1,0:T(8,128)(2,1)S(1)}, bf16[128,1024]{1,0:T(8,128)(2,1)S(1)}, u32[]{:S(2)}, u32[]{:S(2)}) collective-permute-start(bf16[128,1024]{1,0:T(8,128)(2,1)S(1)} %get-tuple-element.125.refs_0_), channel_id=1, source_target_pairs={{0,2},{1,3},{2,0},{3,1},{4,6},{5,7},{6,4},{7,5},{8,10},{9,11},{10,... | collective-permute-start | bytes 786440 | tf_op jit(solution)/shard_map/ppermute | solution.py:84
  122.6 13.7 %collective-permute-start.32 = (bf16[128,1024]{1,0:T(8,128)(2,1)S(1)}, bf16[128,1024]{1,0:T(8,128)(2,1)S(1)}, u32[]{:S(2)}, u32[]{:S(2)}) collective-permute-start(bf16[128,1024]{1,0:T(8,128)(2,1)S(1)} %get-tuple-element.125.refs_0_), channel_id=1, source_target_pairs={{0,3},{1,2},{2,1},{3,0},{4,7},{5,6},{6,5},{7,4},{8,11},{9,10},{10,... | collective-permute-start | bytes 786440 | tf_op jit(solution)/shard_map/ppermute | solution.py:84
  157.4 149.2 %reduce-scatter.3.cloned.1.call-start = ((), (), s32[]{:S(2)}) async-start(), calls=%async_computation.3 | async-start | bytes 2359296 | tf_op jit(solution)/shard_map/reduce_scatter | solution.py:335
  161.9 12.9 %collective-permute-start.37 = (bf16[128,1024]{1,0:T(8,128)(2,1)}, bf16[128,1024]{1,0:T(8,128)(2,1)S(1)}, u32[]{:S(2)}, u32[]{:S(2)}) collective-permute-start(bf16[128,1024]{1,0:T(8,128)(2,1)} %get-tuple-element.138), channel_id=1, source_target_pairs={{0,2},{1,3},{2,0},{3,1},{4,6},{5,7},{6,4},{7,5},{8,10},{9,11},{10,... | collective-permute-start | bytes 786440 | tf_op jit(solution)/shard_map/ppermute | solution.py:84
  162.7 12.1 %collective-permute-start.38 = (bf16[128,1024]{1,0:T(8,128)(2,1)}, bf16[128,1024]{1,0:T(8,128)(2,1)S(1)}, u32[]{:S(2)}, u32[]{:S(2)}) collective-permute-start(bf16[128,1024]{1,0:T(8,128)(2,1)} %get-tuple-element.139), channel_id=1, source_target_pairs={{0,3},{1,2},{2,1},{3,0},{4,7},{5,6},{6,5},{7,4},{8,11},{9,10},{10,... | collective-permute-start | bytes 786440 | tf_op jit(solution)/shard_map/ppermute | solution.py:84
  179.5 21.9 %collective-permute-start.41 = (bf16[128,256]{1,0:T(8,128)(2,1)S(1)}, bf16[128,256]{1,0:T(8,128)(2,1)S(1)}, u32[]{:S(2)}, u32[]{:S(2)}) collective-permute-start(bf16[128,256]{1,0:T(8,128)(2,1)S(1)} %get-tuple-element.145), channel_id=1, source_target_pairs={{0,1},{1,9},{2,17},{3,25},{4,5},{5,13},{6,21},{7,29},{8,0},{9,8},{... | collective-permute-start | bytes 196616 | tf_op jit(solution)/shard_map/ppermute | solution.py:95
  182.6 18.7 %collective-permute-start.42 = (bf16[128,256]{1,0:T(8,128)(2,1)S(1)}, bf16[128,256]{1,0:T(8,128)(2,1)S(1)}, u32[]{:S(2)}, u32[]{:S(2)}) collective-permute-start(bf16[128,256]{1,0:T(8,128)(2,1)S(1)} %get-tuple-element.146), channel_id=1, source_target_pairs={{0,2},{1,10},{2,18},{3,26},{4,6},{5,14},{6,22},{7,30},{8,3},{9,11}... | collective-permute-start | bytes 196616 | tf_op jit(solution)/shard_map/ppermute | solution.py:95
  185.8 16.1 %collective-permute-start.43 = (bf16[128,256]{1,0:T(8,128)(2,1)S(1)}, bf16[128,256]{1,0:T(8,128)(2,1)S(1)}, u32[]{:S(2)}, u32[]{:S(2)}) collective-permute-start(bf16[128,256]{1,0:T(8,128)(2,1)S(1)} %get-tuple-element.147), channel_id=1, source_target_pairs={{0,3},{1,11},{2,19},{3,27},{4,7},{5,15},{6,23},{7,31},{8,2},{9,10}... | collective-permute-start | bytes 196616 | tf_op jit(solution)/shard_map/ppermute | solution.py:95
  185.8 18.1 %collective-permute-start.44 = (bf16[128,256]{1,0:T(8,128)(2,1)S(1)}, bf16[128,256]{1,0:T(8,128)(2,1)S(1)}, u32[]{:S(2)}, u32[]{:S(2)}) collective-permute-start(bf16[128,256]{1,0:T(8,128)(2,1)S(1)} %collective-permute-done.40.refs_3_), channel_id=1, source_target_pairs={{0,4},{4,0},{8,12},{12,8},{16,20},{20,16},{24,28},{28,24},{1,5},{5... | collective-permute-start | bytes 196616 | tf_op jit(solution)/shard_map/ppermute | solution.py:87
  203.4 51.2 %collective-permute-start.62 = (bf16[4,128,1024]{2,1,0:T(8,128)(2,1)S(1)}, bf16[4,128,1024]{2,1,0:T(8,128)(2,1)S(1)}, u32[]{:S(2)}, u32[]{:S(2)}) collective-permute-start(bf16[4,128,1024]{2,1,0:T(8,128)(2,1)S(1)} %get-tuple-element.176), channel_id=1, source_target_pairs={{0,4},{4,0},{8,12},{12,8},{16,20},{20,16},{24,28},{28,24},{1,5},{5... | collective-permute-start | bytes 3145736 | tf_op jit(solution)/shard_map/ppermute | solution.py:87
  214.9 10.1 %collective-permute-start.49 = (bf16[128,384]{1,0:T(8,128)(2,1)S(1)}, bf16[128,384]{1,0:T(8,128)(2,1)S(1)}, u32[]{:S(2)}, u32[]{:S(2)}) collective-permute-start(bf16[128,384]{1,0:T(8,128)(2,1)S(1)} %get-tuple-element.150), channel_id=1, source_target_pairs={{0,8},{4,12},{8,0},{12,4},{16,24},{20,28},{24,16},{28,20},{1,9},{5... | collective-permute-start | bytes 294920 | tf_op jit(solution)/shard_map/ppermute | solution.py:87
  216.2 15.0 %collective-permute-start.50 = (bf16[128,384]{1,0:T(8,128)(2,1)S(1)}, bf16[128,384]{1,0:T(8,128)(2,1)S(1)}, u32[]{:S(2)}, u32[]{:S(2)}) collective-permute-start(bf16[128,384]{1,0:T(8,128)(2,1)S(1)} %get-tuple-element.151), channel_id=1, source_target_pairs={{0,12},{4,8},{8,4},{12,0},{16,28},{20,24},{24,20},{28,16},{1,13},{... | collective-permute-start | bytes 294920 | tf_op jit(solution)/shard_map/ppermute | solution.py:87
  216.7 18.3 %collective-permute-start.51 = (bf16[128,384]{1,0:T(8,128)(2,1)S(1)}, bf16[128,384]{1,0:T(8,128)(2,1)S(1)}, u32[]{:S(2)}, u32[]{:S(2)}) collective-permute-start(bf16[128,384]{1,0:T(8,128)(2,1)S(1)} %get-tuple-element.152), channel_id=1, source_target_pairs={{0,16},{4,20},{8,24},{12,28},{16,0},{20,4},{24,8},{28,12},{1,17},{... | collective-permute-start | bytes 294920 | tf_op jit(solution)/shard_map/ppermute | solution.py:87
  219.9 15.1 %collective-permute-start.52 = (bf16[128,384]{1,0:T(8,128)(2,1)S(1)}, bf16[128,384]{1,0:T(8,128)(2,1)S(1)}, u32[]{:S(2)}, u32[]{:S(2)}) collective-permute-start(bf16[128,384]{1,0:T(8,128)(2,1)S(1)} %get-tuple-element.153), channel_id=1, source_target_pairs={{0,20},{4,16},{8,28},{12,24},{16,4},{20,0},{24,12},{28,8},{1,21},{... | collective-permute-start | bytes 294920 | tf_op jit(solution)/shard_map/ppermute | solution.py:87
  225.0 16.2 %collective-permute-start.53 = (bf16[128,384]{1,0:T(8,128)(2,1)S(1)}, bf16[128,384]{1,0:T(8,128)(2,1)S(1)}, u32[]{:S(2)}, u32[]{:S(2)}) collective-permute-start(bf16[128,384]{1,0:T(8,128)(2,1)S(1)} %get-tuple-element.154), channel_id=1, source_target_pairs={{0,24},{4,28},{8,16},{12,20},{16,8},{20,12},{24,0},{28,4},{1,25},{... | collective-permute-start | bytes 294920 | tf_op jit(solution)/shard_map/ppermute | solution.py:87
  231.3 13.1 %collective-permute-start.54 = (bf16[128,384]{1,0:T(8,128)(2,1)S(1)}, bf16[128,384]{1,0:T(8,128)(2,1)S(1)}, u32[]{:S(2)}, u32[]{:S(2)}) collective-permute-start(bf16[128,384]{1,0:T(8,128)(2,1)S(1)} %get-tuple-element.155), channel_id=1, source_target_pairs={{0,28},{4,24},{8,20},{12,16},{16,12},{20,8},{24,4},{28,0},{1,29},{... | collective-permute-start | bytes 294920 | tf_op jit(solution)/shard_map/ppermute | solution.py:87
  255.4 10.8 %collective-permute-start.63 = (bf16[128,1024]{1,0:T(8,128)(2,1)S(1)}, bf16[128,1024]{1,0:T(8,128)(2,1)S(1)}, u32[]{:S(2)}, u32[]{:S(2)}) collective-permute-start(bf16[128,1024]{1,0:T(8,128)(2,1)S(1)} %get-tuple-element.178), channel_id=1, source_target_pairs={{0,1},{1,0},{2,3},{3,2},{4,5},{5,4},{6,7},{7,6},{8,9},{9,8},{10,11... | collective-permute-start | bytes 786440 | tf_op jit(solution)/shard_map/ppermute | solution.py:84
  255.8 14.3 %collective-permute-start.64 = (bf16[128,1024]{1,0:T(8,128)(2,1)S(1)}, bf16[128,1024]{1,0:T(8,128)(2,1)S(1)}, u32[]{:S(2)}, u32[]{:S(2)}) collective-permute-start(bf16[128,1024]{1,0:T(8,128)(2,1)S(1)} %get-tuple-element.179), channel_id=1, source_target_pairs={{0,2},{1,3},{2,0},{3,1},{4,6},{5,7},{6,4},{7,5},{8,10},{9,11},{10,... | collective-permute-start | bytes 786440 | tf_op jit(solution)/shard_map/ppermute | solution.py:84
  255.8 16.3 %collective-permute-start.65 = (bf16[128,1024]{1,0:T(8,128)(2,1)S(1)}, bf16[128,1024]{1,0:T(8,128)(2,1)S(1)}, u32[]{:S(2)}, u32[]{:S(2)}) collective-permute-start(bf16[128,1024]{1,0:T(8,128)(2,1)S(1)} %get-tuple-element.180), channel_id=1, source_target_pairs={{0,3},{1,2},{2,1},{3,0},{4,7},{5,6},{6,5},{7,4},{8,11},{9,10},{10,... | collective-permute-start | bytes 786440 | tf_op jit(solution)/shard_map/ppermute | solution.py:84
  259.7 17.8 %collective-permute-start.59 = (bf16[144,768]{1,0:T(8,128)(2,1)S(1)}, bf16[144,768]{1,0:T(8,128)(2,1)S(1)}, u32[]{:S(2)}, u32[]{:S(2)}) collective-permute-start(bf16[144,768]{1,0:T(8,128)(2,1)S(1)} %get-tuple-element.171), channel_id=1, source_target_pairs={{0,8},{4,12},{8,0},{12,4},{16,24},{20,28},{24,16},{28,20},{1,9},{5... | collective-permute-start | bytes 663560 | tf_op jit(solution)/shard_map/ppermute | solution.py:87
  264.6 18.7 %collective-permute-start.60 = (bf16[144,768]{1,0:T(8,128)(2,1)S(1)}, bf16[144,768]{1,0:T(8,128)(2,1)S(1)}, u32[]{:S(2)}, u32[]{:S(2)}) collective-permute-start(bf16[144,768]{1,0:T(8,128)(2,1)S(1)} %get-tuple-element.172), channel_id=1, source_target_pairs={{0,16},{4,20},{8,24},{12,28},{16,0},{20,4},{24,8},{28,12},{1,17},{... | collective-permute-start | bytes 663560 | tf_op jit(solution)/shard_map/ppermute | solution.py:87
  266.2 19.8 %collective-permute-start.61 = (bf16[144,768]{1,0:T(8,128)(2,1)S(1)}, bf16[144,768]{1,0:T(8,128)(2,1)S(1)}, u32[]{:S(2)}, u32[]{:S(2)}) collective-permute-start(bf16[144,768]{1,0:T(8,128)(2,1)S(1)} %get-tuple-element.173), channel_id=1, source_target_pairs={{0,24},{4,28},{8,16},{12,20},{16,8},{20,12},{24,0},{28,4},{1,25},{... | collective-permute-start | bytes 663560 | tf_op jit(solution)/shard_map/ppermute | solution.py:87
  270.1 29.5 %collective-permute-start.33 = (bf16[128,1024]{1,0:T(8,128)(2,1)}, bf16[128,1024]{1,0:T(8,128)(2,1)S(1)}, u32[]{:S(2)}, u32[]{:S(2)}) collective-permute-start(bf16[128,1024]{1,0:T(8,128)(2,1)} %get-tuple-element.129), channel_id=1, source_target_pairs={{0,1},{1,0},{2,3},{3,2},{4,5},{5,4},{6,7},{7,6},{8,9},{9,8},{10,11... | collective-permute-start | bytes 786440 | tf_op jit(solution)/shard_map/ppermute | solution.py:84
  273.5 15.0 %collective-permute-start.66 = (bf16[32,1024]{1,0:T(8,128)(2,1)S(1)}, bf16[32,1024]{1,0:T(8,128)(2,1)S(1)}, u32[]{:S(2)}, u32[]{:S(2)}) collective-permute-start(bf16[32,1024]{1,0:T(8,128)(2,1)S(1)} %get-tuple-element.182), channel_id=1, source_target_pairs={{0,8},{4,12},{8,0},{12,4},{16,24},{20,28},{24,16},{28,20},{1,9},{5... | collective-permute-start | bytes 196616 | tf_op jit(solution)/shard_map/ppermute | solution.py:87
  277.5 23.6 %collective-permute-start.34 = (bf16[128,1024]{1,0:T(8,128)(2,1)}, bf16[128,1024]{1,0:T(8,128)(2,1)}, u32[]{:S(2)}, u32[]{:S(2)}) collective-permute-start(bf16[128,1024]{1,0:T(8,128)(2,1)} %get-tuple-element.130), channel_id=1, source_target_pairs={{0,2},{1,3},{2,0},{3,1},{4,6},{5,7},{6,4},{7,5},{8,10},{9,11},{10,... | collective-permute-start | bytes 786440 | tf_op jit(solution)/shard_map/ppermute | solution.py:84
  283.4 17.7 %collective-permute-start.35 = (bf16[128,1024]{1,0:T(8,128)(2,1)}, bf16[128,1024]{1,0:T(8,128)(2,1)}, u32[]{:S(2)}, u32[]{:S(2)}) collective-permute-start(bf16[128,1024]{1,0:T(8,128)(2,1)} %get-tuple-element.131), channel_id=1, source_target_pairs={{0,3},{1,2},{2,1},{3,0},{4,7},{5,6},{6,5},{7,4},{8,11},{9,10},{10,... | collective-permute-start | bytes 786440 | tf_op jit(solution)/shard_map/ppermute | solution.py:84
  303.1 14.1 %collective-permute-start.55 = (bf16[128,1024]{1,0:T(8,128)(2,1)}, bf16[128,1024]{1,0:T(8,128)(2,1)S(1)}, u32[]{:S(2)}, u32[]{:S(2)}) collective-permute-start(bf16[128,1024]{1,0:T(8,128)(2,1)} %get-tuple-element.159), channel_id=1, source_target_pairs={{0,1},{1,0},{2,3},{3,2},{4,5},{5,4},{6,7},{7,6},{8,9},{9,8},{10,11... | collective-permute-start | bytes 786440 | tf_op jit(solution)/shard_map/ppermute | solution.py:84
  305.1 14.4 %collective-permute-start.56 = (bf16[128,1024]{1,0:T(8,128)(2,1)}, bf16[128,1024]{1,0:T(8,128)(2,1)S(1)}, u32[]{:S(2)}, u32[]{:S(2)}) collective-permute-start(bf16[128,1024]{1,0:T(8,128)(2,1)} %get-tuple-element.160), channel_id=1, source_target_pairs={{0,2},{1,3},{2,0},{3,1},{4,6},{5,7},{6,4},{7,5},{8,10},{9,11},{10,... | collective-permute-start | bytes 786440 | tf_op jit(solution)/shard_map/ppermute | solution.py:84
  305.1 22.0 %collective-permute-start.57 = (bf16[128,1024]{1,0:T(8,128)(2,1)}, bf16[128,1024]{1,0:T(8,128)(2,1)S(1)}, u32[]{:S(2)}, u32[]{:S(2)}) collective-permute-start(bf16[128,1024]{1,0:T(8,128)(2,1)} %get-tuple-element.161), channel_id=1, source_target_pairs={{0,3},{1,2},{2,1},{3,0},{4,7},{5,6},{6,5},{7,4},{8,11},{9,10},{10,... | collective-permute-start | bytes 786440 | tf_op jit(solution)/shard_map/ppermute | solution.py:84
  308.0 19.1 %collective-permute-start.39 = (bf16[128,1024]{1,0:T(8,128)(2,1)}, bf16[128,1024]{1,0:T(8,128)(2,1)S(1)}, u32[]{:S(2)}, u32[]{:S(2)}) collective-permute-start(bf16[128,1024]{1,0:T(8,128)(2,1)} %reduce-scatter.3.cloned.1.call-done), channel_id=1, source_target_pairs={{0,0},{1,8},{2,16},{3,24},{4,1},{5,9},{6,17},{7,25},{8,2},{9,10},{... | collective-permute-start | bytes 786440 | tf_op jit(solution)/shard_map/ppermute | solution.py:95
  (97 other events, 1500.5 us)
Sparse Core Ops, SparseCore 0:
  32.2 39.4 all-gather.1
  157.5 35.0 reduce-scatter.4
  194.9 52.0 reduce-scatter.2

commit v2 on v1

--- a/solution.py
+++ b/solution.py
@@ -327,7 +327,7 @@
         ]
         full_up, a2_all, gelled, slope = call(
             forward, outs, idx, a2_parts + [own_w, up_bias] + got_w + other_w,
-            flops=2 * all_rows * width * hidden, mib=54,
+            flops=2 * all_rows * width * hidden,
         )
         g_down = outer(gelled, dz_all).astype(BF)
 
@@ -603,13 +603,21 @@
         z_own, *sends = call(down, outs, idx, [gelled, w_down], flops=2 * all_rows * width * hidden)
         z_got = send_f(sends)
 
-        def add_up(i, own, mid_ref, small_ref, *refs):
+        def add_up(i, own, mid_ref, small_ref, o_ref, *refs):
+            got, got_o, (out, o_sum) = refs[: n_f - 1], refs[n_f - 1 : -2], refs[-2:]
             total = own[...]
-            for g in refs[:-1]:
+            for g in got:
                 total = total + g[...].astype(F32)
-            refs[-1][...] = total + mid_ref[...] + small_ref[7:8, :]
-
-        (result,) = call(add_up, [shaped((rows, width), F32)], idx, [z_own, mid, small] + z_got)
+            out[...] = total + mid_ref[...] + small_ref[7:8, :]
+            total = o_ref[...]
+            for g in got_o:
+                total = total + g[...].astype(F32)
+            o_sum[...] = total
+
+        result, out_out = call(
+            add_up, [shaped((rows, width), F32), shaped((per, width), F32)], idx,
+            [z_own, mid, small, out_own] + z_got + out_got,
+        )
 
         def input_grad(i, x_ref, dmid_ref, small_ref, low_ref, own, *refs):
             got, (out, wider) = refs[:-2], refs[-2:]
@@ -624,13 +632,8 @@
         d_input, out_down = call(input_grad, outs, idx, [x, d_mid, small, low_down, d_own] + got_x)
 
         def over_z(i, *refs):
-            own_ref, got, refs = refs[0], refs[1:n_z], refs[n_z:]
-            o_ref, got_o, up_ref, refs = refs[0], refs[1:n_z], refs[n_z], refs[n_z + 1 :]
-            out_ref, own, send, (held, held_up) = refs[0], refs[1], refs[2:-2], refs[-2:]
-            out = o_ref[...]
-            for g in got_o:
-                out = out + g[...].astype(F32)
-            out_ref[...] = out
+            own_ref, got, up_ref, refs = refs[0], refs[1:n_z], refs[n_z], refs[n_z + 1 :]
+            own, send, (held, held_up) = refs[0], refs[1:-2], refs[-2:]
             total = own_ref[...]
             for g in got:
                 total = total + g[...].astype(F32)
@@ -645,9 +648,9 @@
                 out[per:, : 3 * wide] = held[block:, : 3 * wide].astype(out.dtype)
 
         dims = (per + 16, 3 * wide + hidden)
-        outs = [shaped((per, width), F32), shaped(dims, F32)] + [shaped(dims, BF)] * (n_f - 1)
-        out_out, own, *sends = call(
-            over_z, outs, idx, [own] + got + [out_own] + out_got + [part_up],
+        outs = [shaped(dims, F32)] + [shaped(dims, BF)] * (n_f - 1)
+        own, *sends = call(
+            over_z, outs, idx, [own] + got + [part_up],
             [pltpu.VMEM((block + 16, 3 * wide), F32), pltpu.VMEM((block, hidden), F32)],
             mib=54,
         )

time: 336 us -> 346 us (1.030); the launches traced: 336 us -> 340 us
  local copies, waits for them, and re-layouts: 16 us -> 28 us
  starting transfers between devices: 110 us -> 103 us
    unnamed x141 -> x147, local copies, waits for them, and re-layouts: 14.7 us -> 26.7 us
    ppermute x36, waiting for transfers between devices: 36.2 us -> 45.1 us  [ctx_to(): return lax.ppermute(x, 'ctx', [(i, i ^ e) for i in range(n_ctx)])]
    ppermute x27, starting transfers between devices: 41.3 us -> 33.3 us  [fsdp_to(): return lax.ppermute(x, 'fsdp', [(f, f ^ k) for f in range(n_f)])]
    ppermute x27, waiting for transfers between devices: 68.5 us -> 61.6 us  [fsdp_to(): return lax.ppermute(x, 'fsdp', [(f, f ^ k) for f in range(n_f)])]
  transfers between devices with their start and end apart: 75 -> 75, of which waited for: 30 -> 34; matrix products, arithmetic and copies ran while one was open for 2% -> 2% of each run, Pallas kernels for 15% -> 14%
where the time goes in v2:
time: 346 us; the launch traced here: 340 us
  waiting for transfers between devices  125 us (36%)
  starting transfers between devices  103 us (30%)
  Pallas kernels  60 us (17%)
  local copies, waits for them, and re-layouts  28 us (8%)
  between operations  14.3 us (4%)
  matrix products  8.07 us (2%)
    ppermute x27, waiting for transfers between devices, fsdp_to(): return lax.ppermute(x, 'fsdp', [(f, f ^ k) for f in range(n_f)])  61.6 us
    pallas_call x20, Pallas kernels, call(): pl.pallas_call(kernel, out_shape=outs, in_specs=[pl.BlockSpec(memory_spac...  60 us
    ppermute x36, starting transfers between devices, ctx_to(): return lax.ppermute(x, 'ctx', [(i, i ^ e) for i in range(n_ctx)])  46.1 us
    ppermute x36, waiting for transfers between devices, ctx_to(): return lax.ppermute(x, 'ctx', [(i, i ^ e) for i in range(n_ctx)])  45.1 us
    ppermute x27, starting transfers between devices, fsdp_to(): return lax.ppermute(x, 'fsdp', [(f, f ^ k) for f in range(n_f)])  33.3 us
    unnamed x147, local copies, waits for them, and re-layouts  26.7 us
    ppermute x9, starting transfers between devices, both_to(): return lax.ppermute(x, ('ctx', 'fsdp'), pairs)  23.7 us
    ppermute x9, waiting for transfers between devices, both_to(): return lax.ppermute(x, ('ctx', 'fsdp'), pairs)  18 us
  transfers between devices with their start and end apart: 75, of which 34 were waited for; matrix products, arithmetic and copies ran while one was open for 2% of the time, Pallas kernels for 14%

profile of v2, /device:TPU:0, one launch (start us, length us, event | category | flops | bytes accessed | tf_op | source)
XLA Modules:
  0.0 339.7 jit_solution(8399797474495920186)
XLA Ops:
  14.1 3.0 collective-permute-start
  24.3 7.6 %collective-permute-done.1.refs_2_.refs_10_ = bf16[128,1024]{1,0:T(8,128)(2,1)S(1)} collective-permute-done((bf16[128,1024]{1,0:T(8,128)(2,1)S(1)}, bf16[128,1024]{1,0:T(8,128)(2,1)S(1)}, u32[]{:S(2)}, u32[]{:S(2)}) %collective-permute-start.1) | collective-permute-done | bytes 262176 | tf_op jit(solution)/shard_map/ppermute | solution.py:84
  35.5 2.1 collective-permute-start.24
  43.6 2.4 shard_map.170
  48.7 4.8 %collective-permute-done.24.refs_11_.refs_6_ = bf16[128,2048]{1,0:T(8,128)(2,1)S(1)} collective-permute-done((bf16[128,2048]{1,0:T(8,128)(2,1)S(1)}, bf16[128,2048]{1,0:T(8,128)(2,1)S(1)}, u32[]{:S(2)}, u32[]{:S(2)}) %collective-permute-start.24) | collective-permute-done | bytes 524320 | tf_op jit(solution)/shard_map/ppermute | solution.py:84
  53.5 2.8 collective-permute-start.12
  56.3 4.0 %collective-permute-done.25.refs_12_.refs_7_ = bf16[128,2048]{1,0:T(8,128)(2,1)S(1)} collective-permute-done((bf16[128,2048]{1,0:T(8,128)(2,1)S(1)}, bf16[128,2048]{1,0:T(8,128)(2,1)S(1)}, u32[]{:S(2)}, u32[]{:S(2)}) %collective-permute-start.25) | collective-permute-done | bytes 524320 | tf_op jit(solution)/shard_map/ppermute | solution.py:84
  60.3 10.7 %collective-permute-done.26.refs_13_.refs_8_ = bf16[128,2048]{1,0:T(8,128)(2,1)S(1)} collective-permute-done((bf16[128,2048]{1,0:T(8,128)(2,1)S(1)}, bf16[128,2048]{1,0:T(8,128)(2,1)S(1)}, u32[]{:S(2)}, u32[]{:S(2)}) %collective-permute-start.26) | collective-permute-done | bytes 524320 | tf_op jit(solution)/shard_map/ppermute | solution.py:84
  71.6 2.3 collective-permute-start.13
  75.3 6.3 %collective-permute-done.13.refs_5_ = bf16[128,384]{1,0:T(8,128)(2,1)S(1)} collective-permute-done((bf16[128,384]{1,0:T(8,128)(2,1)S(1)}, bf16[128,384]{1,0:T(8,128)(2,1)S(1)}, u32[]{:S(2)}, u32[]{:S(2)}) %collective-permute-start.13) | collective-permute-done | bytes 98336 | tf_op jit(solution)/shard_map/ppermute | solution.py:87
  81.6 3.4 %collective-permute-start.15 = (bf16[128,384]{1,0:T(8,128)(2,1)S(1)}, bf16[128,384]{1,0:T(8,128)(2,1)S(1)}, u32[]{:S(2)}, u32[]{:S(2)}) collective-permute-start(bf16[128,384]{1,0:T(8,128)(2,1)S(1)} %get-tuple-element.117), channel_id=1, source_target_pairs={{0,28},{4,24},{8,20},{12,16},{16,12},{20,8},{24,4},{28,0},{1,29},{... | collective-permute-start | bytes 294920 | tf_op jit(solution)/shard_map/ppermute | solution.py:87
  85.4 2.7 collective-permute-done.15.refs_7_
  88.1 6.4 %shard_map.171 = (bf16[1024,384]{1,0:T(8,128)(2,1)S(1)}, bf16[1024,128]{1,0:T(8,128)(2,1)S(1)}, f32[1024,128]{1,0:T(8,128)S(1)}, bf16[256,128]{1,0:T(8,128)(2,1)...) custom-call(s32[24]{0:T(128)S(1)} %concatenate.6.i, ...), custom_call_target="tpu_custom_call" | custom-call | flops 536870912 | bytes 2621440 | tf_op jit(solution)/shard_map/pallas_call | solution.py:66
  96.9 4.2 %collective-permute-start.17 = (bf16[256,128]{1,0:T(8,128)(2,1)S(1)}, bf16[256,128]{1,0:T(8,128)(2,1)S(1)}, u32[]{:S(2)}, u32[]{:S(2)}) collective-permute-start(bf16[256,128]{1,0:T(8,128)(2,1)S(1)} %get-tuple-element.119), channel_id=1, source_target_pairs={{0,8},{1,0},{2,24},{3,16},{4,12},{5,4},{6,28},{7,20},{8,9},{9,1},{... | collective-permute-start | bytes 196616 | tf_op jit(solution)/shard_map/ppermute | solution.py:95
  101.1 3.7 %collective-permute-start.18 = (bf16[256,128]{1,0:T(8,128)(2,1)S(1)}, bf16[256,128]{1,0:T(8,128)(2,1)S(1)}, u32[]{:S(2)}, u32[]{:S(2)}) collective-permute-start(bf16[256,128]{1,0:T(8,128)(2,1)S(1)} %get-tuple-element.120), channel_id=1, source_target_pairs={{0,16},{1,24},{2,0},{3,8},{4,20},{5,28},{6,4},{7,12},{8,17},{9,25}... | collective-permute-start | bytes 196616 | tf_op jit(solution)/shard_map/ppermute | solution.py:95
  104.8 6.2 %collective-permute-start.19 = (bf16[256,128]{1,0:T(8,128)(2,1)S(1)}, bf16[256,128]{1,0:T(8,128)(2,1)S(1)}, u32[]{:S(2)}, u32[]{:S(2)}) collective-permute-start(bf16[256,128]{1,0:T(8,128)(2,1)S(1)} %get-tuple-element.121), channel_id=1, source_target_pairs={{0,24},{1,16},{2,8},{3,0},{4,28},{5,20},{6,12},{7,4},{8,25},{9,17}... | collective-permute-start | bytes 196616 | tf_op jit(solution)/shard_map/ppermute | solution.py:95
  111.0 3.0 collective-permute-done.19.refs_5_.refs_3_
  118.3 4.3 %collective-permute-start.30 = (bf16[128,1024]{1,0:T(8,128)(2,1)S(1)}, bf16[128,1024]{1,0:T(8,128)(2,1)S(1)}, u32[]{:S(2)}, u32[]{:S(2)}) collective-permute-start(bf16[128,1024]{1,0:T(8,128)(2,1)S(1)} %get-tuple-element.126.refs_0_), channel_id=1, source_target_pairs={{0,1},{1,0},{2,3},{3,2},{4,5},{5,4},{6,7},{7,6},{8,9},{9,8},{10,11... | collective-permute-start | bytes 786440 | tf_op jit(solution)/shard_map/ppermute | solution.py:84
  124.1 5.6 %collective-permute-done.30.refs_1_ = bf16[128,1024]{1,0:T(8,128)(2,1)S(1)} collective-permute-done((bf16[128,1024]{1,0:T(8,128)(2,1)S(1)}, bf16[128,1024]{1,0:T(8,128)(2,1)S(1)}, u32[]{:S(2)}, u32[]{:S(2)}) %collective-permute-start.30) | collective-permute-done | bytes 262176 | tf_op jit(solution)/shard_map/ppermute | solution.py:84
  129.7 6.5 %collective-permute-done.31.refs_2_ = bf16[128,1024]{1,0:T(8,128)(2,1)S(1)} collective-permute-done((bf16[128,1024]{1,0:T(8,128)(2,1)S(1)}, bf16[128,1024]{1,0:T(8,128)(2,1)S(1)}, u32[]{:S(2)}, u32[]{:S(2)}) %collective-permute-start.31) | collective-permute-done | bytes 262176 | tf_op jit(solution)/shard_map/ppermute | solution.py:84
  136.3 3.3 shard_map.174
  143.8 9.3 %shard_map.176 = (bf16[512,1024]{1,0:T(8,128)(2,1)}, f32[1,1024]{1,0:T(1,128)}, f32[128,1024]{1,0:T(8,128)}, bf16[128,1024]{1,0:T(8,128)(2,1)}, bf16[128,1024]{1,0:T(8,128)(2,1)}, /*index=5*/bf16[128,1024]{1,0:T(8,128)(2,1)}) custom-call(s32[24]{0:T(128)} %copy-done.27, bf16[512,1024]{1,0:T(8,128)(2,1)} %all-gather.2.cloned.1.call-done.dz_ref, ...), custom_call_target="tpu_custom_call" | custom-call | flops 2147483648 | bytes 8654848 | tf_op jit(solution)/shard_map/pallas_call | solution.py:66
  153.1 3.9 %convolution_convert_fusion = bf16[1024,1024]{1,0:T(8,128)(2,1)} fusion(bf16[512,1024]{1,0:T(8,128)(2,1)S(1)} %copy-done.45, bf16[512,1024]{1,0:T(8,128)(2,1)} %get-tuple-element.188), kind=kOutput, calls=%fused_computation | convolution fusion | flops 1074790400 | bytes 4194304 | tf_op jit(solution)/shard_map/dot_general | solution.py:49
  157.1 4.2 %convolution_convert_fusion.1 = bf16[1024,1024]{1,0:T(8,128)(2,1)} fusion(bf16[512,1024]{1,0:T(8,128)(2,1)} %copy-done.42, bf16[512,1024]{1,0:T(8,128)(2,1)} %all-gather.2.cloned.1.call-done.dz_ref), kind=kOutput, calls=%fused_computation.1 | convolution fusion | flops 1074790400 | bytes 4194304 | tf_op jit(solution)/shard_map/dot_general | solution.py:49
  164.9 5.9 %collective-permute-done.33.refs_5_ = bf16[128,1024]{1,0:T(8,128)(2,1)S(1)} collective-permute-done((bf16[128,1024]{1,0:T(8,128)(2,1)}, bf16[128,1024]{1,0:T(8,128)(2,1)S(1)}, u32[]{:S(2)}, u32[]{:S(2)}) %collective-permute-start.33) | collective-permute-done | bytes 262176 | tf_op jit(solution)/shard_map/ppermute | solution.py:84
  170.8 3.7 %collective-permute-done.35.refs_7_ = bf16[128,1024]{1,0:T(8,128)(2,1)S(1)} collective-permute-done((bf16[128,1024]{1,0:T(8,128)(2,1)}, bf16[128,1024]{1,0:T(8,128)(2,1)S(1)}, u32[]{:S(2)}, u32[]{:S(2)}) %collective-permute-start.35) | collective-permute-done | bytes 262176 | tf_op jit(solution)/shard_map/ppermute | solution.py:84
  179.8 3.1 collective-permute-start.48
  182.9 3.5 %collective-permute-start.49 = (bf16[128,256]{1,0:T(8,128)(2,1)S(1)}, bf16[128,256]{1,0:T(8,128)(2,1)S(1)}, u32[]{:S(2)}, u32[]{:S(2)}) collective-permute-start(bf16[128,256]{1,0:T(8,128)(2,1)S(1)} %get-tuple-element.159), channel_id=1, source_target_pairs={{0,2},{1,10},{2,18},{3,26},{4,6},{5,14},{6,22},{7,30},{8,3},{9,11}... | collective-permute-start | bytes 196616 | tf_op jit(solution)/shard_map/ppermute | solution.py:95
  186.4 14.9 %collective-permute-done.48.refs_4_ = bf16[128,256]{1,0:T(8,128)(2,1)S(1)} collective-permute-done((bf16[128,256]{1,0:T(8,128)(2,1)S(1)}, bf16[128,256]{1,0:T(8,128)(2,1)S(1)}, u32[]{:S(2)}, u32[]{:S(2)}) %collective-permute-start.48) | collective-permute-done | bytes 65568 | tf_op jit(solution)/shard_map/ppermute | solution.py:95
  203.2 10.2 %shard_map.182 = (f32[8,128]{1,0:T(8,128)S(1)}, bf16[128,384]{1,0:T(8,128)(2,1)S(1)}, bf16[128,384]{1,0:T(8,128)(2,1)S(1)}, bf16[128,384]{1,0:T(8,128)(2,1)S(1)}...) custom-call(s32[24]{0:T(128)S(1)} %copy-done.28, ...), custom_call_target="tpu_custom_call" | custom-call | flops 1342177280 | bytes 2887680 | tf_op jit(solution)/shard_map/pallas_call | solution.py:66
  215.9 3.5 %collective-permute-start.58 = (bf16[128,384]{1,0:T(8,128)(2,1)S(1)}, bf16[128,384]{1,0:T(8,128)(2,1)S(1)}, u32[]{:S(2)}, u32[]{:S(2)}) collective-permute-start(bf16[128,384]{1,0:T(8,128)(2,1)S(1)} %get-tuple-element.165), channel_id=1, source_target_pairs={{0,16},{4,20},{8,24},{12,28},{16,0},{20,4},{24,8},{28,12},{1,17},{... | collective-permute-start | bytes 294920 | tf_op jit(solution)/shard_map/ppermute | solution.py:87
  219.4 3.8 %collective-permute-start.60 = (bf16[128,384]{1,0:T(8,128)(2,1)S(1)}, bf16[128,384]{1,0:T(8,128)(2,1)S(1)}, u32[]{:S(2)}, u32[]{:S(2)}) collective-permute-start(bf16[128,384]{1,0:T(8,128)(2,1)S(1)} %get-tuple-element.167), channel_id=1, source_target_pairs={{0,24},{4,28},{8,16},{12,20},{16,8},{20,12},{24,0},{28,4},{1,25},{... | collective-permute-start | bytes 294920 | tf_op jit(solution)/shard_map/ppermute | solution.py:87
  224.7 2.6 collective-permute-start.61
  227.4 3.1 collective-permute-done.57.refs_3_
  232.2 8.3 %collective-permute-done.60.refs_6_ = bf16[128,384]{1,0:T(8,128)(2,1)S(1)} collective-permute-done((bf16[128,384]{1,0:T(8,128)(2,1)S(1)}, bf16[128,384]{1,0:T(8,128)(2,1)S(1)}, u32[]{:S(2)}, u32[]{:S(2)}) %collective-permute-start.60) | collective-permute-done | bytes 98336 | tf_op jit(solution)/shard_map/ppermute | solution.py:87
  240.5 3.0 collective-permute-done.61.refs_7_
  244.2 5.3 %shard_map.183 = (bf16[512,768]{1,0:T(8,128)(2,1)}, f32[8,1024]{1,0:T(8,128)}, f32[128,1024]{1,0:T(8,128)}, bf16[128,1024]{1,0:T(8,128)(2,1)}, bf16[128,1024]{1,0:T(8,128)(2,1)}, /*index=5*/bf16[128,1024]{1,0:T(8,128)(2,1)}) custom-call(s32[24]{0:T(128)} %copy-done.27, bf16[128,384]{1,0:T(8,128)(2,1)} %copy-done.31, bf16[128,384]{1,0:T(8,128)(2,1)} %copy-done.66, ...), custom_call_target="tpu_custom_call" | custom-call | flops 805306368 | bytes 5570560 | tf_op jit(solution)/shard_map/pallas_call | solution.py:66
  255.7 2.6 shard_map.175
  259.8 7.2 %collective-permute-start.66 = (bf16[144,768]{1,0:T(8,128)(2,1)S(1)}, bf16[144,768]{1,0:T(8,128)(2,1)S(1)}, u32[]{:S(2)}, u32[]{:S(2)}) collective-permute-start(bf16[144,768]{1,0:T(8,128)(2,1)S(1)} %get-tuple-element.184), channel_id=1, source_target_pairs={{0,8},{4,12},{8,0},{12,4},{16,24},{20,28},{24,16},{28,20},{1,9},{5... | collective-permute-start | bytes 663560 | tf_op jit(solution)/shard_map/ppermute | solution.py:87
  273.5 3.3 collective-permute-done.66.refs_1_
  277.5 8.1 %collective-permute-done.67.refs_2_ = bf16[144,768]{1,0:T(8,128)(2,1)S(1)} collective-permute-done((bf16[144,768]{1,0:T(8,128)(2,1)S(1)}, bf16[144,768]{1,0:T(8,128)(2,1)S(1)}, u32[]{:S(2)}, u32[]{:S(2)}) %collective-permute-start.67) | collective-permute-done | bytes 221216 | tf_op jit(solution)/shard_map/ppermute | solution.py:87
  288.4 2.5 shard_map.187
  300.2 2.7 collective-permute-done.41.refs_1_
  304.2 2.8 collective-permute-start.44
  307.3 4.8 %collective-permute-start.45 = (bf16[32,1024]{1,0:T(8,128)(2,1)S(1)}, bf16[32,1024]{1,0:T(8,128)(2,1)S(1)}, u32[]{:S(2)}, u32[]{:S(2)}) collective-permute-start(bf16[32,1024]{1,0:T(8,128)(2,1)S(1)} %get-tuple-element.151), channel_id=1, source_target_pairs={{0,24},{4,28},{8,16},{12,20},{16,8},{20,12},{24,0},{28,4},{1,25},{... | collective-permute-start | bytes 196616 | tf_op jit(solution)/shard_map/ppermute | solution.py:87
  312.1 2.2 collective-permute-done.45.refs_5_
  321.8 2.1 shard_map.188
  325.7 5.5 %collective-permute-done.64.refs_2_ = bf16[128,1024]{1,0:T(8,128)(2,1)S(1)} collective-permute-done((bf16[128,1024]{1,0:T(8,128)(2,1)}, bf16[128,1024]{1,0:T(8,128)(2,1)S(1)}, u32[]{:S(2)}, u32[]{:S(2)}) %collective-permute-start.64) | collective-permute-done | bytes 262176 | tf_op jit(solution)/shard_map/ppermute | solution.py:84
  (280 shorter events, 97.8 us)
Async XLA Ops:
  7.2 136.7 %all-gather.2.cloned.1.call-start = ((), (), s32[]{:S(2)}) async-start(), calls=%async_computation.2 | async-start | bytes 1310720 | tf_op jit(solution)/shard_map/all_gather | solution.py:219
  17.1 14.8 %collective-permute-start.1 = (bf16[128,1024]{1,0:T(8,128)(2,1)S(1)}, bf16[128,1024]{1,0:T(8,128)(2,1)S(1)}, u32[]{:S(2)}, u32[]{:S(2)}) collective-permute-start(bf16[128,1024]{1,0:T(8,128)(2,1)S(1)} %get-tuple-element.104.refs_0_.refs_8_), channel_id=1, source_target_pairs={{0,2},{1,3},{2,0},{3,1},{4,6},{5,7},{6,4},{7,5},{8,10},{9,11},{10,... | collective-permute-start | bytes 786440 | tf_op jit(solution)/shard_map/ppermute | solution.py:84
  18.6 13.3 %collective-permute-start.2 = (bf16[128,1024]{1,0:T(8,128)(2,1)S(1)}, bf16[128,1024]{1,0:T(8,128)(2,1)}, u32[]{:S(2)}, u32[]{:S(2)}) collective-permute-start(bf16[128,1024]{1,0:T(8,128)(2,1)S(1)} %get-tuple-element.104.refs_0_.refs_8_), channel_id=1, source_target_pairs={{0,3},{1,2},{2,1},{3,0},{4,7},{5,6},{6,5},{7,4},{8,11},{9,10},{10,... | collective-permute-start | bytes 786440 | tf_op jit(solution)/shard_map/ppermute | solution.py:84
  18.6 16.1 %collective-permute-start.3 = (bf16[144,768]{1,0:T(8,128)(2,1)}, bf16[144,768]{1,0:T(8,128)(2,1)}, u32[]{:S(2)}, u32[]{:S(2)}) collective-permute-start(bf16[144,768]{1,0:T(8,128)(2,1)} %get-tuple-element.106), channel_id=1, source_target_pairs={{0,1},{1,0},{2,3},{3,2},{4,5},{5,4},{6,7},{7,6},{8,9},{9,8},{10,11... | collective-permute-start | bytes 663560 | tf_op jit(solution)/shard_map/ppermute | solution.py:84
  20.6 19.5 %collective-permute-start.4 = (bf16[144,768]{1,0:T(8,128)(2,1)}, bf16[144,768]{1,0:T(8,128)(2,1)}, u32[]{:S(2)}, u32[]{:S(2)}) collective-permute-start(bf16[144,768]{1,0:T(8,128)(2,1)} %get-tuple-element.107), channel_id=1, source_target_pairs={{0,2},{1,3},{2,0},{3,1},{4,6},{5,7},{6,4},{7,5},{8,10},{9,11},{10,... | collective-permute-start | bytes 663560 | tf_op jit(solution)/shard_map/ppermute | solution.py:84
  31.9 256.5 %reduce-scatter.5.cloned.1.call-start = ((), (), s32[]{:S(2)}) async-start(), calls=%async_computation.4 | async-start | bytes 2359296 | tf_op jit(solution)/shard_map/reduce_scatter | solution.py:335
  35.5 18.0 %collective-permute-start.24 = (bf16[128,2048]{1,0:T(8,128)(2,1)S(1)}, bf16[128,2048]{1,0:T(8,128)(2,1)S(1)}, u32[]{:S(2)}, u32[]{:S(2)}) collective-permute-start(bf16[128,2048]{1,0:T(8,128)(2,1)S(1)} %get-tuple-element.123), channel_id=1, source_target_pairs={{0,1},{1,0},{2,3},{3,2},{4,5},{5,4},{6,7},{7,6},{8,9},{9,8},{10,11... | collective-permute-start | bytes 1572872 | tf_op jit(solution)/shard_map/ppermute | solution.py:84
  37.6 22.7 %collective-permute-start.25 = (bf16[128,2048]{1,0:T(8,128)(2,1)S(1)}, bf16[128,2048]{1,0:T(8,128)(2,1)S(1)}, u32[]{:S(2)}, u32[]{:S(2)}) collective-permute-start(bf16[128,2048]{1,0:T(8,128)(2,1)S(1)} %get-tuple-element.124), channel_id=1, source_target_pairs={{0,2},{1,3},{2,0},{3,1},{4,6},{5,7},{6,4},{7,5},{8,10},{9,11},{10,... | collective-permute-start | bytes 1572872 | tf_op jit(solution)/shard_map/ppermute | solution.py:84
  40.1 31.0 %collective-permute-start.26 = (bf16[128,2048]{1,0:T(8,128)(2,1)S(1)}, bf16[128,2048]{1,0:T(8,128)(2,1)S(1)}, u32[]{:S(2)}, u32[]{:S(2)}) collective-permute-start(bf16[128,2048]{1,0:T(8,128)(2,1)S(1)} %get-tuple-element.125), channel_id=1, source_target_pairs={{0,3},{1,2},{2,1},{3,0},{4,7},{5,6},{6,5},{7,4},{8,11},{9,10},{10,... | collective-permute-start | bytes 1572872 | tf_op jit(solution)/shard_map/ppermute | solution.py:84
  47.1 24.0 %collective-permute-start.10 = (bf16[128,384]{1,0:T(8,128)(2,1)S(1)}, bf16[128,384]{1,0:T(8,128)(2,1)S(1)}, u32[]{:S(2)}, u32[]{:S(2)}) collective-permute-start(bf16[128,384]{1,0:T(8,128)(2,1)S(1)} %get-tuple-element.112), channel_id=1, source_target_pairs={{0,8},{4,12},{8,0},{12,4},{16,24},{20,28},{24,16},{28,20},{1,9},{5... | collective-permute-start | bytes 294920 | tf_op jit(solution)/shard_map/ppermute | solution.py:87
  48.7 22.9 %collective-permute-start.11 = (bf16[128,384]{1,0:T(8,128)(2,1)S(1)}, bf16[128,384]{1,0:T(8,128)(2,1)S(1)}, u32[]{:S(2)}, u32[]{:S(2)}) collective-permute-start(bf16[128,384]{1,0:T(8,128)(2,1)S(1)} %get-tuple-element.113), channel_id=1, source_target_pairs={{0,12},{4,8},{8,4},{12,0},{16,28},{20,24},{24,20},{28,16},{1,13},{... | collective-permute-start | bytes 294920 | tf_op jit(solution)/shard_map/ppermute | solution.py:87
  53.5 20.4 %collective-permute-start.12 = (bf16[128,384]{1,0:T(8,128)(2,1)S(1)}, bf16[128,384]{1,0:T(8,128)(2,1)S(1)}, u32[]{:S(2)}, u32[]{:S(2)}) collective-permute-start(bf16[128,384]{1,0:T(8,128)(2,1)S(1)} %get-tuple-element.114), channel_id=1, source_target_pairs={{0,16},{4,20},{8,24},{12,28},{16,0},{20,4},{24,8},{28,12},{1,17},{... | collective-permute-start | bytes 294920 | tf_op jit(solution)/shard_map/ppermute | solution.py:87
  60.3 56.2 %collective-permute-start.27 = (bf16[128,2048]{1,0:T(8,128)(2,1)S(1)}, bf16[128,2048]{1,0:T(8,128)(2,1)S(1)}, u32[]{:S(2)}, u32[]{:S(2)}) collective-permute-start(bf16[128,2048]{1,0:T(8,128)(2,1)S(1)} %collective-permute-done.24.refs_11_.refs_6_), channel_id=1, source_target_pairs={{0,4},{4,0},{8,12},{12,8},{16,20},{20,16},{24,28},{28,24},{1,5},{5... | collective-permute-start | bytes 1572872 | tf_op jit(solution)/shard_map/ppermute | solution.py:87
  71.1 45.5 %collective-permute-start.28 = (bf16[128,2048]{1,0:T(8,128)(2,1)S(1)}, bf16[128,2048]{1,0:T(8,128)(2,1)S(1)}, u32[]{:S(2)}, u32[]{:S(2)}) collective-permute-start(bf16[128,2048]{1,0:T(8,128)(2,1)S(1)} %collective-permute-done.25.refs_12_.refs_7_), channel_id=1, source_target_pairs={{0,4},{4,0},{8,12},{12,8},{16,20},{20,16},{24,28},{28,24},{1,5},{5... | collective-permute-start | bytes 1572872 | tf_op jit(solution)/shard_map/ppermute | solution.py:87
  71.1 45.5 %collective-permute-start.29 = (bf16[128,2048]{1,0:T(8,128)(2,1)S(1)}, bf16[128,2048]{1,0:T(8,128)(2,1)S(1)}, u32[]{:S(2)}, u32[]{:S(2)}) collective-permute-start(bf16[128,2048]{1,0:T(8,128)(2,1)S(1)} %collective-permute-done.26.refs_13_.refs_8_), channel_id=1, source_target_pairs={{0,4},{4,0},{8,12},{12,8},{16,20},{20,16},{24,28},{28,24},{1,5},{5... | collective-permute-start | bytes 1572872 | tf_op jit(solution)/shard_map/ppermute | solution.py:87
  73.9 11.1 %collective-permute-start.14 = (bf16[128,384]{1,0:T(8,128)(2,1)S(1)}, bf16[128,384]{1,0:T(8,128)(2,1)S(1)}, u32[]{:S(2)}, u32[]{:S(2)}) collective-permute-start(bf16[128,384]{1,0:T(8,128)(2,1)S(1)} %get-tuple-element.116), channel_id=1, source_target_pairs={{0,24},{4,28},{8,16},{12,20},{16,8},{20,12},{24,0},{28,4},{1,25},{... | collective-permute-start | bytes 294920 | tf_op jit(solution)/shard_map/ppermute | solution.py:87
  118.3 11.4 %collective-permute-start.30 = (bf16[128,1024]{1,0:T(8,128)(2,1)S(1)}, bf16[128,1024]{1,0:T(8,128)(2,1)S(1)}, u32[]{:S(2)}, u32[]{:S(2)}) collective-permute-start(bf16[128,1024]{1,0:T(8,128)(2,1)S(1)} %get-tuple-element.126.refs_0_), channel_id=1, source_target_pairs={{0,1},{1,0},{2,3},{3,2},{4,5},{5,4},{6,7},{7,6},{8,9},{9,8},{10,11... | collective-permute-start | bytes 786440 | tf_op jit(solution)/shard_map/ppermute | solution.py:84
  122.6 13.7 %collective-permute-start.31 = (bf16[128,1024]{1,0:T(8,128)(2,1)S(1)}, bf16[128,1024]{1,0:T(8,128)(2,1)S(1)}, u32[]{:S(2)}, u32[]{:S(2)}) collective-permute-start(bf16[128,1024]{1,0:T(8,128)(2,1)S(1)} %get-tuple-element.126.refs_0_), channel_id=1, source_target_pairs={{0,2},{1,3},{2,0},{3,1},{4,6},{5,7},{6,4},{7,5},{8,10},{9,11},{10,... | collective-permute-start | bytes 786440 | tf_op jit(solution)/shard_map/ppermute | solution.py:84
  122.6 13.7 %collective-permute-start.32 = (bf16[128,1024]{1,0:T(8,128)(2,1)S(1)}, bf16[128,1024]{1,0:T(8,128)(2,1)S(1)}, u32[]{:S(2)}, u32[]{:S(2)}) collective-permute-start(bf16[128,1024]{1,0:T(8,128)(2,1)S(1)} %get-tuple-element.126.refs_0_), channel_id=1, source_target_pairs={{0,3},{1,2},{2,1},{3,0},{4,7},{5,6},{6,5},{7,4},{8,11},{9,10},{10,... | collective-permute-start | bytes 786440 | tf_op jit(solution)/shard_map/ppermute | solution.py:84
  157.1 162.2 %reduce-scatter.3.cloned.1.call-start = ((), (), s32[]{:S(2)}) async-start(), calls=%async_computation.3 | async-start | bytes 2359296 | tf_op jit(solution)/shard_map/reduce_scatter | solution.py:335
  163.1 11.4 %collective-permute-start.35 = (bf16[128,1024]{1,0:T(8,128)(2,1)}, bf16[128,1024]{1,0:T(8,128)(2,1)S(1)}, u32[]{:S(2)}, u32[]{:S(2)}) collective-permute-start(bf16[128,1024]{1,0:T(8,128)(2,1)} %get-tuple-element.137), channel_id=1, source_target_pairs={{0,3},{1,2},{2,1},{3,0},{4,7},{5,6},{6,5},{7,4},{8,11},{9,10},{10,... | collective-permute-start | bytes 786440 | tf_op jit(solution)/shard_map/ppermute | solution.py:84
  179.8 21.6 %collective-permute-start.48 = (bf16[128,256]{1,0:T(8,128)(2,1)S(1)}, bf16[128,256]{1,0:T(8,128)(2,1)S(1)}, u32[]{:S(2)}, u32[]{:S(2)}) collective-permute-start(bf16[128,256]{1,0:T(8,128)(2,1)S(1)} %get-tuple-element.158), channel_id=1, source_target_pairs={{0,1},{1,9},{2,17},{3,25},{4,5},{5,13},{6,21},{7,29},{8,0},{9,8},{... | collective-permute-start | bytes 196616 | tf_op jit(solution)/shard_map/ppermute | solution.py:95
  182.9 18.4 %collective-permute-start.49 = (bf16[128,256]{1,0:T(8,128)(2,1)S(1)}, bf16[128,256]{1,0:T(8,128)(2,1)S(1)}, u32[]{:S(2)}, u32[]{:S(2)}) collective-permute-start(bf16[128,256]{1,0:T(8,128)(2,1)S(1)} %get-tuple-element.159), channel_id=1, source_target_pairs={{0,2},{1,10},{2,18},{3,26},{4,6},{5,14},{6,22},{7,30},{8,3},{9,11}... | collective-permute-start | bytes 196616 | tf_op jit(solution)/shard_map/ppermute | solution.py:95
  186.4 15.5 %collective-permute-start.50 = (bf16[128,256]{1,0:T(8,128)(2,1)S(1)}, bf16[128,256]{1,0:T(8,128)(2,1)S(1)}, u32[]{:S(2)}, u32[]{:S(2)}) collective-permute-start(bf16[128,256]{1,0:T(8,128)(2,1)S(1)} %get-tuple-element.160), channel_id=1, source_target_pairs={{0,3},{1,11},{2,19},{3,27},{4,7},{5,15},{6,23},{7,31},{8,2},{9,10}... | collective-permute-start | bytes 196616 | tf_op jit(solution)/shard_map/ppermute | solution.py:95
  186.4 15.5 %collective-permute-start.51 = (bf16[128,256]{1,0:T(8,128)(2,1)S(1)}, bf16[128,256]{1,0:T(8,128)(2,1)S(1)}, u32[]{:S(2)}, u32[]{:S(2)}) collective-permute-start(bf16[128,256]{1,0:T(8,128)(2,1)S(1)} %collective-permute-done.47.refs_3_), channel_id=1, source_target_pairs={{0,4},{4,0},{8,12},{12,8},{16,20},{20,16},{24,28},{28,24},{1,5},{5... | collective-permute-start | bytes 196616 | tf_op jit(solution)/shard_map/ppermute | solution.py:87
  214.2 10.5 %collective-permute-start.56 = (bf16[128,384]{1,0:T(8,128)(2,1)S(1)}, bf16[128,384]{1,0:T(8,128)(2,1)S(1)}, u32[]{:S(2)}, u32[]{:S(2)}) collective-permute-start(bf16[128,384]{1,0:T(8,128)(2,1)S(1)} %get-tuple-element.163), channel_id=1, source_target_pairs={{0,8},{4,12},{8,0},{12,4},{16,24},{20,28},{24,16},{28,20},{1,9},{5... | collective-permute-start | bytes 294920 | tf_op jit(solution)/shard_map/ppermute | solution.py:87
  215.6 14.8 %collective-permute-start.57 = (bf16[128,384]{1,0:T(8,128)(2,1)S(1)}, bf16[128,384]{1,0:T(8,128)(2,1)S(1)}, u32[]{:S(2)}, u32[]{:S(2)}) collective-permute-start(bf16[128,384]{1,0:T(8,128)(2,1)S(1)} %get-tuple-element.164), channel_id=1, source_target_pairs={{0,12},{4,8},{8,4},{12,0},{16,28},{20,24},{24,20},{28,16},{1,13},{... | collective-permute-start | bytes 294920 | tf_op jit(solution)/shard_map/ppermute | solution.py:87
  215.9 14.6 %collective-permute-start.58 = (bf16[128,384]{1,0:T(8,128)(2,1)S(1)}, bf16[128,384]{1,0:T(8,128)(2,1)S(1)}, u32[]{:S(2)}, u32[]{:S(2)}) collective-permute-start(bf16[128,384]{1,0:T(8,128)(2,1)S(1)} %get-tuple-element.165), channel_id=1, source_target_pairs={{0,16},{4,20},{8,24},{12,28},{16,0},{20,4},{24,8},{28,12},{1,17},{... | collective-permute-start | bytes 294920 | tf_op jit(solution)/shard_map/ppermute | solution.py:87
  219.4 12.8 %collective-permute-start.59 = (bf16[128,384]{1,0:T(8,128)(2,1)S(1)}, bf16[128,384]{1,0:T(8,128)(2,1)S(1)}, u32[]{:S(2)}, u32[]{:S(2)}) collective-permute-start(bf16[128,384]{1,0:T(8,128)(2,1)S(1)} %get-tuple-element.166), channel_id=1, source_target_pairs={{0,20},{4,16},{8,28},{12,24},{16,4},{20,0},{24,12},{28,8},{1,21},{... | collective-permute-start | bytes 294920 | tf_op jit(solution)/shard_map/ppermute | solution.py:87
  219.4 21.1 %collective-permute-start.60 = (bf16[128,384]{1,0:T(8,128)(2,1)S(1)}, bf16[128,384]{1,0:T(8,128)(2,1)S(1)}, u32[]{:S(2)}, u32[]{:S(2)}) collective-permute-start(bf16[128,384]{1,0:T(8,128)(2,1)S(1)} %get-tuple-element.167), channel_id=1, source_target_pairs={{0,24},{4,28},{8,16},{12,20},{16,8},{20,12},{24,0},{28,4},{1,25},{... | collective-permute-start | bytes 294920 | tf_op jit(solution)/shard_map/ppermute | solution.py:87
  224.7 18.8 %collective-permute-start.61 = (bf16[128,384]{1,0:T(8,128)(2,1)S(1)}, bf16[128,384]{1,0:T(8,128)(2,1)S(1)}, u32[]{:S(2)}, u32[]{:S(2)}) collective-permute-start(bf16[128,384]{1,0:T(8,128)(2,1)S(1)} %get-tuple-element.168), channel_id=1, source_target_pairs={{0,28},{4,24},{8,20},{12,16},{16,12},{20,8},{24,4},{28,0},{1,29},{... | collective-permute-start | bytes 294920 | tf_op jit(solution)/shard_map/ppermute | solution.py:87
  255.6 14.5 %collective-permute-start.36 = (bf16[4,128,1024]{2,1,0:T(8,128)(2,1)S(1)}, bf16[4,128,1024]{2,1,0:T(8,128)(2,1)S(1)}, u32[]{:S(2)}, u32[]{:S(2)}) collective-permute-start(bf16[4,128,1024]{2,1,0:T(8,128)(2,1)S(1)} %get-tuple-element.140), channel_id=1, source_target_pairs={{0,4},{4,0},{8,12},{12,8},{16,20},{20,16},{24,28},{28,24},{1,5},{5... | collective-permute-start | bytes 3145736 | tf_op jit(solution)/shard_map/ppermute | solution.py:87
  258.3 13.9 %collective-permute-start.40 = (bf16[128,1024]{1,0:T(8,128)(2,1)S(1)}, bf16[128,1024]{1,0:T(8,128)(2,1)S(1)}, u32[]{:S(2)}, u32[]{:S(2)}) collective-permute-start(bf16[128,1024]{1,0:T(8,128)(2,1)S(1)} %get-tuple-element.146), channel_id=1, source_target_pairs={{0,1},{1,0},{2,3},{3,2},{4,5},{5,4},{6,7},{7,6},{8,9},{9,8},{10,11... | collective-permute-start | bytes 786440 | tf_op jit(solution)/shard_map/ppermute | solution.py:84
  259.8 17.1 %collective-permute-start.66 = (bf16[144,768]{1,0:T(8,128)(2,1)S(1)}, bf16[144,768]{1,0:T(8,128)(2,1)S(1)}, u32[]{:S(2)}, u32[]{:S(2)}) collective-permute-start(bf16[144,768]{1,0:T(8,128)(2,1)S(1)} %get-tuple-element.184), channel_id=1, source_target_pairs={{0,8},{4,12},{8,0},{12,4},{16,24},{20,28},{24,16},{28,20},{1,9},{5... | collective-permute-start | bytes 663560 | tf_op jit(solution)/shard_map/ppermute | solution.py:87
  267.0 18.7 %collective-permute-start.67 = (bf16[144,768]{1,0:T(8,128)(2,1)S(1)}, bf16[144,768]{1,0:T(8,128)(2,1)S(1)}, u32[]{:S(2)}, u32[]{:S(2)}) collective-permute-start(bf16[144,768]{1,0:T(8,128)(2,1)S(1)} %get-tuple-element.185), channel_id=1, source_target_pairs={{0,16},{4,20},{8,24},{12,28},{16,0},{20,4},{24,8},{28,12},{1,17},{... | collective-permute-start | bytes 663560 | tf_op jit(solution)/shard_map/ppermute | solution.py:87
  268.6 18.2 %collective-permute-start.68 = (bf16[144,768]{1,0:T(8,128)(2,1)S(1)}, bf16[144,768]{1,0:T(8,128)(2,1)S(1)}, u32[]{:S(2)}, u32[]{:S(2)}) collective-permute-start(bf16[144,768]{1,0:T(8,128)(2,1)S(1)} %get-tuple-element.186), channel_id=1, source_target_pairs={{0,24},{4,28},{8,16},{12,20},{16,8},{20,12},{24,0},{28,4},{1,25},{... | collective-permute-start | bytes 663560 | tf_op jit(solution)/shard_map/ppermute | solution.py:87
  271.7 19.2 %collective-permute-start.37 = (bf16[128,1024]{1,0:T(8,128)(2,1)}, bf16[128,1024]{1,0:T(8,128)(2,1)S(1)}, u32[]{:S(2)}, u32[]{:S(2)}) collective-permute-start(bf16[128,1024]{1,0:T(8,128)(2,1)} %get-tuple-element.142), channel_id=1, source_target_pairs={{0,1},{1,0},{2,3},{3,2},{4,5},{5,4},{6,7},{7,6},{8,9},{9,8},{10,11... | collective-permute-start | bytes 786440 | tf_op jit(solution)/shard_map/ppermute | solution.py:84
  272.1 20.9 %collective-permute-start.38 = (bf16[128,1024]{1,0:T(8,128)(2,1)}, bf16[128,1024]{1,0:T(8,128)(2,1)S(1)}, u32[]{:S(2)}, u32[]{:S(2)}) collective-permute-start(bf16[128,1024]{1,0:T(8,128)(2,1)} %get-tuple-element.143), channel_id=1, source_target_pairs={{0,2},{1,3},{2,0},{3,1},{4,6},{5,7},{6,4},{7,5},{8,10},{9,11},{10,... | collective-permute-start | bytes 786440 | tf_op jit(solution)/shard_map/ppermute | solution.py:84
  276.8 18.2 %collective-permute-start.39 = (bf16[128,1024]{1,0:T(8,128)(2,1)}, bf16[128,1024]{1,0:T(8,128)(2,1)S(1)}, u32[]{:S(2)}, u32[]{:S(2)}) collective-permute-start(bf16[128,1024]{1,0:T(8,128)(2,1)} %get-tuple-element.144), channel_id=1, source_target_pairs={{0,3},{1,2},{2,1},{3,0},{4,7},{5,6},{6,5},{7,4},{8,11},{9,10},{10,... | collective-permute-start | bytes 786440 | tf_op jit(solution)/shard_map/ppermute | solution.py:84
  285.7 17.2 %collective-permute-start.41 = (bf16[128,1024]{1,0:T(8,128)(2,1)}, bf16[128,1024]{1,0:T(8,128)(2,1)}, u32[]{:S(2)}, u32[]{:S(2)}) collective-permute-start(bf16[128,1024]{1,0:T(8,128)(2,1)} %get-tuple-element.147), channel_id=1, source_target_pairs={{0,2},{1,3},{2,0},{3,1},{4,6},{5,7},{6,4},{7,5},{8,10},{9,11},{10,... | collective-permute-start | bytes 786440 | tf_op jit(solution)/shard_map/ppermute | solution.py:84
  287.6 16.6 %collective-permute-start.42 = (bf16[128,1024]{1,0:T(8,128)(2,1)}, bf16[128,1024]{1,0:T(8,128)(2,1)}, u32[]{:S(2)}, u32[]{:S(2)}) collective-permute-start(bf16[128,1024]{1,0:T(8,128)(2,1)} %get-tuple-element.148), channel_id=1, source_target_pairs={{0,3},{1,2},{2,1},{3,0},{4,7},{5,6},{6,5},{7,4},{8,11},{9,10},{10,... | collective-permute-start | bytes 786440 | tf_op jit(solution)/shard_map/ppermute | solution.py:84
  291.6 25.7 %collective-permute-start.69 = (bf16[48,1792]{1,0:T(8,128)(2,1)}, bf16[48,1792]{1,0:T(8,128)(2,1)S(1)}, u32[]{:S(2)}, u32[]{:S(2)}) collective-permute-start(bf16[48,1792]{1,0:T(8,128)(2,1)} %get-tuple-element.190), channel_id=1, source_target_pairs={{0,1},{1,0},{2,3},{3,2},{4,5},{5,4},{6,7},{7,6},{8,9},{9,8},{10,11... | collective-permute-start | bytes 516104 | tf_op jit(solution)/shard_map/ppermute | solution.py:84
  293.8 25.5 %collective-permute-start.70 = (bf16[48,1792]{1,0:T(8,128)(2,1)}, bf16[48,1792]{1,0:T(8,128)(2,1)}, u32[]{:S(2)}, u32[]{:S(2)}) collective-permute-start(bf16[48,1792]{1,0:T(8,128)(2,1)} %get-tuple-element.191), channel_id=1, source_target_pairs={{0,2},{1,3},{2,0},{3,1},{4,6},{5,7},{6,4},{7,5},{8,10},{9,11},{10,... | collective-permute-start | bytes 516104 | tf_op jit(solution)/shard_map/ppermute | solution.py:84
  295.7 25.2 %collective-permute-start.71 = (bf16[48,1792]{1,0:T(8,128)(2,1)}, bf16[48,1792]{1,0:T(8,128)(2,1)}, u32[]{:S(2)}, u32[]{:S(2)}) collective-permute-start(bf16[48,1792]{1,0:T(8,128)(2,1)} %get-tuple-element.192), channel_id=1, source_target_pairs={{0,3},{1,2},{2,1},{3,0},{4,7},{5,6},{6,5},{7,4},{8,11},{9,10},{10,... | collective-permute-start | bytes 516104 | tf_op jit(solution)/shard_map/ppermute | solution.py:84
  312.1 12.9 %collective-permute-start.62 = (bf16[128,1024]{1,0:T(8,128)(2,1)}, bf16[128,1024]{1,0:T(8,128)(2,1)S(1)}, u32[]{:S(2)}, u32[]{:S(2)}) collective-permute-start(bf16[128,1024]{1,0:T(8,128)(2,1)} %get-tuple-element.172), channel_id=1, source_target_pairs={{0,1},{1,0},{2,3},{3,2},{4,5},{5,4},{6,7},{7,6},{8,9},{9,8},{10,11... | collective-permute-start | bytes 786440 | tf_op jit(solution)/shard_map/ppermute | solution.py:84
  314.4 11.3 %collective-permute-start.63 = (bf16[128,1024]{1,0:T(8,128)(2,1)}, bf16[128,1024]{1,0:T(8,128)(2,1)S(1)}, u32[]{:S(2)}, u32[]{:S(2)}) collective-permute-start(bf16[128,1024]{1,0:T(8,128)(2,1)} %get-tuple-element.173), channel_id=1, source_target_pairs={{0,2},{1,3},{2,0},{3,1},{4,6},{5,7},{6,4},{7,5},{8,10},{9,11},{10,... | collective-permute-start | bytes 786440 | tf_op jit(solution)/shard_map/ppermute | solution.py:84
  318.0 13.2 %collective-permute-start.64 = (bf16[128,1024]{1,0:T(8,128)(2,1)}, bf16[128,1024]{1,0:T(8,128)(2,1)S(1)}, u32[]{:S(2)}, u32[]{:S(2)}) collective-permute-start(bf16[128,1024]{1,0:T(8,128)(2,1)} %get-tuple-element.174), channel_id=1, source_target_pairs={{0,3},{1,2},{2,1},{3,0},{4,7},{5,6},{6,5},{7,4},{8,11},{9,10},{10,... | collective-permute-start | bytes 786440 | tf_op jit(solution)/shard_map/ppermute | solution.py:84
  319.3 11.9 %collective-permute-start.46 = (bf16[128,1024]{1,0:T(8,128)(2,1)}, bf16[128,1024]{1,0:T(8,128)(2,1)S(1)}, u32[]{:S(2)}, u32[]{:S(2)}) collective-permute-start(bf16[128,1024]{1,0:T(8,128)(2,1)} %reduce-scatter.3.cloned.1.call-done), channel_id=1, source_target_pairs={{0,0},{1,8},{2,16},{3,24},{4,1},{5,9},{6,17},{7,25},{8,2},{9,10},{... | collective-permute-start | bytes 786440 | tf_op jit(solution)/shard_map/ppermute | solution.py:95
  (100 other events, 1184.8 us)
Sparse Core Ops, SparseCore 0:
  32.1 39.5 all-gather.1
  157.2 35.3 reduce-scatter.4
  194.9 52.7 reduce-scatter.2

commit v3 on v2

--- a/solution.py
+++ b/solution.py
@@ -1,3 +1,5 @@
+import functools
+
 import jax
 import jax.numpy as jnp
 from jax import lax
@@ -218,20 +220,23 @@
         dz, _ = lax.optimization_barrier((d_result.astype(BF), n_all))
         dz_all = lax.all_gather(dz, "fsdp", axis=0, tiled=True)
 
-        def positions(i, block, along):
-            dims = (rows, 1) if along == 0 else (1, rows)
-            at = lax.broadcasted_iota(jnp.int32, dims, along)
-            pos = at + i[ORDER + block * slots] * blk
-            for s in range(1, slots):
-                moved = at - s * blk + i[ORDER + block * slots + s] * blk
-                pos = jnp.where(at >= s * blk, moved, pos)
-            return pos
+        low_rows = length // 2
+
+        def place(i, block, slot):
+            late = i[ORDER + (i[CI] ^ block) * slots + slot] >= n_ctx * slots // 2
+            return pl.multiple_of(jnp.where(late, low_rows, 0) + block * blk, blk)
 
         def fill_positions(i, kpos, qpos):
+            along = lax.broadcasted_iota(jnp.int32, (1, blk), 1)
+            down_to = lax.broadcasted_iota(jnp.int32, (blk, 1), 0)
             for e in range(n_ctx):
-                here = slice(e * rows, (e + 1) * rows)
-                kpos[:, here] = positions(i, i[CI] ^ e, 1)
-                qpos[here, :] = positions(i, i[CI] ^ e, 0)
+                at = ORDER + (i[CI] ^ e) * slots
+                early = jnp.minimum(i[at], i[at + 1]) * blk
+                late = jnp.maximum(i[at], i[at + 1]) * blk
+                for base, start in ((0, early), (low_rows, late)):
+                    here = slice(base + e * blk, base + (e + 1) * blk)
+                    kpos[:, here] = start + along
+                    qpos[here, :] = start + down_to
 
         tall = 2 * rows
         places = [pltpu.VMEM((1, length), jnp.int32), pltpu.VMEM((length, 1), jnp.int32)]
@@ -241,16 +246,17 @@
             seq, att, lse_ref, refs = refs[0], refs[1], refs[2], refs[3:]
             send, (kpos, qpos) = refs[:n_f], refs[n_f:]
             for e in range(n_ctx):
-                seq[e * rows : (e + 1) * rows, :] = got[e][...]
+                for j in range(slots):
+                    seq[pl.ds(place(i, e, j), blk), :] = got[e][j * blk : (j + 1) * blk, :]
             fill_positions(i, kpos, qpos)
 
-            def step(e, _):
+            def step(span, e, _):
                 here = pl.ds(pl.multiple_of(e * tall, tall), tall)
-                allowed = kpos[...] <= qpos[here, :]
+                allowed = kpos[:, :span] <= qpos[here, :]
                 for h in range(heads):
                     cut = slice(h * hd, (h + 1) * hd)
-                    keys = seq[:, pair + h * hd : pair + (h + 1) * hd]
-                    values = seq[:, 2 * pair + h * hd : 2 * pair + (h + 1) * hd]
+                    keys = seq[:span, pair + h * hd : pair + (h + 1) * hd]
+                    values = seq[:span, 2 * pair + h * hd : 2 * pair + (h + 1) * hd]
                     scores = jnp.where(allowed, through(seq[here, cut], keys), -1e30)
                     top = jnp.max(scores, axis=1, keepdims=True)
                     probs = jnp.exp(scores - top)
@@ -260,12 +266,15 @@
                     lse_ref[here, cut] = jnp.broadcast_to(top + jnp.log(norm), (tall, hd))
                 return 0
 
-            lax.fori_loop(0, length // tall, step, 0)
+            steps = low_rows // tall
+            lax.fori_loop(0, steps, functools.partial(step, low_rows), 0)
+            lax.fori_loop(steps, 2 * steps, functools.partial(step, length), 0)
             for m in range(n_f):
                 for core in range(2):
                     block = (2 * (m ^ i[FI]) + core) ^ i[CI]
-                    at = pl.multiple_of(block * rows, rows)
-                    send[m][core * rows : (core + 1) * rows, :] = att[pl.ds(at, rows), :]
+                    for j in range(slots):
+                        to = core * rows + j * blk
+                        send[m][to : to + blk, :] = att[pl.ds(place(i, block, j), blk), :]
 
         outs = [shaped((length, 3 * pair), BF), shaped((length, pair), BF), shaped((length, pair), F32)]
         outs += [shaped((tall, pair), BF)] * n_f
@@ -309,7 +318,7 @@
             a_refs, refs = refs[:n_f], refs[n_f:]
             own_w_ref, bias, refs = refs[0], refs[1], refs[2:]
             got_u, other_u = refs[: n_f - 1], refs[n_f - 1 : 2 * n_f - 2]
-            up, a_ref, gel, slope_ref = refs[2 * n_f - 2 :]
+            dz_ref, up, a_ref, gel, slope_ref, g_ref = refs[2 * n_f - 2 :]
             fill_rows(up, own_w_ref, got_u, other_u, i[FI], i[CORE], slice(0, hidden))
             for k in range(n_f):
                 here = pl.ds(pl.multiple_of((i[FI] ^ k) * rows, rows), rows)
@@ -318,18 +327,21 @@
                 value, slope = gelu_parts(dot(a_two, up[...]) + bias[...].astype(F32))
                 gel[here, :] = value.astype(BF)
                 slope_ref[here, :] = slope.astype(BF)
+            for at in range(0, hidden, wide):
+                cut = slice(at, at + wide)
+                g_ref[cut, :] = outer(gel[:, cut], dz_ref[...]).astype(BF)
 
         outs = [
             shaped((width, hidden), BF),
             shaped((all_rows, width), BF),
             shaped((all_rows, hidden), BF),
             shaped((all_rows, hidden), BF),
+            shaped((hidden, width), BF),
         ]
-        full_up, a2_all, gelled, slope = call(
-            forward, outs, idx, a2_parts + [own_w, up_bias] + got_w + other_w,
-            flops=2 * all_rows * width * hidden,
-        )
-        g_down = outer(gelled, dz_all).astype(BF)
+        full_up, a2_all, gelled, slope, g_down = call(
+            forward, outs, idx, a2_parts + [own_w, up_bias] + got_w + other_w + [dz_all],
+            flops=4 * all_rows * width * hidden, mib=54,
+        )
 
         def scatter_ctx(g):
             return lax.psum_scatter(g, "ctx", scatter_dimension=0, tiled=True)
@@ -406,21 +418,21 @@
                 for swap in range(2):
                     part = got[swap * n_f + m]
                     block = (2 * (m ^ i[FI]) + (i[CORE] ^ swap)) ^ i[CI]
-                    at = pl.multiple_of(block * rows, rows)
-                    d_out[pl.ds(at, rows), :] = jnp.where(
-                        i[CORE] == 0, part[:, :pair], part[:, pair:]
-                    )
+                    rows_of = jnp.where(i[CORE] == 0, part[:, :pair], part[:, pair:])
+                    for j in range(slots):
+                        at = place(i, block, j)
+                        d_out[pl.ds(at, blk), :] = rows_of[j * blk : (j + 1) * blk, :]
             d_keys[...] = jnp.zeros_like(d_keys)
             d_values[...] = jnp.zeros_like(d_values)
 
-            def step(e, _):
+            def step(span, e, _):
                 here = pl.ds(pl.multiple_of(e * tall, tall), tall)
-                allowed = kpos[...] <= qpos[here, :]
+                allowed = kpos[:, :span] <= qpos[here, :]
                 for h in range(heads):
                     cut = slice(h * hd, (h + 1) * hd)
                     query, d_att = seq_ref[here, cut], d_out[here, cut]
-                    keys = seq_ref[:, pair + h * hd : pair + (h + 1) * hd]
-                    values = seq_ref[:, 2 * pair + h * hd : 2 * pair + (h + 1) * hd]
+                    keys = seq_ref[:span, pair + h * hd : pair + (h + 1) * hd]
+                    values = seq_ref[:span, 2 * pair + h * hd : 2 * pair + (h + 1) * hd]
                     lse = lse_ref[here, h * hd : h * hd + 1]
                     scores = jnp.where(allowed, through(query, keys), -1e30)
                     probs = jnp.exp(scores - lse)
@@ -429,16 +441,19 @@
                     )
                     d_scores = (probs * (through(d_att, values) - delta)).astype(BF)
                     d_query[here, cut] = dot(d_scores, keys) * SCALE
-                    d_keys[:, cut] += outer(d_scores, query)
-                    d_values[:, cut] += outer(probs.astype(BF), d_att)
+                    d_keys[:span, cut] += outer(d_scores, query)
+                    d_values[:span, cut] += outer(probs.astype(BF), d_att)
                 return 0
 
-            lax.fori_loop(0, length // tall, step, 0)
+            steps = low_rows // tall
+            lax.fori_loop(0, steps, functools.partial(step, low_rows), 0)
+            lax.fori_loop(steps, 2 * steps, functools.partial(step, length), 0)
             for e in range(n_ctx):
-                here = slice(e * rows, (e + 1) * rows)
-                send[e][:, :pair] = d_query[here, :].astype(BF)
-                send[e][:, pair : 2 * pair] = d_keys[here, :].astype(BF)
-                send[e][:, 2 * pair :] = d_values[here, :].astype(BF)
+                for j in range(slots):
+                    here, to = pl.ds(place(i, e, j), blk), slice(j * blk, (j + 1) * blk)
+                    send[e][to, :pair] = d_query[here, :].astype(BF)
+                    send[e][to, pair : 2 * pair] = d_keys[here, :].astype(BF)
+                    send[e][to, 2 * pair :] = d_values[here, :].astype(BF)
             sum_ref[...] = jnp.zeros_like(sum_ref)
             sum_ref[3:4, :] = jnp.sum(d_query[...], axis=0, keepdims=True)
             sum_ref[4:5, :] = jnp.sum(d_values[...], axis=0, keepdims=True)

time: 346 us -> 351 us (1.014)
  waiting for transfers between devices: 125 us -> 141 us
  starting transfers between devices: 103 us -> 97.1 us
  matrix products: 8.07 us -> 3.9 us
  local copies, waits for them, and re-layouts: 28 us -> 24.4 us
    ppermute x36, waiting for transfers between devices: 45.1 us -> 52.1 us  [ctx_to(): return lax.ppermute(x, 'ctx', [(i, i ^ e) for i in range(n_ctx)])]
    ppermute x36, starting transfers between devices: 46.1 us -> 40.6 us  [ctx_to(): return lax.ppermute(x, 'ctx', [(i, i ^ e) for i in range(n_ctx)])]
    ppermute x27, waiting for transfers between devices: 61.6 us -> 67 us  [fsdp_to(): return lax.ppermute(x, 'fsdp', [(f, f ^ k) for f in range(n_f)])]
    dot_general x2 -> x1, matrix products: 8.07 us -> 3.9 us  [outer(): lax.dot_general(left, right, (((0,), (0,)), ((), ())), preferred_element_...]
    unnamed x147 -> x155, local copies, waits for them, and re-layouts: 26.7 us -> 23.1 us
  transfers between devices with their start and end apart: 75 -> 75, of which waited for: 34 -> 34; matrix products, arithmetic and copies ran while one was open for 2% -> 1% of each run, Pallas kernels for 14% -> 12%
where the time goes in v3:
time: 351 us; the launch traced here: 345 us
  waiting for transfers between devices  141 us (40%)
  starting transfers between devices  97.1 us (28%)
  Pallas kernels  62.8 us (18%)
  local copies, waits for them, and re-layouts  24.4 us (7%)
  between operations  14.4 us (4%)
  matrix products  3.9 us (1%)
    ppermute x27, waiting for transfers between devices, fsdp_to(): return lax.ppermute(x, 'fsdp', [(f, f ^ k) for f in range(n_f)])  67 us
    pallas_call x20, Pallas kernels, call(): pl.pallas_call(kernel, out_shape=outs, in_specs=[pl.BlockSpec(memory_spac...  62.8 us
    ppermute x36, waiting for transfers between devices, ctx_to(): return lax.ppermute(x, 'ctx', [(i, i ^ e) for i in range(n_ctx)])  52.1 us
    ppermute x36, starting transfers between devices, ctx_to(): return lax.ppermute(x, 'ctx', [(i, i ^ e) for i in range(n_ctx)])  40.6 us
    ppermute x27, starting transfers between devices, fsdp_to(): return lax.ppermute(x, 'fsdp', [(f, f ^ k) for f in range(n_f)])  35.5 us
    unnamed x155, local copies, waits for them, and re-layouts  23.1 us
    ppermute x9, waiting for transfers between devices, both_to(): return lax.ppermute(x, ('ctx', 'fsdp'), pairs)  21.3 us
    ppermute x9, starting transfers between devices, both_to(): return lax.ppermute(x, ('ctx', 'fsdp'), pairs)  20.9 us
  transfers between devices with their start and end apart: 75, of which 34 were waited for; matrix products, arithmetic and copies ran while one was open for 1% of the time, Pallas kernels for 12%

profile of v3, /device:TPU:0, one launch (start us, length us, event | category | flops | bytes accessed | tf_op | source)
XLA Modules:
  0.0 345.1 jit_solution(7009843607322446341)
XLA Ops:
  14.8 3.9 %collective-permute-start.2 = (bf16[128,1024]{1,0:T(8,128)(2,1)S(1)}, bf16[128,1024]{1,0:T(8,128)(2,1)S(1)}, u32[]{:S(2)}, u32[]{:S(2)}) collective-permute-start(bf16[128,1024]{1,0:T(8,128)(2,1)S(1)} %get-tuple-element.105.refs_0_.refs_8_), channel_id=1, source_target_pairs={{0,3},{1,2},{2,1},{3,0},{4,7},{5,6},{6,5},{7,4},{8,11},{9,10},{10,... | collective-permute-start | bytes 786440 | tf_op jit(solution)/shard_map/ppermute | solution.py:86
  22.0 3.9 %collective-permute-done.2.refs_3_.refs_11_ = bf16[128,1024]{1,0:T(8,128)(2,1)S(1)} collective-permute-done((bf16[128,1024]{1,0:T(8,128)(2,1)S(1)}, bf16[128,1024]{1,0:T(8,128)(2,1)S(1)}, u32[]{:S(2)}, u32[]{:S(2)}) %collective-permute-start.2) | collective-permute-done | bytes 262176 | tf_op jit(solution)/shard_map/ppermute | solution.py:86
  25.9 4.7 %collective-permute-done.1.refs_2_.refs_10_ = bf16[128,1024]{1,0:T(8,128)(2,1)S(1)} collective-permute-done((bf16[128,1024]{1,0:T(8,128)(2,1)S(1)}, bf16[128,1024]{1,0:T(8,128)(2,1)S(1)}, u32[]{:S(2)}, u32[]{:S(2)}) %collective-permute-start.1) | collective-permute-done | bytes 262176 | tf_op jit(solution)/shard_map/ppermute | solution.py:86
  32.5 2.7 collective-permute-start.5
  39.3 7.6 %collective-permute-done.4.refs_7_ = bf16[144,768]{1,0:T(8,128)(2,1)S(1)} collective-permute-done((bf16[144,768]{1,0:T(8,128)(2,1)}, bf16[144,768]{1,0:T(8,128)(2,1)S(1)}, u32[]{:S(2)}, u32[]{:S(2)}) %collective-permute-start.4) | collective-permute-done | bytes 221216 | tf_op jit(solution)/shard_map/ppermute | solution.py:86
  50.1 2.3 shard_map.170
  55.5 16.9 %collective-permute-done.25.refs_12_.refs_7_ = bf16[128,2048]{1,0:T(8,128)(2,1)S(1)} collective-permute-done((bf16[128,2048]{1,0:T(8,128)(2,1)S(1)}, bf16[128,2048]{1,0:T(8,128)(2,1)S(1)}, u32[]{:S(2)}, u32[]{:S(2)}) %collective-permute-start.25) | collective-permute-done | bytes 524320 | tf_op jit(solution)/shard_map/ppermute | solution.py:86
  73.0 3.2 collective-permute-start.12
  76.3 7.7 %collective-permute-done.12.refs_4_ = bf16[128,384]{1,0:T(8,128)(2,1)S(1)} collective-permute-done((bf16[128,384]{1,0:T(8,128)(2,1)S(1)}, bf16[128,384]{1,0:T(8,128)(2,1)S(1)}, u32[]{:S(2)}, u32[]{:S(2)}) %collective-permute-start.12) | collective-permute-done | bytes 98336 | tf_op jit(solution)/shard_map/ppermute | solution.py:89
  84.0 3.3 collective-permute-start.14
  90.5 3.8 %collective-permute-done.15.refs_7_ = bf16[128,384]{1,0:T(8,128)(2,1)S(1)} collective-permute-done((bf16[128,384]{1,0:T(8,128)(2,1)S(1)}, bf16[128,384]{1,0:T(8,128)(2,1)S(1)}, u32[]{:S(2)}, u32[]{:S(2)}) %collective-permute-start.15) | collective-permute-done | bytes 98336 | tf_op jit(solution)/shard_map/ppermute | solution.py:89
  94.3 5.8 %shard_map.171 = (bf16[1024,384]{1,0:T(8,128)(2,1)S(1)}, bf16[1024,128]{1,0:T(8,128)(2,1)S(1)}, f32[1024,128]{1,0:T(8,128)S(1)}, bf16[256,128]{1,0:T(8,128)(2,1)...) custom-call(s32[24]{0:T(128)S(1)} %concatenate.6.i, ...), custom_call_target="tpu_custom_call" | custom-call | flops 536870912 | bytes 2621440 | tf_op jit(solution)/shard_map/pallas_call | solution.py:68
  102.5 4.4 %collective-permute-start.17 = (bf16[256,128]{1,0:T(8,128)(2,1)S(1)}, bf16[256,128]{1,0:T(8,128)(2,1)S(1)}, u32[]{:S(2)}, u32[]{:S(2)}) collective-permute-start(bf16[256,128]{1,0:T(8,128)(2,1)S(1)} %get-tuple-element.120), channel_id=1, source_target_pairs={{0,8},{1,0},{2,24},{3,16},{4,12},{5,4},{6,28},{7,20},{8,9},{9,1},{... | collective-permute-start | bytes 196616 | tf_op jit(solution)/shard_map/ppermute | solution.py:97
  106.8 6.6 %collective-permute-start.18 = (bf16[256,128]{1,0:T(8,128)(2,1)S(1)}, bf16[256,128]{1,0:T(8,128)(2,1)S(1)}, u32[]{:S(2)}, u32[]{:S(2)}) collective-permute-start(bf16[256,128]{1,0:T(8,128)(2,1)S(1)} %get-tuple-element.121), channel_id=1, source_target_pairs={{0,16},{1,24},{2,0},{3,8},{4,20},{5,28},{6,4},{7,12},{8,17},{9,25}... | collective-permute-start | bytes 196616 | tf_op jit(solution)/shard_map/ppermute | solution.py:97
  115.6 2.9 collective-permute-done.19.refs_5_.refs_3_
  122.9 2.5 collective-permute-start.32
  125.4 2.7 collective-permute-start.31
  128.1 4.9 %collective-permute-done.32.refs_3_ = bf16[128,1024]{1,0:T(8,128)(2,1)S(1)} collective-permute-done((bf16[128,1024]{1,0:T(8,128)(2,1)S(1)}, bf16[128,1024]{1,0:T(8,128)(2,1)S(1)}, u32[]{:S(2)}, u32[]{:S(2)}) %collective-permute-start.32) | collective-permute-done | bytes 262176 | tf_op jit(solution)/shard_map/ppermute | solution.py:86
  133.1 5.8 %collective-permute-done.31.refs_2_ = bf16[128,1024]{1,0:T(8,128)(2,1)S(1)} collective-permute-done((bf16[128,1024]{1,0:T(8,128)(2,1)S(1)}, bf16[128,1024]{1,0:T(8,128)(2,1)S(1)}, u32[]{:S(2)}, u32[]{:S(2)}) %collective-permute-start.31) | collective-permute-done | bytes 262176 | tf_op jit(solution)/shard_map/ppermute | solution.py:86
  140.0 8.2 %shard_map.174 = (bf16[1024,1024]{1,0:T(8,128)(2,1)}, bf16[512,1024]{1,0:T(8,128)(2,1)}, bf16[512,1024]{1,0:T(8,128)(2,1)}, bf16[512,1024]{1,0:T(8,128)(2,1)}, bf16[1024,1024]{1,0:T(8,128)(2,1)}) custom-call(s32[24]{0:T(128)} %copy-done.35, bf16[128,1024]{1,0:T(8,128)(2,1)} %copy-done.50, bf16[128,1024]{1,0:T(8,128)(2,1)} %collective-permute-done.30.refs_1_, ...), custom_call_target="tpu_custom_call" | custom-call | flops 2147483648 | bytes 13633536 | tf_op jit(solution)/shard_map/pallas_call | solution.py:68
  148.2 9.3 %shard_map.176 = (bf16[512,1024]{1,0:T(8,128)(2,1)}, f32[1,1024]{1,0:T(1,128)}, f32[128,1024]{1,0:T(8,128)}, bf16[128,1024]{1,0:T(8,128)(2,1)}, bf16[128,1024]{1,0:T(8,128)(2,1)}, /*index=5*/bf16[128,1024]{1,0:T(8,128)(2,1)}) custom-call(s32[24]{0:T(128)} %copy-done.35, bf16[512,1024]{1,0:T(8,128)(2,1)} %all-gather.2.cloned.1.call-done.refs_12_.dz_ref, ...), custom_call_target="tpu_custom_call" | custom-call | flops 2147483648 | bytes 8654848 | tf_op jit(solution)/shard_map/pallas_call | solution.py:68
  157.5 3.9 %convolution_convert_fusion = bf16[1024,1024]{1,0:T(8,128)(2,1)} fusion(bf16[512,1024]{1,0:T(8,128)(2,1)S(1)} %copy-done.76, bf16[512,1024]{1,0:T(8,128)(2,1)} %get-tuple-element.190), kind=kOutput, calls=%fused_computation | convolution fusion | flops 1074790400 | bytes 4194304 | tf_op jit(solution)/shard_map/dot_general | solution.py:51
  162.1 2.4 collective-permute-start.33
  166.0 5.8 %collective-permute-done.33.refs_5_ = bf16[128,1024]{1,0:T(8,128)(2,1)S(1)} collective-permute-done((bf16[128,1024]{1,0:T(8,128)(2,1)}, bf16[128,1024]{1,0:T(8,128)(2,1)S(1)}, u32[]{:S(2)}, u32[]{:S(2)}) %collective-permute-start.33) | collective-permute-done | bytes 262176 | tf_op jit(solution)/shard_map/ppermute | solution.py:86
  171.8 6.4 %collective-permute-done.34.refs_6_ = bf16[128,1024]{1,0:T(8,128)(2,1)S(1)} collective-permute-done((bf16[128,1024]{1,0:T(8,128)(2,1)}, bf16[128,1024]{1,0:T(8,128)(2,1)S(1)}, u32[]{:S(2)}, u32[]{:S(2)}) %collective-permute-start.34) | collective-permute-done | bytes 262176 | tf_op jit(solution)/shard_map/ppermute | solution.py:86
  182.9 2.9 collective-permute-start.48
  185.7 2.8 collective-permute-start.49
  188.7 17.4 %collective-permute-done.48.refs_4_ = bf16[128,256]{1,0:T(8,128)(2,1)S(1)} collective-permute-done((bf16[128,256]{1,0:T(8,128)(2,1)S(1)}, bf16[128,256]{1,0:T(8,128)(2,1)S(1)}, u32[]{:S(2)}, u32[]{:S(2)}) %collective-permute-start.48) | collective-permute-done | bytes 65568 | tf_op jit(solution)/shard_map/ppermute | solution.py:97
  207.9 9.0 %shard_map.182 = (f32[8,128]{1,0:T(8,128)S(1)}, bf16[128,384]{1,0:T(8,128)(2,1)S(1)}, bf16[128,384]{1,0:T(8,128)(2,1)S(1)}, bf16[128,384]{1,0:T(8,128)(2,1)S(1)}...) custom-call(s32[24]{0:T(128)S(1)} %copy-done.36, ...), custom_call_target="tpu_custom_call" | custom-call | flops 1342177280 | bytes 2887680 | tf_op jit(solution)/shard_map/pallas_call | solution.py:68
  219.7 3.1 collective-permute-start.58
  222.8 3.8 %collective-permute-start.60 = (bf16[128,384]{1,0:T(8,128)(2,1)S(1)}, bf16[128,384]{1,0:T(8,128)(2,1)S(1)}, u32[]{:S(2)}, u32[]{:S(2)}) collective-permute-start(bf16[128,384]{1,0:T(8,128)(2,1)S(1)} %get-tuple-element.169), channel_id=1, source_target_pairs={{0,24},{4,28},{8,16},{12,20},{16,8},{20,12},{24,0},{28,4},{1,25},{... | collective-permute-start | bytes 294920 | tf_op jit(solution)/shard_map/ppermute | solution.py:89
  226.6 5.0 %collective-permute-done.56.refs_2_ = bf16[128,384]{1,0:T(8,128)(2,1)S(1)} collective-permute-done((bf16[128,384]{1,0:T(8,128)(2,1)S(1)}, bf16[128,384]{1,0:T(8,128)(2,1)S(1)}, u32[]{:S(2)}, u32[]{:S(2)}) %collective-permute-start.56) | collective-permute-done | bytes 98336 | tf_op jit(solution)/shard_map/ppermute | solution.py:89
  231.6 3.9 %collective-permute-done.57.refs_3_ = bf16[128,384]{1,0:T(8,128)(2,1)S(1)} collective-permute-done((bf16[128,384]{1,0:T(8,128)(2,1)S(1)}, bf16[128,384]{1,0:T(8,128)(2,1)S(1)}, u32[]{:S(2)}, u32[]{:S(2)}) %collective-permute-start.57) | collective-permute-done | bytes 98336 | tf_op jit(solution)/shard_map/ppermute | solution.py:89
  235.5 9.3 %collective-permute-done.60.refs_6_ = bf16[128,384]{1,0:T(8,128)(2,1)S(1)} collective-permute-done((bf16[128,384]{1,0:T(8,128)(2,1)S(1)}, bf16[128,384]{1,0:T(8,128)(2,1)S(1)}, u32[]{:S(2)}, u32[]{:S(2)}) %collective-permute-start.60) | collective-permute-done | bytes 98336 | tf_op jit(solution)/shard_map/ppermute | solution.py:89
  244.8 3.5 %collective-permute-done.61.refs_7_ = bf16[128,384]{1,0:T(8,128)(2,1)S(1)} collective-permute-done((bf16[128,384]{1,0:T(8,128)(2,1)S(1)}, bf16[128,384]{1,0:T(8,128)(2,1)S(1)}, u32[]{:S(2)}, u32[]{:S(2)}) %collective-permute-start.61) | collective-permute-done | bytes 98336 | tf_op jit(solution)/shard_map/ppermute | solution.py:89
  249.0 5.3 %shard_map.183 = (bf16[512,768]{1,0:T(8,128)(2,1)}, f32[8,1024]{1,0:T(8,128)}, f32[128,1024]{1,0:T(8,128)}, bf16[128,1024]{1,0:T(8,128)(2,1)}, bf16[128,1024]{1,0:T(8,128)(2,1)}, /*index=5*/bf16[128,1024]{1,0:T(8,128)(2,1)}) custom-call(s32[24]{0:T(128)} %copy-done.35, bf16[128,384]{1,0:T(8,128)(2,1)} %copy-done.34, bf16[128,384]{1,0:T(8,128)(2,1)} %copy-done.67, ...), custom_call_target="tpu_custom_call" | custom-call | flops 805306368 | bytes 5570560 | tf_op jit(solution)/shard_map/pallas_call | solution.py:68
  260.3 2.5 shard_map.175
  264.3 6.9 %collective-permute-start.66 = (bf16[144,768]{1,0:T(8,128)(2,1)S(1)}, bf16[144,768]{1,0:T(8,128)(2,1)S(1)}, u32[]{:S(2)}, u32[]{:S(2)}) collective-permute-start(bf16[144,768]{1,0:T(8,128)(2,1)S(1)} %get-tuple-element.186), channel_id=1, source_target_pairs={{0,8},{4,12},{8,0},{12,4},{16,24},{20,28},{24,16},{28,20},{1,9},{5... | collective-permute-start | bytes 663560 | tf_op jit(solution)/shard_map/ppermute | solution.py:89
  278.8 2.3 collective-permute-done.66.refs_1_
  282.4 7.6 %collective-permute-done.67.refs_2_ = bf16[144,768]{1,0:T(8,128)(2,1)S(1)} collective-permute-done((bf16[144,768]{1,0:T(8,128)(2,1)S(1)}, bf16[144,768]{1,0:T(8,128)(2,1)S(1)}, u32[]{:S(2)}, u32[]{:S(2)}) %collective-permute-start.67) | collective-permute-done | bytes 221216 | tf_op jit(solution)/shard_map/ppermute | solution.py:89
  289.9 2.6 collective-permute-start.41
  293.8 2.5 shard_map.187
  307.1 2.4 collective-permute-start.43
  312.4 4.0 %collective-permute-start.45 = (bf16[32,1024]{1,0:T(8,128)(2,1)S(1)}, bf16[32,1024]{1,0:T(8,128)(2,1)S(1)}, u32[]{:S(2)}, u32[]{:S(2)}) collective-permute-start(bf16[32,1024]{1,0:T(8,128)(2,1)S(1)} %get-tuple-element.152), channel_id=1, source_target_pairs={{0,24},{4,28},{8,16},{12,20},{16,8},{20,12},{24,0},{28,4},{1,25},{... | collective-permute-start | bytes 196616 | tf_op jit(solution)/shard_map/ppermute | solution.py:89
  316.6 2.1 collective-permute-done.45.refs_5_
  320.9 2.0 shard_map.181
  327.3 2.1 shard_map.188
  330.5 6.1 %collective-permute-done.64.refs_2_ = bf16[128,1024]{1,0:T(8,128)(2,1)S(1)} collective-permute-done((bf16[128,1024]{1,0:T(8,128)(2,1)}, bf16[128,1024]{1,0:T(8,128)(2,1)S(1)}, u32[]{:S(2)}, u32[]{:S(2)}) %collective-permute-start.64) | collective-permute-done | bytes 262176 | tf_op jit(solution)/shard_map/ppermute | solution.py:86
  (287 shorter events, 90.2 us)
Async XLA Ops:
  7.2 132.8 %all-gather.2.cloned.1.call-start = ((), (), s32[]{:S(2)}) async-start(), calls=%async_computation.2 | async-start | bytes 1310720 | tf_op jit(solution)/shard_map/all_gather | solution.py:221
  18.7 11.9 %collective-permute-start.1 = (bf16[128,1024]{1,0:T(8,128)(2,1)S(1)}, bf16[128,1024]{1,0:T(8,128)(2,1)S(1)}, u32[]{:S(2)}, u32[]{:S(2)}) collective-permute-start(bf16[128,1024]{1,0:T(8,128)(2,1)S(1)} %get-tuple-element.105.refs_0_.refs_8_), channel_id=1, source_target_pairs={{0,2},{1,3},{2,0},{3,1},{4,6},{5,7},{6,4},{7,5},{8,10},{9,11},{10,... | collective-permute-start | bytes 786440 | tf_op jit(solution)/shard_map/ppermute | solution.py:86
  19.2 12.9 %collective-permute-start = (bf16[128,1024]{1,0:T(8,128)(2,1)S(1)}, bf16[128,1024]{1,0:T(8,128)(2,1)}, u32[]{:S(2)}, u32[]{:S(2)}) collective-permute-start(bf16[128,1024]{1,0:T(8,128)(2,1)S(1)} %get-tuple-element.105.refs_0_.refs_8_), channel_id=1, source_target_pairs={{0,1},{1,0},{2,3},{3,2},{4,5},{5,4},{6,7},{7,6},{8,9},{9,8},{10,11... | collective-permute-start | bytes 786440 | tf_op jit(solution)/shard_map/ppermute | solution.py:86
  19.3 17.2 %collective-permute-start.3 = (bf16[144,768]{1,0:T(8,128)(2,1)}, bf16[144,768]{1,0:T(8,128)(2,1)}, u32[]{:S(2)}, u32[]{:S(2)}) collective-permute-start(bf16[144,768]{1,0:T(8,128)(2,1)} %get-tuple-element.107), channel_id=1, source_target_pairs={{0,1},{1,0},{2,3},{3,2},{4,5},{5,4},{6,7},{7,6},{8,9},{9,8},{10,11... | collective-permute-start | bytes 663560 | tf_op jit(solution)/shard_map/ppermute | solution.py:86
  32.2 261.6 %reduce-scatter.5.cloned.1.call-start = ((), (), s32[]{:S(2)}) async-start(), calls=%async_computation.4 | async-start | bytes 2359296 | tf_op jit(solution)/shard_map/reduce_scatter | solution.py:347
  32.2 14.6 %collective-permute-start.4 = (bf16[144,768]{1,0:T(8,128)(2,1)}, bf16[144,768]{1,0:T(8,128)(2,1)S(1)}, u32[]{:S(2)}, u32[]{:S(2)}) collective-permute-start(bf16[144,768]{1,0:T(8,128)(2,1)} %copy-done.52), channel_id=1, source_target_pairs={{0,2},{1,3},{2,0},{3,1},{4,6},{5,7},{6,4},{7,5},{8,10},{9,11},{10,... | collective-permute-start | bytes 663560 | tf_op jit(solution)/shard_map/ppermute | solution.py:86
  32.5 15.8 %collective-permute-start.5 = (bf16[144,768]{1,0:T(8,128)(2,1)}, bf16[144,768]{1,0:T(8,128)(2,1)S(1)}, u32[]{:S(2)}, u32[]{:S(2)}) collective-permute-start(bf16[144,768]{1,0:T(8,128)(2,1)} %copy-done.51), channel_id=1, source_target_pairs={{0,3},{1,2},{2,1},{3,0},{4,7},{5,6},{6,5},{7,4},{8,11},{9,10},{10,... | collective-permute-start | bytes 663560 | tf_op jit(solution)/shard_map/ppermute | solution.py:86
  36.5 11.9 %collective-permute-start.6 = (bf16[144,768]{1,0:T(8,128)(2,1)}, bf16[144,768]{1,0:T(8,128)(2,1)S(1)}, u32[]{:S(2)}, u32[]{:S(2)}) collective-permute-start(bf16[144,768]{1,0:T(8,128)(2,1)} %collective-permute-done.3.refs_6_), channel_id=1, source_target_pairs={{0,4},{4,0},{8,12},{12,8},{16,20},{20,16},{24,28},{28,24},{1,5},{5... | collective-permute-start | bytes 663560 | tf_op jit(solution)/shard_map/ppermute | solution.py:89
  37.2 18.1 %collective-permute-start.24 = (bf16[128,2048]{1,0:T(8,128)(2,1)S(1)}, bf16[128,2048]{1,0:T(8,128)(2,1)S(1)}, u32[]{:S(2)}, u32[]{:S(2)}) collective-permute-start(bf16[128,2048]{1,0:T(8,128)(2,1)S(1)} %get-tuple-element.124), channel_id=1, source_target_pairs={{0,1},{1,0},{2,3},{3,2},{4,5},{5,4},{6,7},{7,6},{8,9},{9,8},{10,11... | collective-permute-start | bytes 1572872 | tf_op jit(solution)/shard_map/ppermute | solution.py:86
  38.6 33.8 %collective-permute-start.25 = (bf16[128,2048]{1,0:T(8,128)(2,1)S(1)}, bf16[128,2048]{1,0:T(8,128)(2,1)S(1)}, u32[]{:S(2)}, u32[]{:S(2)}) collective-permute-start(bf16[128,2048]{1,0:T(8,128)(2,1)S(1)} %get-tuple-element.125), channel_id=1, source_target_pairs={{0,2},{1,3},{2,0},{3,1},{4,6},{5,7},{6,4},{7,5},{8,10},{9,11},{10,... | collective-permute-start | bytes 1572872 | tf_op jit(solution)/shard_map/ppermute | solution.py:86
  46.9 25.5 %collective-permute-start.26 = (bf16[128,2048]{1,0:T(8,128)(2,1)S(1)}, bf16[128,2048]{1,0:T(8,128)(2,1)S(1)}, u32[]{:S(2)}, u32[]{:S(2)}) collective-permute-start(bf16[128,2048]{1,0:T(8,128)(2,1)S(1)} %get-tuple-element.126), channel_id=1, source_target_pairs={{0,3},{1,2},{2,1},{3,0},{4,7},{5,6},{6,5},{7,4},{8,11},{9,10},{10,... | collective-permute-start | bytes 1572872 | tf_op jit(solution)/shard_map/ppermute | solution.py:86
  53.5 19.4 %collective-permute-start.9 = (bf16[128,384]{1,0:T(8,128)(2,1)S(1)}, bf16[128,384]{1,0:T(8,128)(2,1)S(1)}, u32[]{:S(2)}, u32[]{:S(2)}) collective-permute-start(bf16[128,384]{1,0:T(8,128)(2,1)S(1)} %get-tuple-element.112), channel_id=1, source_target_pairs={{0,4},{4,0},{8,12},{12,8},{16,20},{20,16},{24,28},{28,24},{1,5},{5... | collective-permute-start | bytes 294920 | tf_op jit(solution)/shard_map/ppermute | solution.py:89
  53.7 19.3 %collective-permute-start.10 = (bf16[128,384]{1,0:T(8,128)(2,1)S(1)}, bf16[128,384]{1,0:T(8,128)(2,1)S(1)}, u32[]{:S(2)}, u32[]{:S(2)}) collective-permute-start(bf16[128,384]{1,0:T(8,128)(2,1)S(1)} %get-tuple-element.113), channel_id=1, source_target_pairs={{0,8},{4,12},{8,0},{12,4},{16,24},{20,28},{24,16},{28,20},{1,9},{5... | collective-permute-start | bytes 294920 | tf_op jit(solution)/shard_map/ppermute | solution.py:89
  55.4 20.8 %collective-permute-start.11 = (bf16[128,384]{1,0:T(8,128)(2,1)S(1)}, bf16[128,384]{1,0:T(8,128)(2,1)S(1)}, u32[]{:S(2)}, u32[]{:S(2)}) collective-permute-start(bf16[128,384]{1,0:T(8,128)(2,1)S(1)} %get-tuple-element.114), channel_id=1, source_target_pairs={{0,12},{4,8},{8,4},{12,0},{16,28},{20,24},{24,20},{28,16},{1,13},{... | collective-permute-start | bytes 294920 | tf_op jit(solution)/shard_map/ppermute | solution.py:89
  72.4 48.7 %collective-permute-start.27 = (bf16[128,2048]{1,0:T(8,128)(2,1)S(1)}, bf16[128,2048]{1,0:T(8,128)(2,1)S(1)}, u32[]{:S(2)}, u32[]{:S(2)}) collective-permute-start(bf16[128,2048]{1,0:T(8,128)(2,1)S(1)} %collective-permute-done.24.refs_11_.refs_6_), channel_id=1, source_target_pairs={{0,4},{4,0},{8,12},{12,8},{16,20},{20,16},{24,28},{28,24},{1,5},{5... | collective-permute-start | bytes 1572872 | tf_op jit(solution)/shard_map/ppermute | solution.py:89
  72.4 48.7 %collective-permute-start.28 = (bf16[128,2048]{1,0:T(8,128)(2,1)S(1)}, bf16[128,2048]{1,0:T(8,128)(2,1)S(1)}, u32[]{:S(2)}, u32[]{:S(2)}) collective-permute-start(bf16[128,2048]{1,0:T(8,128)(2,1)S(1)} %collective-permute-done.25.refs_12_.refs_7_), channel_id=1, source_target_pairs={{0,4},{4,0},{8,12},{12,8},{16,20},{20,16},{24,28},{28,24},{1,5},{5... | collective-permute-start | bytes 1572872 | tf_op jit(solution)/shard_map/ppermute | solution.py:89
  72.9 48.2 %collective-permute-start.29 = (bf16[128,2048]{1,0:T(8,128)(2,1)S(1)}, bf16[128,2048]{1,0:T(8,128)(2,1)S(1)}, u32[]{:S(2)}, u32[]{:S(2)}) collective-permute-start(bf16[128,2048]{1,0:T(8,128)(2,1)S(1)} %collective-permute-done.26.refs_13_.refs_8_), channel_id=1, source_target_pairs={{0,4},{4,0},{8,12},{12,8},{16,20},{20,16},{24,28},{28,24},{1,5},{5... | collective-permute-start | bytes 1572872 | tf_op jit(solution)/shard_map/ppermute | solution.py:89
  125.4 13.4 %collective-permute-start.31 = (bf16[128,1024]{1,0:T(8,128)(2,1)S(1)}, bf16[128,1024]{1,0:T(8,128)(2,1)S(1)}, u32[]{:S(2)}, u32[]{:S(2)}) collective-permute-start(bf16[128,1024]{1,0:T(8,128)(2,1)S(1)} %get-tuple-element.127.refs_0_), channel_id=1, source_target_pairs={{0,2},{1,3},{2,0},{3,1},{4,6},{5,7},{6,4},{7,5},{8,10},{9,11},{10,... | collective-permute-start | bytes 786440 | tf_op jit(solution)/shard_map/ppermute | solution.py:86
  128.1 11.8 %collective-permute-start.30 = (bf16[128,1024]{1,0:T(8,128)(2,1)S(1)}, bf16[128,1024]{1,0:T(8,128)(2,1)}, u32[]{:S(2)}, u32[]{:S(2)}) collective-permute-start(bf16[128,1024]{1,0:T(8,128)(2,1)S(1)} %get-tuple-element.127.refs_0_), channel_id=1, source_target_pairs={{0,1},{1,0},{2,3},{3,2},{4,5},{5,4},{6,7},{7,6},{8,9},{9,8},{10,11... | collective-permute-start | bytes 786440 | tf_op jit(solution)/shard_map/ppermute | solution.py:86
  161.4 163.4 %reduce-scatter.3.cloned.1.call-start = ((), (), s32[]{:S(2)}) async-start(), calls=%async_computation.3 | async-start | bytes 2359296 | tf_op jit(solution)/shard_map/reduce_scatter | solution.py:347
  164.5 13.8 %collective-permute-start.34 = (bf16[128,1024]{1,0:T(8,128)(2,1)}, bf16[128,1024]{1,0:T(8,128)(2,1)S(1)}, u32[]{:S(2)}, u32[]{:S(2)}) collective-permute-start(bf16[128,1024]{1,0:T(8,128)(2,1)} %get-tuple-element.137), channel_id=1, source_target_pairs={{0,2},{1,3},{2,0},{3,1},{4,6},{5,7},{6,4},{7,5},{8,10},{9,11},{10,... | collective-permute-start | bytes 786440 | tf_op jit(solution)/shard_map/ppermute | solution.py:86
  164.5 13.8 %collective-permute-start.35 = (bf16[128,1024]{1,0:T(8,128)(2,1)}, bf16[128,1024]{1,0:T(8,128)(2,1)S(1)}, u32[]{:S(2)}, u32[]{:S(2)}) collective-permute-start(bf16[128,1024]{1,0:T(8,128)(2,1)} %get-tuple-element.138), channel_id=1, source_target_pairs={{0,3},{1,2},{2,1},{3,0},{4,7},{5,6},{6,5},{7,4},{8,11},{9,10},{10,... | collective-permute-start | bytes 786440 | tf_op jit(solution)/shard_map/ppermute | solution.py:86
  182.9 23.2 %collective-permute-start.48 = (bf16[128,256]{1,0:T(8,128)(2,1)S(1)}, bf16[128,256]{1,0:T(8,128)(2,1)S(1)}, u32[]{:S(2)}, u32[]{:S(2)}) collective-permute-start(bf16[128,256]{1,0:T(8,128)(2,1)S(1)} %get-tuple-element.160), channel_id=1, source_target_pairs={{0,1},{1,9},{2,17},{3,25},{4,5},{5,13},{6,21},{7,29},{8,0},{9,8},{... | collective-permute-start | bytes 196616 | tf_op jit(solution)/shard_map/ppermute | solution.py:97
  185.7 20.4 %collective-permute-start.49 = (bf16[128,256]{1,0:T(8,128)(2,1)S(1)}, bf16[128,256]{1,0:T(8,128)(2,1)S(1)}, u32[]{:S(2)}, u32[]{:S(2)}) collective-permute-start(bf16[128,256]{1,0:T(8,128)(2,1)S(1)} %get-tuple-element.161), channel_id=1, source_target_pairs={{0,2},{1,10},{2,18},{3,26},{4,6},{5,14},{6,22},{7,30},{8,3},{9,11}... | collective-permute-start | bytes 196616 | tf_op jit(solution)/shard_map/ppermute | solution.py:97
  188.5 18.1 %collective-permute-start.50 = (bf16[128,256]{1,0:T(8,128)(2,1)S(1)}, bf16[128,256]{1,0:T(8,128)(2,1)S(1)}, u32[]{:S(2)}, u32[]{:S(2)}) collective-permute-start(bf16[128,256]{1,0:T(8,128)(2,1)S(1)} %get-tuple-element.162), channel_id=1, source_target_pairs={{0,3},{1,11},{2,19},{3,27},{4,7},{5,15},{6,23},{7,31},{8,2},{9,10}... | collective-permute-start | bytes 196616 | tf_op jit(solution)/shard_map/ppermute | solution.py:97
  188.7 18.0 %collective-permute-start.51 = (bf16[128,256]{1,0:T(8,128)(2,1)S(1)}, bf16[128,256]{1,0:T(8,128)(2,1)S(1)}, u32[]{:S(2)}, u32[]{:S(2)}) collective-permute-start(bf16[128,256]{1,0:T(8,128)(2,1)S(1)} %collective-permute-done.47.refs_3_), channel_id=1, source_target_pairs={{0,4},{4,0},{8,12},{12,8},{16,20},{20,16},{24,28},{28,24},{1,5},{5... | collective-permute-start | bytes 196616 | tf_op jit(solution)/shard_map/ppermute | solution.py:89
  217.7 13.9 %collective-permute-start.56 = (bf16[128,384]{1,0:T(8,128)(2,1)S(1)}, bf16[128,384]{1,0:T(8,128)(2,1)S(1)}, u32[]{:S(2)}, u32[]{:S(2)}) collective-permute-start(bf16[128,384]{1,0:T(8,128)(2,1)S(1)} %get-tuple-element.165), channel_id=1, source_target_pairs={{0,8},{4,12},{8,0},{12,4},{16,24},{20,28},{24,16},{28,20},{1,9},{5... | collective-permute-start | bytes 294920 | tf_op jit(solution)/shard_map/ppermute | solution.py:89
  219.7 15.8 %collective-permute-start.57 = (bf16[128,384]{1,0:T(8,128)(2,1)S(1)}, bf16[128,384]{1,0:T(8,128)(2,1)S(1)}, u32[]{:S(2)}, u32[]{:S(2)}) collective-permute-start(bf16[128,384]{1,0:T(8,128)(2,1)S(1)} %get-tuple-element.166), channel_id=1, source_target_pairs={{0,12},{4,8},{8,4},{12,0},{16,28},{20,24},{24,20},{28,16},{1,13},{... | collective-permute-start | bytes 294920 | tf_op jit(solution)/shard_map/ppermute | solution.py:89
  219.7 15.8 %collective-permute-start.58 = (bf16[128,384]{1,0:T(8,128)(2,1)S(1)}, bf16[128,384]{1,0:T(8,128)(2,1)S(1)}, u32[]{:S(2)}, u32[]{:S(2)}) collective-permute-start(bf16[128,384]{1,0:T(8,128)(2,1)S(1)} %get-tuple-element.167), channel_id=1, source_target_pairs={{0,16},{4,20},{8,24},{12,28},{16,0},{20,4},{24,8},{28,12},{1,17},{... | collective-permute-start | bytes 294920 | tf_op jit(solution)/shard_map/ppermute | solution.py:89
  222.8 12.7 %collective-permute-start.59 = (bf16[128,384]{1,0:T(8,128)(2,1)S(1)}, bf16[128,384]{1,0:T(8,128)(2,1)S(1)}, u32[]{:S(2)}, u32[]{:S(2)}) collective-permute-start(bf16[128,384]{1,0:T(8,128)(2,1)S(1)} %get-tuple-element.168), channel_id=1, source_target_pairs={{0,20},{4,16},{8,28},{12,24},{16,4},{20,0},{24,12},{28,8},{1,21},{... | collective-permute-start | bytes 294920 | tf_op jit(solution)/shard_map/ppermute | solution.py:89
  222.8 22.0 %collective-permute-start.60 = (bf16[128,384]{1,0:T(8,128)(2,1)S(1)}, bf16[128,384]{1,0:T(8,128)(2,1)S(1)}, u32[]{:S(2)}, u32[]{:S(2)}) collective-permute-start(bf16[128,384]{1,0:T(8,128)(2,1)S(1)} %get-tuple-element.169), channel_id=1, source_target_pairs={{0,24},{4,28},{8,16},{12,20},{16,8},{20,12},{24,0},{28,4},{1,25},{... | collective-permute-start | bytes 294920 | tf_op jit(solution)/shard_map/ppermute | solution.py:89
  231.6 16.8 %collective-permute-start.61 = (bf16[128,384]{1,0:T(8,128)(2,1)S(1)}, bf16[128,384]{1,0:T(8,128)(2,1)S(1)}, u32[]{:S(2)}, u32[]{:S(2)}) collective-permute-start(bf16[128,384]{1,0:T(8,128)(2,1)S(1)} %get-tuple-element.170), channel_id=1, source_target_pairs={{0,28},{4,24},{8,20},{12,16},{16,12},{20,8},{24,4},{28,0},{1,29},{... | collective-permute-start | bytes 294920 | tf_op jit(solution)/shard_map/ppermute | solution.py:89
  260.2 14.2 %collective-permute-start.36 = (bf16[4,128,1024]{2,1,0:T(8,128)(2,1)S(1)}, bf16[4,128,1024]{2,1,0:T(8,128)(2,1)S(1)}, u32[]{:S(2)}, u32[]{:S(2)}) collective-permute-start(bf16[4,128,1024]{2,1,0:T(8,128)(2,1)S(1)} %get-tuple-element.141), channel_id=1, source_target_pairs={{0,4},{4,0},{8,12},{12,8},{16,20},{20,16},{24,28},{28,24},{1,5},{5... | collective-permute-start | bytes 3145736 | tf_op jit(solution)/shard_map/ppermute | solution.py:89
  262.8 14.2 %collective-permute-start.40 = (bf16[128,1024]{1,0:T(8,128)(2,1)S(1)}, bf16[128,1024]{1,0:T(8,128)(2,1)S(1)}, u32[]{:S(2)}, u32[]{:S(2)}) collective-permute-start(bf16[128,1024]{1,0:T(8,128)(2,1)S(1)} %get-tuple-element.147), channel_id=1, source_target_pairs={{0,1},{1,0},{2,3},{3,2},{4,5},{5,4},{6,7},{7,6},{8,9},{9,8},{10,11... | collective-permute-start | bytes 786440 | tf_op jit(solution)/shard_map/ppermute | solution.py:86
  264.3 16.8 %collective-permute-start.66 = (bf16[144,768]{1,0:T(8,128)(2,1)S(1)}, bf16[144,768]{1,0:T(8,128)(2,1)S(1)}, u32[]{:S(2)}, u32[]{:S(2)}) collective-permute-start(bf16[144,768]{1,0:T(8,128)(2,1)S(1)} %get-tuple-element.186), channel_id=1, source_target_pairs={{0,8},{4,12},{8,0},{12,4},{16,24},{20,28},{24,16},{28,20},{1,9},{5... | collective-permute-start | bytes 663560 | tf_op jit(solution)/shard_map/ppermute | solution.py:89
  271.2 18.7 %collective-permute-start.67 = (bf16[144,768]{1,0:T(8,128)(2,1)S(1)}, bf16[144,768]{1,0:T(8,128)(2,1)S(1)}, u32[]{:S(2)}, u32[]{:S(2)}) collective-permute-start(bf16[144,768]{1,0:T(8,128)(2,1)S(1)} %get-tuple-element.187), channel_id=1, source_target_pairs={{0,16},{4,20},{8,24},{12,28},{16,0},{20,4},{24,8},{28,12},{1,17},{... | collective-permute-start | bytes 663560 | tf_op jit(solution)/shard_map/ppermute | solution.py:89
  272.9 19.6 %collective-permute-start.68 = (bf16[144,768]{1,0:T(8,128)(2,1)S(1)}, bf16[144,768]{1,0:T(8,128)(2,1)S(1)}, u32[]{:S(2)}, u32[]{:S(2)}) collective-permute-start(bf16[144,768]{1,0:T(8,128)(2,1)S(1)} %get-tuple-element.188), channel_id=1, source_target_pairs={{0,24},{4,28},{8,16},{12,20},{16,8},{20,12},{24,0},{28,4},{1,25},{... | collective-permute-start | bytes 663560 | tf_op jit(solution)/shard_map/ppermute | solution.py:89
  275.9 20.4 %collective-permute-start.37 = (bf16[128,1024]{1,0:T(8,128)(2,1)}, bf16[128,1024]{1,0:T(8,128)(2,1)S(1)}, u32[]{:S(2)}, u32[]{:S(2)}) collective-permute-start(bf16[128,1024]{1,0:T(8,128)(2,1)} %get-tuple-element.143), channel_id=1, source_target_pairs={{0,1},{1,0},{2,3},{3,2},{4,5},{5,4},{6,7},{7,6},{8,9},{9,8},{10,11... | collective-permute-start | bytes 786440 | tf_op jit(solution)/shard_map/ppermute | solution.py:86
  277.1 20.9 %collective-permute-start.38 = (bf16[128,1024]{1,0:T(8,128)(2,1)}, bf16[128,1024]{1,0:T(8,128)(2,1)S(1)}, u32[]{:S(2)}, u32[]{:S(2)}) collective-permute-start(bf16[128,1024]{1,0:T(8,128)(2,1)} %get-tuple-element.144), channel_id=1, source_target_pairs={{0,2},{1,3},{2,0},{3,1},{4,6},{5,7},{6,4},{7,5},{8,10},{9,11},{10,... | collective-permute-start | bytes 786440 | tf_op jit(solution)/shard_map/ppermute | solution.py:86
  281.1 19.6 %collective-permute-start.39 = (bf16[128,1024]{1,0:T(8,128)(2,1)}, bf16[128,1024]{1,0:T(8,128)(2,1)S(1)}, u32[]{:S(2)}, u32[]{:S(2)}) collective-permute-start(bf16[128,1024]{1,0:T(8,128)(2,1)} %get-tuple-element.145), channel_id=1, source_target_pairs={{0,3},{1,2},{2,1},{3,0},{4,7},{5,6},{6,5},{7,4},{8,11},{9,10},{10,... | collective-permute-start | bytes 786440 | tf_op jit(solution)/shard_map/ppermute | solution.py:86
  289.9 17.2 %collective-permute-start.41 = (bf16[128,1024]{1,0:T(8,128)(2,1)}, bf16[128,1024]{1,0:T(8,128)(2,1)}, u32[]{:S(2)}, u32[]{:S(2)}) collective-permute-start(bf16[128,1024]{1,0:T(8,128)(2,1)} %get-tuple-element.148), channel_id=1, source_target_pairs={{0,2},{1,3},{2,0},{3,1},{4,6},{5,7},{6,4},{7,5},{8,10},{9,11},{10,... | collective-permute-start | bytes 786440 | tf_op jit(solution)/shard_map/ppermute | solution.py:86
  293.2 16.3 %collective-permute-start.42 = (bf16[128,1024]{1,0:T(8,128)(2,1)}, bf16[128,1024]{1,0:T(8,128)(2,1)}, u32[]{:S(2)}, u32[]{:S(2)}) collective-permute-start(bf16[128,1024]{1,0:T(8,128)(2,1)} %get-tuple-element.149), channel_id=1, source_target_pairs={{0,3},{1,2},{2,1},{3,0},{4,7},{5,6},{6,5},{7,4},{8,11},{9,10},{10,... | collective-permute-start | bytes 786440 | tf_op jit(solution)/shard_map/ppermute | solution.py:86
  297.0 26.0 %collective-permute-start.69 = (bf16[48,1792]{1,0:T(8,128)(2,1)}, bf16[48,1792]{1,0:T(8,128)(2,1)S(1)}, u32[]{:S(2)}, u32[]{:S(2)}) collective-permute-start(bf16[48,1792]{1,0:T(8,128)(2,1)} %get-tuple-element.192), channel_id=1, source_target_pairs={{0,1},{1,0},{2,3},{3,2},{4,5},{5,4},{6,7},{7,6},{8,9},{9,8},{10,11... | collective-permute-start | bytes 516104 | tf_op jit(solution)/shard_map/ppermute | solution.py:86
  298.7 26.1 %collective-permute-start.70 = (bf16[48,1792]{1,0:T(8,128)(2,1)}, bf16[48,1792]{1,0:T(8,128)(2,1)}, u32[]{:S(2)}, u32[]{:S(2)}) collective-permute-start(bf16[48,1792]{1,0:T(8,128)(2,1)} %get-tuple-element.193), channel_id=1, source_target_pairs={{0,2},{1,3},{2,0},{3,1},{4,6},{5,7},{6,4},{7,5},{8,10},{9,11},{10,... | collective-permute-start | bytes 516104 | tf_op jit(solution)/shard_map/ppermute | solution.py:86
  301.3 25.0 %collective-permute-start.71 = (bf16[48,1792]{1,0:T(8,128)(2,1)}, bf16[48,1792]{1,0:T(8,128)(2,1)}, u32[]{:S(2)}, u32[]{:S(2)}) collective-permute-start(bf16[48,1792]{1,0:T(8,128)(2,1)} %get-tuple-element.194), channel_id=1, source_target_pairs={{0,3},{1,2},{2,1},{3,0},{4,7},{5,6},{6,5},{7,4},{8,11},{9,10},{10,... | collective-permute-start | bytes 516104 | tf_op jit(solution)/shard_map/ppermute | solution.py:86
  316.4 14.1 %collective-permute-start.62 = (bf16[128,1024]{1,0:T(8,128)(2,1)}, bf16[128,1024]{1,0:T(8,128)(2,1)S(1)}, u32[]{:S(2)}, u32[]{:S(2)}) collective-permute-start(bf16[128,1024]{1,0:T(8,128)(2,1)} %get-tuple-element.174), channel_id=1, source_target_pairs={{0,1},{1,0},{2,3},{3,2},{4,5},{5,4},{6,7},{7,6},{8,9},{9,8},{10,11... | collective-permute-start | bytes 786440 | tf_op jit(solution)/shard_map/ppermute | solution.py:86
  323.6 13.0 %collective-permute-start.64 = (bf16[128,1024]{1,0:T(8,128)(2,1)}, bf16[128,1024]{1,0:T(8,128)(2,1)S(1)}, u32[]{:S(2)}, u32[]{:S(2)}) collective-permute-start(bf16[128,1024]{1,0:T(8,128)(2,1)} %get-tuple-element.176), channel_id=1, source_target_pairs={{0,3},{1,2},{2,1},{3,0},{4,7},{5,6},{6,5},{7,4},{8,11},{9,10},{10,... | collective-permute-start | bytes 786440 | tf_op jit(solution)/shard_map/ppermute | solution.py:86
  324.7 11.9 %collective-permute-start.46 = (bf16[128,1024]{1,0:T(8,128)(2,1)}, bf16[128,1024]{1,0:T(8,128)(2,1)S(1)}, u32[]{:S(2)}, u32[]{:S(2)}) collective-permute-start(bf16[128,1024]{1,0:T(8,128)(2,1)} %reduce-scatter.3.cloned.1.call-done), channel_id=1, source_target_pairs={{0,0},{1,8},{2,16},{3,24},{4,1},{5,9},{6,17},{7,25},{8,2},{9,10},{... | collective-permute-start | bytes 786440 | tf_op jit(solution)/shard_map/ppermute | solution.py:97
  (104 other events, 1456.1 us)
Sparse Core Ops, SparseCore 0:
  32.3 42.0 all-gather.1
  161.5 45.0 reduce-scatter.4
  208.9 48.6 reduce-scatter.2
